TPU v7x, 256 devices: a whole 4x4x8 slice. The times are simulated.
256 devices in a mesh: view: 16 (over z, core), blk: 16 (over y, x).
Axes of the slice: x: 4, y: 4, z: 8, core: 2. Of those that a mesh axis runs over, the one named last changes fastest.
Arguments:
- estimate: float32 [256, 128, 128], P('blk'), may hold values from 0.5 to 2
- images: bfloat16 [16, 256, 64, 128], P('view', 'blk'), may hold values from 0.5 to 2
- point_spread: float32 [8, 9, 7, 25], replicated, may hold values from 0.01 to 1
- covered: int32 [8, 16, 4], P(None, 'blk'), may hold values from 0 to 1, as said below
Outputs:
- estimate_next: float32 [256, 128, 128], P('blk')
Inputs may be any that keep to these rules, and one draw needn't show every extreme that they name: For each view and each block layer along the first dimension, the covered blocks are consecutive along the second dimension and at most 3; for every view some block layer has exactly 3.
All inputs are finite; a program needn't handle non-finite values.
Results may differ from a plain program's by a relative error of at most 0.0003.
Values may be sent and summed in bfloat16 or wider, within the bound.
A program may use at most 64 MiB of HBM per device.

v0:
```python
import jax
import jax.numpy as jnp
from jax import lax
from jax.sharding import PartitionSpec as P

BY = 32


def with_halo(cells, sides, width):
    for axis, dim in sides:
        count = lax.axis_size(axis)
        ends = count - 1
        head = lax.slice_in_dim(cells, 0, width, axis=dim)
        tail = lax.slice_in_dim(cells, cells.shape[dim] - width, cells.shape[dim], axis=dim)
        cells = jnp.concatenate(
            [
                lax.ppermute(tail, axis, [(i, (i + 1) % count) for i in range(ends)]),
                cells,
                lax.ppermute(head, axis, [((i + 1) % count, i) for i in range(ends)]),
            ],
            axis=dim,
        )
    return cells


def swapped(block, axis, stride):
    count = lax.axis_size(axis)
    route = []
    for low in range(count):
        high = low | 1 << stride
        if high != low and high < count:
            route += [(low, high), (high, low)]
    return lax.ppermute(block, axis, route)


def merged(part, axis, combine):
    gathered = lax.all_gather(part, axis)

    def take(source):
        return lax.dynamic_index_in_dim(gathered, source, 0, False)

    return lax.fori_loop(
        1, lax.axis_size(axis), lambda source, state: combine(state, take(source)), take(0)
    )


def band_table(kernel, depth):
    taps_x, taps_y, taps_z = kernel.shape
    span_z = depth + taps_z - 1
    shape_three = (taps_z, span_z, depth)
    offset = lax.broadcasted_iota(jnp.int32, shape_three, 1) - lax.broadcasted_iota(
        jnp.int32, shape_three, 2
    )
    onehot = (offset == lax.broadcasted_iota(jnp.int32, shape_three, 0)).astype(jnp.bfloat16)
    banded = jnp.einsum("abt,tpz->abpz", kernel, onehot, preferred_element_type=jnp.float32).astype(
        jnp.bfloat16
    )
    inner_width = taps_y * span_z
    padded_width = -(-inner_width // 128) * 128
    banded = banded.reshape(taps_x, inner_width, depth)
    return jnp.pad(banded, ((0, 0), (0, padded_width - inner_width), (0, 0)))


def convolve(padded_part, banded, rows_x, rows_y):
    taps_x = padded_part.shape[0] - rows_x + 1
    taps_y = padded_part.shape[1] - rows_y + 1
    columns = jnp.concatenate(
        [padded_part[:, step_y : step_y + rows_y, :] for step_y in range(taps_y)], axis=2
    )
    columns = jnp.pad(columns, ((0, 0), (0, 0), (0, banded.shape[1] - columns.shape[2])))
    output = None
    for shift_x in range(taps_x):
        partial_sum = jnp.dot(
            columns[shift_x : shift_x + rows_x].reshape(rows_x * rows_y, -1),
            banded[shift_x],
            preferred_element_type=jnp.float32,
        )
        output = partial_sum if output is None else output + partial_sum
    return output.reshape(rows_x, rows_y, -1)


def local(estimate, images, point_spread, covered):
    slab_x, width_y, depth = estimate.shape
    share_w = images.shape[2]
    view_count, taps_x, taps_y, taps_z = point_spread.shape
    rim_x, rim_y, rim_z = ((taps_x - 1) // 2, (taps_y - 1) // 2, (taps_z - 1) // 2)
    shares = width_y // share_w
    share_blocks = share_w // BY
    group = lax.axis_index("view")
    view_id = group // shares
    part = group % shares
    y_start = part * share_w
    source = estimate.astype(jnp.bfloat16)
    rimmed = with_halo(source, (("blk", 0),), rim_x)
    padded = jnp.pad(rimmed, ((0, 0), (rim_y, rim_y), (rim_z, rim_z)))
    spread = lax.dynamic_index_in_dim(point_spread, view_id, 0, keepdims=False)
    kernel = (spread / jnp.sum(spread)).astype(jnp.bfloat16)
    forward = band_table(kernel, depth)
    backward = band_table(kernel[::-1, ::-1, ::-1], depth)
    coverage_row = lax.dynamic_index_in_dim(covered[:, 0, :], view_id, 0, keepdims=False) > 0
    share_cover = lax.dynamic_slice_in_dim(coverage_row, part * share_blocks, share_blocks)
    cell_cover = jnp.repeat(share_cover, BY)[None, :, None]
    image = images[0]
    region = lax.dynamic_slice(
        padded, (0, y_start, 0), (slab_x + 2 * rim_x, share_w + 2 * rim_y, depth + 2 * rim_z)
    )
    blurred = convolve(region, forward, slab_x, share_w)
    quotient = jnp.where(cell_cover, image.astype(jnp.float32) / blurred, 0.0).astype(jnp.bfloat16)
    rim_zeros = jnp.zeros((slab_x, rim_y, depth), jnp.bfloat16)
    edge_rows = jnp.where(part == 0, quotient[:, share_w - rim_y :, :], quotient[:, :rim_y, :])
    partner = swapped(edge_rows, "view", 0)
    lower_rim = jnp.where(part > 0, partner, rim_zeros)
    upper_rim = jnp.where(part < shares - 1, partner, rim_zeros)
    extended = jnp.concatenate([lower_rim, quotient, upper_rim], axis=1)
    quotient_rimmed = with_halo(extended, (("blk", 0),), rim_x)
    padded_quotient = jnp.pad(quotient_rimmed, ((0, 0), (0, 0), (rim_z, rim_z)))
    correction = convolve(padded_quotient, backward, slab_x, share_w)
    share_factor = jnp.where(cell_cover, correction, 1.0)
    factor = lax.dynamic_update_slice(
        jnp.ones((slab_x, width_y, depth), jnp.float32), share_factor, (0, y_start, 0)
    )
    product_all = merged(factor, "view", lambda former, latter: former * latter)
    return estimate * product_all


def solution(mesh):
    in_specs = (P("blk", None, None), P("view", "blk", None, None), P(), P(None, "blk", None))
    out_specs = P("blk", None, None)
    return jax.shard_map(local, mesh=mesh, in_specs=in_specs, out_specs=out_specs, check_vma=False)
```

profile of v0, /device:TPU:1, one launch (start us, length us, event | category | flops | bytes accessed | tf_op | source)
XLA Modules:
  0.0 236.4 jit_solution(9890922093268774380)
XLA Ops:
  7.9 4.0 %collective-permute-start = (bf16[4,128,128]{2,1,0:T(8,128)(2,1)S(1)}, bf16[4,128,128]{2,1,0:T(8,128)(2,1)S(1)}, u32[]{:S(2)}, u32[]{:S(2)}) collective-permute-start(bf16[4,128,128]{2,1,0:T(8,128)(2,1)S(1)} %get-tuple-element.135), channel_id=1, source_target_pairs={{0,1},{1,2},{2,3},{3,4},{4,5},{5,6},{6,7},{7,8},{8,9},{9,10},{10,1... | collective-permute-start | bytes 393224 | tf_op jit(solution)/shard_map/ppermute | solution.py:17
  13.2 1.7 fusion.97
  14.8 3.2 %fusion.10 = bf16[9,7,152,128]{3,1,2,0:T(8,128)(2,1)} fusion(f32[1,9,7,25]{3,0,2,1:T(1,128)S(1)} %get-tuple-element.101, f32[]{:T(128)} %get-tuple-element.100), kind=kOutput, calls=%fused_computation.14 | convolution fusion | flops 63488080 | bytes 2457760 | tf_op jit(solution)/shard_map/abt,tpz->abpz/dot_general | solution.py:55
  18.0 1.6 iota_compare_fusion
  19.6 2.1 copy.10
  22.1 2.9 %fusion.23 = bf16[24,70,152]{2,1,0:T(8,128)(2,1)S(1)} fusion(s32[]{:T(128)S(6)} %select_n.78, bf16[4,128,128]{2,1,0:T(8,128)(2,1)S(1)} %collective-permute-done, bf16[16,128,128]{2,1,0:T(8,128)(2,1)S(1)} %convert_element_type.38, pred[24,134,152]{2,1,0:T(8,128)(4,1)} %get-tuple-element.140, pred[24,134,152]{2,1,0:T(8,128)(4,1)} %get-tuple-element.141, ...), kind=kLoop, calls=%fused_computation.63 | loop fusion | flops 5873280 | bytes 1808896 | tf_op jit(solution)/shard_map/concatenate | solution.py:15
  25.0 3.1 %fusion.99 = (bf16[24,64,152]{2,1,0:T(8,128)(2,1)S(1)}, bf16[24,64,152]{2,1,0:T(8,128)(2,1)}, bf16[24,64,152]{2,1,0:T(8,128)(2,1)}, bf16[24,64,152]{2,1,0:T(8,12...) fusion(bf16[24,70,152]{2,1,0:T(8,128)(2,1)S(1)} %fusion.23), kind=kLoop, calls=%fused_computation.152 | loop fusion | bytes 6537216 | tf_op jit(solution)/shard_map/slice | solution.py:68
  28.1 8.4 %concatenate.16 = bf16[24,64,1064]{2,1,0:T(8,128)(2,1)} concatenate(bf16[24,64,152]{2,1,0:T(8,128)(2,1)} %get-tuple-element.133, bf16[24,64,152]{2,1,0:T(8,128)(2,1)} %get-tuple-element.132, bf16[24,64,152]{2,1,0:T(8,128)(2,1)} %get-tuple-element.131, bf16[24,64,152]{2,1,0:T(8,128)(2,1)} %get-tuple-element.130, bf16[24,64,152]{2,1,0:T(8,128)(2,1)} %get-tuple-element.129, ...), dimensions={2} | concatenate | bytes 6537216 | tf_op jit(solution)/shard_map/concatenate | solution.py:67
  36.5 12.4 %pad_slice_fusion.27 = (bf16[16,64,1152]{2,1,0:T(8,128)(2,1)S(1)}, bf16[16,64,1152]{2,1,0:T(8,128)(2,1)S(1)}, bf16[16,64,1152]{2,1,0:T(8,128)(2,1)S(1)}, bf16[16...) fusion(bf16[24,64,1064]{2,1,0:T(8,128)(2,1)} %concatenate.16), kind=kLoop, calls=%fused_computation.107 | loop fusion | bytes 24502272 | tf_op jit(solution)/shard_map/slice | solution.py:74
  58.3 4.3 %collective-permute-start.3 = (bf16[4,70,128]{2,1,0:T(8,128)(2,1)S(1)}, bf16[4,70,128]{2,1,0:T(8,128)(2,1)S(1)}, u32[]{:S(2)}, u32[]{:S(2)}) collective-permute-start(bf16[4,70,128]{2,1,0:T(8,128)(2,1)S(1)} %get-tuple-element.136), channel_id=1, source_target_pairs={{0,1},{1,2},{2,3},{3,4},{4,5},{5,6},{6,7},{7,8},{8,9},{9,10},{10,1... | collective-permute-start | bytes 215048 | tf_op jit(solution)/shard_map/ppermute | solution.py:17
  65.2 2.5 %collective-permute-done.4 = bf16[4,70,128]{2,1,0:T(8,128)(2,1)S(1)} collective-permute-done((bf16[4,70,128]{2,1,0:T(8,128)(2,1)S(1)}, bf16[4,70,128]{2,1,0:T(8,128)(2,1)S(1)}, u32[]{:S(2)}, u32[]{:S(2)}) %collective-permute-start.4) | collective-permute-done | bytes 71712 | tf_op jit(solution)/shard_map/ppermute | solution.py:19
  68.4 3.1 %fusion.98 = (bf16[24,64,152]{2,1,0:T(8,128)(2,1)S(1)}, bf16[24,64,152]{2,1,0:T(8,128)(2,1)}, bf16[24,64,152]{2,1,0:T(8,128)(2,1)}, bf16[24,64,152]{2,1,0:T(8,12...) fusion(bf16[24,70,152]{2,1,0:T(8,128)(2,1)S(1)} %select_maximum_fusion), kind=kLoop, calls=%fused_computation.151 | loop fusion | bytes 6537216 | tf_op jit(solution)/shard_map/slice | solution.py:68
  71.5 8.4 %concatenate.19 = bf16[24,64,1064]{2,1,0:T(8,128)(2,1)} concatenate(bf16[24,64,152]{2,1,0:T(8,128)(2,1)} %get-tuple-element.126, bf16[24,64,152]{2,1,0:T(8,128)(2,1)} %get-tuple-element.125, bf16[24,64,152]{2,1,0:T(8,128)(2,1)} %get-tuple-element.124, bf16[24,64,152]{2,1,0:T(8,128)(2,1)} %get-tuple-element.123, bf16[24,64,152]{2,1,0:T(8,128)(2,1)} %get-tuple-element.122, ...), dimensions={2} | concatenate | bytes 6537216 | tf_op jit(solution)/shard_map/concatenate | solution.py:67
  80.0 12.4 %pad_slice_fusion.18 = (bf16[16,64,1152]{2,1,0:T(8,128)(2,1)S(1)}, bf16[16,64,1152]{2,1,0:T(8,128)(2,1)S(1)}, bf16[16,64,1152]{2,1,0:T(8,128)(2,1)S(1)}, bf16[16...) fusion(bf16[24,64,1064]{2,1,0:T(8,128)(2,1)} %concatenate.19), kind=kLoop, calls=%fused_computation.98 | loop fusion | bytes 24502272 | tf_op jit(solution)/shard_map/slice | solution.py:74
  100.7 103.7 %all-gather.2.cloned.1.call-done = f32[16,16,128,128]{3,2,1,0:T(8,128)} async-done(((f32[1,16,128,128]{3,2,1,0:T(8,128)}), f32[16,16,128,128]{3,2,1,0:T(8,128)}) %all-gather.2.cloned.1.call-update) | async-done | bytes 16777232 | tf_op jit(solution)/shard_map/all_gather | solution.py:37
  205.7 22.7 %while.15 = (s32[]{:T(128)}, f32[16,128,128]{2,1,0:T(8,128)S(1)}, f32[16,16,128,128]{3,2,1,0:T(8,128)}, s32[]{:T(128)}, s32[]{:T(128)}, /*index=5*/s32[]{:T(128)}) while((s32[]{:T(128)}, f32[16,128,128]{2,1,0:T(8,128)S(1)}, f32[16,16,128,128]{3,2,1,0:T(8,128)}, s32[]{:T(128)}, s32[]{:T(128)}, /*index=5*/s32[]{:T(128)}) %tuple.69), condition=%wide.region_2.3_spmd, body=%wide.region_1.2_spmd.sunk | while | flops 262149 | bytes 3145843 | solution.py:42
  205.7 1.6 bitcast_multiply_fusion.2
  207.3 1.5 bitcast_multiply_fusion.2
  208.8 1.5 bitcast_multiply_fusion.2
  210.3 1.5 bitcast_multiply_fusion.2
  211.8 1.5 bitcast_multiply_fusion.2
  213.3 1.5 bitcast_multiply_fusion.2
  214.9 1.5 bitcast_multiply_fusion.2
  216.4 1.5 bitcast_multiply_fusion.2
  (61 shorter events, 36.6 us)
Async XLA Ops:
  6.5 197.8 %all-gather.2.cloned.1.call-start = ((), (), s32[]{:S(2)}) async-start(), calls=%async_computation | async-start | bytes 17825792 | tf_op jit(solution)/shard_map/all_gather | solution.py:37
  7.9 14.2 %collective-permute-start = (bf16[4,128,128]{2,1,0:T(8,128)(2,1)S(1)}, bf16[4,128,128]{2,1,0:T(8,128)(2,1)S(1)}, u32[]{:S(2)}, u32[]{:S(2)}) collective-permute-start(bf16[4,128,128]{2,1,0:T(8,128)(2,1)S(1)} %get-tuple-element.135), channel_id=1, source_target_pairs={{0,1},{1,2},{2,3},{3,4},{4,5},{5,6},{6,7},{7,8},{8,9},{9,10},{10,1... | collective-permute-start | bytes 393224 | tf_op jit(solution)/shard_map/ppermute | solution.py:17
  11.8 10.3 %collective-permute-start.1 = (bf16[4,128,128]{2,1,0:T(8,128)(2,1)S(1)}, bf16[4,128,128]{2,1,0:T(8,128)(2,1)S(1)}, u32[]{:S(2)}, u32[]{:S(2)}) collective-permute-start(bf16[4,128,128]{2,1,0:T(8,128)(2,1)S(1)} %get-tuple-element.134), channel_id=1, source_target_pairs={{1,0},{2,1},{3,2},{4,3},{5,4},{6,5},{7,6},{8,7},{9,8},{10,9},{11,1... | collective-permute-start | bytes 393224 | tf_op jit(solution)/shard_map/ppermute | solution.py:19
  19.6 2.2 copy-start.3
  55.2 1.0 copy-start.2
  56.3 1.9 collective-permute-start.2
  58.3 6.9 %collective-permute-start.3 = (bf16[4,70,128]{2,1,0:T(8,128)(2,1)S(1)}, bf16[4,70,128]{2,1,0:T(8,128)(2,1)S(1)}, u32[]{:S(2)}, u32[]{:S(2)}) collective-permute-start(bf16[4,70,128]{2,1,0:T(8,128)(2,1)S(1)} %get-tuple-element.136), channel_id=1, source_target_pairs={{0,1},{1,2},{2,3},{3,4},{4,5},{5,6},{6,7},{7,8},{8,9},{9,10},{10,1... | collective-permute-start | bytes 215048 | tf_op jit(solution)/shard_map/ppermute | solution.py:17
  62.6 5.1 %collective-permute-start.4 = (bf16[4,70,128]{2,1,0:T(8,128)(2,1)S(1)}, bf16[4,70,128]{2,1,0:T(8,128)(2,1)S(1)}, u32[]{:S(2)}, u32[]{:S(2)}) collective-permute-start(bf16[4,70,128]{2,1,0:T(8,128)(2,1)S(1)} %get-tuple-element.137), channel_id=1, source_target_pairs={{1,0},{2,1},{3,2},{4,3},{5,4},{6,5},{7,6},{8,7},{9,8},{10,9},{11,1... | collective-permute-start | bytes 215048 | tf_op jit(solution)/shard_map/ppermute | solution.py:19
  99.7 1.0 copy-start.1
  205.7 22.8 %copy-start = (f32[16,128,128]{2,1,0:T(8,128)S(1)}, f32[16,128,128]{2,1,0:T(8,128)}, u32[]{:S(2)}) copy-start(f32[16,128,128]{2,1,0:T(8,128)} %param.6) | copy-start | bytes 3145732
Sparse Core Ops, SparseCore 0:
  100.8 103.5 all-gather.1
where the time goes:
time: 238 us; the launch traced here: 236 us
  waiting for transfers between devices  106 us (45%)
  local copies, waits for them, and re-layouts  53.3 us (22%)
  other arithmetic  32.7 us (14%)
  matrix products  18.2 us (8%)
  between operations  13.8 us (6%)
  starting transfers between devices  11.9 us (5%)
    all_gather x1, waiting for transfers between devices, merged(): gathered = lax.all_gather(part, axis)  104 us
    slice x2, local copies, waits for them, and re-layouts, convolve(): columns[shift_x:shift_x + rows_x].reshape(rows_x * rows_y, -1)  24.8 us
    mul x15, other arithmetic, local(): product_all = merged(factor, 'view', lambda former, latter: former * latter)  22.4 us
    concatenate x2, local copies, waits for them, and re-layouts, convolve(): jnp.concatenate([padded_part[:, step_y:step_y + rows_y, :] for step_y in...  16.9 us
    dot_general x18, matrix products, convolve(): jnp.dot(columns[shift_x:shift_x + rows_x].reshape(rows_x * rows_y, -1), b...  14 us
    ppermute x2, starting transfers between devices, with_halo(): lax.ppermute(tail, axis, [(i, (i + 1) % count) for i in range(ends)])  8.22 us
    slice x2, local copies, waits for them, and re-layouts, convolve(): padded_part[:, step_y:step_y + rows_y, :]  6.2 us
  transfers between devices with their start and end apart: 6, of which 3 were waited for; matrix products, arithmetic and copies ran while one was open for 5% of the time, Pallas kernels for 0%

commit v1 on v0

--- a/solution.py
+++ b/solution.py
@@ -116,11 +116,15 @@
     padded_quotient = jnp.pad(quotient_rimmed, ((0, 0), (0, 0), (rim_z, rim_z)))
     correction = convolve(padded_quotient, backward, slab_x, share_w)
     share_factor = jnp.where(cell_cover, correction, 1.0)
-    factor = lax.dynamic_update_slice(
-        jnp.ones((slab_x, width_y, depth), jnp.float32), share_factor, (0, y_start, 0)
-    )
-    product_all = merged(factor, "view", lambda former, latter: former * latter)
-    return estimate * product_all
+    n_view = lax.axis_size("view")
+    step_x = slab_x // n_view
+    rows = share_factor.reshape(n_view, step_x, share_w, depth)
+    got = lax.all_to_all(rows, "view", 0, 0)
+    got = got.reshape(n_view // shares, shares, step_x, share_w, depth)
+    product_rows = jnp.prod(got, axis=0)
+    product_rows = jnp.transpose(product_rows, (1, 0, 2, 3)).reshape(step_x, width_y, depth)
+    mine = lax.dynamic_slice_in_dim(estimate, group * step_x, step_x, axis=0)
+    return lax.all_gather(mine * product_rows, "view", axis=0, tiled=True)
 
 
 def solution(mesh):

time: 238 us -> 177 us (0.74)
  waiting for transfers between devices: 106 us -> 56.6 us
  other arithmetic: 32.7 us -> 11.5 us
  starting transfers between devices: 11.9 us -> 22.2 us
    all_gather x1, waiting for transfers between devices: 104 us -> 39.1 us  [local(): return lax.all_gather(mine * product_rows, 'view', axis=0, tiled=True)]
    mul x16 -> x1, other arithmetic: 23.5 us -> 1.49 us  [local(): return lax.all_gather(mine * product_rows, 'view', axis=0, tiled=True)]
    all_to_all x0 -> x1, waiting for transfers between devices: none -> 17.3 us  [local(): got = lax.all_to_all(rows, 'view', 0, 0)]
    all_to_all x0 -> x1, starting transfers between devices: none -> 9.68 us  [local(): got = lax.all_to_all(rows, 'view', 0, 0)]
    ppermute x2, waiting for transfers between devices: 2.46 us -> 0.01 us  [with_halo(): lax.ppermute(head, axis, [((i + 1) % count, i) for i in range(ends)])]
  transfers between devices with their start and end apart: 6 -> 7, of which waited for: 3 -> 4; matrix products, arithmetic and copies ran while one was open for 5% -> 6% of each run, Pallas kernels for 0% -> 0%
where the time goes in v1:
time: 177 us; the launch traced here: 176 us
  waiting for transfers between devices  56.6 us (32%)
  local copies, waits for them, and re-layouts  53.6 us (30%)
  starting transfers between devices  22.2 us (13%)
  matrix products  18.2 us (10%)
  between operations  13.7 us (8%)
  other arithmetic  11.5 us (6%)
    all_gather x1, waiting for transfers between devices, local(): return lax.all_gather(mine * product_rows, 'view', axis=0, tiled=True)  39.1 us
    slice x2, local copies, waits for them, and re-layouts, convolve(): columns[shift_x:shift_x + rows_x].reshape(rows_x * rows_y, -1)  25.2 us
    all_to_all x1, waiting for transfers between devices, local(): got = lax.all_to_all(rows, 'view', 0, 0)  17.3 us
    concatenate x2, local copies, waits for them, and re-layouts, convolve(): jnp.concatenate([padded_part[:, step_y:step_y + rows_y, :] for step_y in...  16.9 us
    dot_general x18, matrix products, convolve(): jnp.dot(columns[shift_x:shift_x + rows_x].reshape(rows_x * rows_y, -1), b...  14 us
    all_to_all x1, starting transfers between devices, local(): got = lax.all_to_all(rows, 'view', 0, 0)  9.68 us
    ppermute x2, starting transfers between devices, with_halo(): lax.ppermute(tail, axis, [(i, (i + 1) % count) for i in range(ends)])  8.85 us
    slice x2, local copies, waits for them, and re-layouts, convolve(): padded_part[:, step_y:step_y + rows_y, :]  6.25 us
  transfers between devices with their start and end apart: 7, of which 4 were waited for; matrix products, arithmetic and copies ran while one was open for 6% of the time, Pallas kernels for 0%

profile of v1, /device:TPU:1, one launch (start us, length us, event | category | flops | bytes accessed | tf_op | source)
XLA Modules:
  0.0 175.8 jit_solution(12433264027804252495)
XLA Ops:
  6.5 1.3 convert_element_type.38
  7.9 4.0 %collective-permute-start = (bf16[4,128,128]{2,1,0:T(8,128)(2,1)S(1)}, bf16[4,128,128]{2,1,0:T(8,128)(2,1)S(1)}, u32[]{:S(2)}, u32[]{:S(2)}) collective-permute-start(bf16[4,128,128]{2,1,0:T(8,128)(2,1)S(1)} %get-tuple-element.40), channel_id=1, source_target_pairs={{0,1},{1,2},{2,3},{3,4},{4,5},{5,6},{6,7},{7,8},{8,9},{9,10},{10,1... | collective-permute-start | bytes 393224 | tf_op jit(solution)/shard_map/ppermute | solution.py:17
  11.8 1.3 collective-permute-start.1
  13.2 1.7 fusion.97
  14.8 3.2 %fusion.10 = bf16[9,7,152,128]{3,1,2,0:T(8,128)(2,1)} fusion(f32[1,9,7,25]{3,0,2,1:T(1,128)S(1)} %get-tuple-element.6, f32[]{:T(128)} %get-tuple-element.5), kind=kOutput, calls=%fused_computation.13 | convolution fusion | flops 63488080 | bytes 2457760 | tf_op jit(solution)/shard_map/abt,tpz->abpz/dot_general | solution.py:55
  18.0 1.6 iota_compare_fusion
  19.6 2.1 %copy.10 = bf16[9,7,152,128]{3,2,1,0:T(8,128)(2,1)S(1)} copy(bf16[9,7,152,128]{3,1,2,0:T(8,128)(2,1)} %fusion.10) | data formatting | bytes 4902912 | tf_op jit(solution)/shard_map/convert_element_type | solution.py:55
  22.1 2.9 %fusion.23 = bf16[24,70,152]{2,1,0:T(8,128)(2,1)S(1)} fusion(s32[]{:T(128)S(6)} %select_n.67, bf16[4,128,128]{2,1,0:T(8,128)(2,1)S(1)} %collective-permute-done, bf16[16,128,128]{2,1,0:T(8,128)(2,1)S(1)} %convert_element_type.38, pred[24,134,152]{2,1,0:T(8,128)(4,1)} %get-tuple-element.45, pred[24,134,152]{2,1,0:T(8,128)(4,1)} %get-tuple-element.46, ...), kind=kLoop, calls=%fused_computation.61 | loop fusion | flops 5873280 | bytes 1808896 | tf_op jit(solution)/shard_map/concatenate | solution.py:15
  25.0 3.1 %fusion.99 = (bf16[24,64,152]{2,1,0:T(8,128)(2,1)S(1)}, bf16[24,64,152]{2,1,0:T(8,128)(2,1)}, bf16[24,64,152]{2,1,0:T(8,128)(2,1)}, bf16[24,64,152]{2,1,0:T(8,12...) fusion(bf16[24,70,152]{2,1,0:T(8,128)(2,1)S(1)} %fusion.23), kind=kLoop, calls=%fused_computation.152 | loop fusion | bytes 6537216 | tf_op jit(solution)/shard_map/slice | solution.py:68
  28.1 8.4 %concatenate.16 = bf16[24,64,1064]{2,1,0:T(8,128)(2,1)} concatenate(bf16[24,64,152]{2,1,0:T(8,128)(2,1)} %get-tuple-element.38, bf16[24,64,152]{2,1,0:T(8,128)(2,1)} %get-tuple-element.37, bf16[24,64,152]{2,1,0:T(8,128)(2,1)} %get-tuple-element.36, bf16[24,64,152]{2,1,0:T(8,128)(2,1)} %get-tuple-element.35, bf16[24,64,152]{2,1,0:T(8,128)(2,1)} %get-tuple-element.34, ...), dimensions={2} | concatenate | bytes 6537216 | tf_op jit(solution)/shard_map/concatenate | solution.py:67
  36.5 12.6 %pad_slice_fusion.27 = (bf16[16,64,1152]{2,1,0:T(8,128)(2,1)S(1)}, bf16[16,64,1152]{2,1,0:T(8,128)(2,1)S(1)}, bf16[16,64,1152]{2,1,0:T(8,128)(2,1)S(1)}, bf16[16...) fusion(bf16[24,64,1064]{2,1,0:T(8,128)(2,1)} %concatenate.16), kind=kLoop, calls=%fused_computation.106 | loop fusion | bytes 24502272 | tf_op jit(solution)/shard_map/slice | solution.py:74
  56.6 1.1 collective-permute-start.2
  58.6 1.3 collective-permute-start.4
  59.9 4.9 %collective-permute-start.3 = (bf16[4,70,128]{2,1,0:T(8,128)(2,1)S(1)}, bf16[4,70,128]{2,1,0:T(8,128)(2,1)S(1)}, u32[]{:S(2)}, u32[]{:S(2)}) collective-permute-start(bf16[4,70,128]{2,1,0:T(8,128)(2,1)S(1)} %get-tuple-element.41), channel_id=1, source_target_pairs={{0,1},{1,2},{2,3},{3,4},{4,5},{5,6},{6,7},{7,8},{8,9},{9,10},{10,1... | collective-permute-start | bytes 215048 | tf_op jit(solution)/shard_map/ppermute | solution.py:17
  64.8 1.0 fusion.13
  66.8 3.1 %fusion.98 = (bf16[24,64,152]{2,1,0:T(8,128)(2,1)S(1)}, bf16[24,64,152]{2,1,0:T(8,128)(2,1)}, bf16[24,64,152]{2,1,0:T(8,128)(2,1)}, bf16[24,64,152]{2,1,0:T(8,12...) fusion(bf16[24,70,152]{2,1,0:T(8,128)(2,1)S(1)} %select_maximum_fusion), kind=kLoop, calls=%fused_computation.151 | loop fusion | bytes 6537216 | tf_op jit(solution)/shard_map/slice | solution.py:68
  70.0 8.4 %concatenate.19 = bf16[24,64,1064]{2,1,0:T(8,128)(2,1)} concatenate(bf16[24,64,152]{2,1,0:T(8,128)(2,1)} %get-tuple-element.31, bf16[24,64,152]{2,1,0:T(8,128)(2,1)} %get-tuple-element.30, bf16[24,64,152]{2,1,0:T(8,128)(2,1)} %get-tuple-element.29, bf16[24,64,152]{2,1,0:T(8,128)(2,1)} %get-tuple-element.28, bf16[24,64,152]{2,1,0:T(8,128)(2,1)} %get-tuple-element.27, ...), dimensions={2} | concatenate | bytes 6537216 | tf_op jit(solution)/shard_map/concatenate | solution.py:67
  78.4 12.6 %pad_slice_fusion.18 = (bf16[16,64,1152]{2,1,0:T(8,128)(2,1)S(1)}, bf16[16,64,1152]{2,1,0:T(8,128)(2,1)S(1)}, bf16[16,64,1152]{2,1,0:T(8,128)(2,1)S(1)}, bf16[16...) fusion(bf16[24,64,1064]{2,1,0:T(8,128)(2,1)} %concatenate.19), kind=kLoop, calls=%fused_computation.97 | loop fusion | bytes 24502272 | tf_op jit(solution)/shard_map/slice | solution.py:74
  98.1 0.9 broadcast_select_fusion
  99.0 9.7 %all-to-all-start = ((f32[16,1,64,128]{3,2,1,0:T(8,128)}), f32[16,1,64,128]{3,2,1,0:T(8,128)S(1)}, u32[]{:S(2)}, u32[]{:S(2)}) async-start(f32[16,1,64,128]{3,2,1,0:T(8,128)} %broadcast_select_fusion), calls=%async_computation | async-start | bytes 1048576 | tf_op jit(solution)/shard_map/all_to_all | solution.py:122
  108.7 17.3 %all-to-all-done = f32[16,1,64,128]{3,2,1,0:T(8,128)S(1)} async-done(((f32[16,1,64,128]{3,2,1,0:T(8,128)}), f32[16,1,64,128]{3,2,1,0:T(8,128)S(1)}, u32[]{:S(2)}, u32[]{:S(2)}) %all-to-all-start) | async-done | bytes 524320 | tf_op jit(solution)/shard_map/all_to_all | solution.py:122
  126.0 1.5 bitcast_multiply_fusion
  127.5 39.1 %all-gather.2.cloned.1.call-done = f32[16,128,128]{2,1,0:T(8,128)} async-done(((f32[1,128,128]{2,1,0:T(8,128)}), f32[16,128,128]{2,1,0:T(8,128)}) %all-gather.2.cloned.1.call-update) | async-done | bytes 1048592 | tf_op jit(solution)/shard_map/all_gather | solution.py:127
  166.7 2.3 %copy.26 = f32[16,128,128]{2,1,0:T(8,128)} copy(f32[16,128,128]{2,1,0:T(8,128)} %all-gather.2.cloned.1.call-done) | data formatting | bytes 2097152
  (43 shorter events, 16.8 us)
Async XLA Ops:
  7.9 14.2 %collective-permute-start = (bf16[4,128,128]{2,1,0:T(8,128)(2,1)S(1)}, bf16[4,128,128]{2,1,0:T(8,128)(2,1)S(1)}, u32[]{:S(2)}, u32[]{:S(2)}) collective-permute-start(bf16[4,128,128]{2,1,0:T(8,128)(2,1)S(1)} %get-tuple-element.40), channel_id=1, source_target_pairs={{0,1},{1,2},{2,3},{3,4},{4,5},{5,6},{6,7},{7,8},{8,9},{9,10},{10,1... | collective-permute-start | bytes 393224 | tf_op jit(solution)/shard_map/ppermute | solution.py:17
  11.8 10.3 %collective-permute-start.1 = (bf16[4,128,128]{2,1,0:T(8,128)(2,1)S(1)}, bf16[4,128,128]{2,1,0:T(8,128)(2,1)S(1)}, u32[]{:S(2)}, u32[]{:S(2)}) collective-permute-start(bf16[4,128,128]{2,1,0:T(8,128)(2,1)S(1)} %get-tuple-element.39), channel_id=1, source_target_pairs={{1,0},{2,1},{3,2},{4,3},{5,4},{6,5},{7,6},{8,7},{9,8},{10,9},{11,1... | collective-permute-start | bytes 393224 | tf_op jit(solution)/shard_map/ppermute | solution.py:19
  19.6 2.2 %copy-start.1 = (s32[8,1,4]{0,2,1:T(4,128)S(1)}, s32[8,1,4]{0,2,1:T(4,128)}, u32[]{:S(2)}) copy-start(s32[8,1,4]{0,2,1:T(4,128)} %param.7) | copy-start | bytes 388
  55.4 1.0 copy-start
  56.6 1.9 %collective-permute-start.2 = (bf16[16,3,128]{2,1,0:T(4,128)(2,1)S(1)}, bf16[16,3,128]{2,1,0:T(4,128)(2,1)S(1)}, u32[]{:S(2)}, u32[]{:S(2)}) collective-permute-start(bf16[16,3,128]{2,1,0:T(4,128)(2,1)S(1)} %slice_select_fusion), channel_id=1, source_target_pairs={{0,16},{16,0},{32,48},{48,32},{64,80},{80,64},{96,112},{112,96},{1... | collective-permute-start | bytes 36872 | tf_op jit(solution)/shard_map/ppermute | solution.py:33
  58.6 7.5 %collective-permute-start.4 = (bf16[4,70,128]{2,1,0:T(8,128)(2,1)S(1)}, bf16[4,70,128]{2,1,0:T(8,128)(2,1)S(1)}, u32[]{:S(2)}, u32[]{:S(2)}) collective-permute-start(bf16[4,70,128]{2,1,0:T(8,128)(2,1)S(1)} %get-tuple-element.42), channel_id=1, source_target_pairs={{1,0},{2,1},{3,2},{4,3},{5,4},{6,5},{7,6},{8,7},{9,8},{10,9},{11,1... | collective-permute-start | bytes 215048 | tf_op jit(solution)/shard_map/ppermute | solution.py:19
  59.9 6.3 %collective-permute-start.3 = (bf16[4,70,128]{2,1,0:T(8,128)(2,1)S(1)}, bf16[4,70,128]{2,1,0:T(8,128)(2,1)S(1)}, u32[]{:S(2)}, u32[]{:S(2)}) collective-permute-start(bf16[4,70,128]{2,1,0:T(8,128)(2,1)S(1)} %get-tuple-element.41), channel_id=1, source_target_pairs={{0,1},{1,2},{2,3},{3,4},{4,5},{5,6},{6,7},{7,8},{8,9},{9,10},{10,1... | collective-permute-start | bytes 215048 | tf_op jit(solution)/shard_map/ppermute | solution.py:17
  99.0 27.0 %all-to-all-start = ((f32[16,1,64,128]{3,2,1,0:T(8,128)}), f32[16,1,64,128]{3,2,1,0:T(8,128)S(1)}, u32[]{:S(2)}, u32[]{:S(2)}) async-start(f32[16,1,64,128]{3,2,1,0:T(8,128)} %broadcast_select_fusion), calls=%async_computation | async-start | bytes 1048576 | tf_op jit(solution)/shard_map/all_to_all | solution.py:122
  108.7 58.0 %all-gather.2.cloned.1.call-start = ((), (), s32[]{:S(2)}) async-start(), calls=%async_computation.1 | async-start | bytes 1114112 | tf_op jit(solution)/shard_map/all_gather | solution.py:127
Sparse Core Ops, SparseCore 0:
  127.7 38.9 all-gather.1

commit v2 on v1

--- a/solution.py
+++ b/solution.py
@@ -46,19 +46,18 @@
 
 def band_table(kernel, depth):
     taps_x, taps_y, taps_z = kernel.shape
-    span_z = depth + taps_z - 1
-    shape_three = (taps_z, span_z, depth)
+    rim_z = (taps_z - 1) // 2
+    shape_three = (taps_z, depth, depth)
     offset = lax.broadcasted_iota(jnp.int32, shape_three, 1) - lax.broadcasted_iota(
         jnp.int32, shape_three, 2
     )
-    onehot = (offset == lax.broadcasted_iota(jnp.int32, shape_three, 0)).astype(jnp.bfloat16)
+    onehot = (offset + rim_z == lax.broadcasted_iota(jnp.int32, shape_three, 0)).astype(
+        jnp.bfloat16
+    )
     banded = jnp.einsum("abt,tpz->abpz", kernel, onehot, preferred_element_type=jnp.float32).astype(
         jnp.bfloat16
     )
-    inner_width = taps_y * span_z
-    padded_width = -(-inner_width // 128) * 128
-    banded = banded.reshape(taps_x, inner_width, depth)
-    return jnp.pad(banded, ((0, 0), (0, padded_width - inner_width), (0, 0)))
+    return banded.reshape(taps_x, taps_y * depth, depth)
 
 
 def convolve(padded_part, banded, rows_x, rows_y):
@@ -67,7 +66,6 @@
     columns = jnp.concatenate(
         [padded_part[:, step_y : step_y + rows_y, :] for step_y in range(taps_y)], axis=2
     )
-    columns = jnp.pad(columns, ((0, 0), (0, 0), (0, banded.shape[1] - columns.shape[2])))
     output = None
     for shift_x in range(taps_x):
         partial_sum = jnp.dot(
@@ -92,7 +90,7 @@
     y_start = part * share_w
     source = estimate.astype(jnp.bfloat16)
     rimmed = with_halo(source, (("blk", 0),), rim_x)
-    padded = jnp.pad(rimmed, ((0, 0), (rim_y, rim_y), (rim_z, rim_z)))
+    padded = jnp.pad(rimmed, ((0, 0), (rim_y, rim_y), (0, 0)))
     spread = lax.dynamic_index_in_dim(point_spread, view_id, 0, keepdims=False)
     kernel = (spread / jnp.sum(spread)).astype(jnp.bfloat16)
     forward = band_table(kernel, depth)
@@ -102,7 +100,7 @@
     cell_cover = jnp.repeat(share_cover, BY)[None, :, None]
     image = images[0]
     region = lax.dynamic_slice(
-        padded, (0, y_start, 0), (slab_x + 2 * rim_x, share_w + 2 * rim_y, depth + 2 * rim_z)
+        padded, (0, y_start, 0), (slab_x + 2 * rim_x, share_w + 2 * rim_y, depth)
     )
     blurred = convolve(region, forward, slab_x, share_w)
     quotient = jnp.where(cell_cover, image.astype(jnp.float32) / blurred, 0.0).astype(jnp.bfloat16)
@@ -113,8 +111,7 @@
     upper_rim = jnp.where(part < shares - 1, partner, rim_zeros)
     extended = jnp.concatenate([lower_rim, quotient, upper_rim], axis=1)
     quotient_rimmed = with_halo(extended, (("blk", 0),), rim_x)
-    padded_quotient = jnp.pad(quotient_rimmed, ((0, 0), (0, 0), (rim_z, rim_z)))
-    correction = convolve(padded_quotient, backward, slab_x, share_w)
+    correction = convolve(quotient_rimmed, backward, slab_x, share_w)
     share_factor = jnp.where(cell_cover, correction, 1.0)
     n_view = lax.axis_size("view")
     step_x = slab_x // n_view

time: 177 us -> 129 us (0.73)
  local copies, waits for them, and re-layouts: 53.6 us -> 12.9 us
  other arithmetic: 11.5 us -> 6.78 us
  matrix products: 18.2 us -> 14 us
    slice x2, local copies, waits for them, and re-layouts: 25.2 us -> 6.38 us  [convolve(): columns[shift_x:shift_x + rows_x].reshape(rows_x * rows_y, -1)]
    concatenate x2, local copies, waits for them, and re-layouts: 16.9 us -> 0.34 us  [convolve(): jnp.concatenate([padded_part[:, step_y:step_y + rows_y, :] for step_y in...]
    slice x2 -> x20, local copies, waits for them, and re-layouts: 6.25 us -> 0.94 us  [convolve(): banded[shift_x]]
    concatenate x2, other arithmetic: 3.59 us -> 0.44 us  [with_halo(): jnp.concatenate([lax.ppermute(tail, axis, [(i, (i + 1) % count) for i in...]
    convert_element_type x2 -> x0, local copies, waits for them, and re-layouts: 2.47 us -> none  [band_table(): jnp.einsum('abt,tpz->abpz', kernel, onehot, preferred_element_type=jnp.fl...]
    unnamed x5 -> x17, local copies, waits for them, and re-layouts: 2.46 us -> 4.82 us
    dot_general x18, matrix products: 14 us -> 11.7 us  [convolve(): jnp.dot(columns[shift_x:shift_x + rows_x].reshape(rows_x * rows_y, -1), b...]
  transfers between devices with their start and end apart: 7 -> 7, of which waited for: 4 -> 3; matrix products, arithmetic and copies ran while one was open for 6% -> 5% of each run, Pallas kernels for 0% -> 0%
where the time goes in v2:
time: 129 us; the launch traced here: 128 us
  waiting for transfers between devices  58.2 us (45%)
  starting transfers between devices  22.3 us (17%)
  matrix products  14 us (11%)
  between operations  14 us (11%)
  local copies, waits for them, and re-layouts  12.9 us (10%)
  other arithmetic  6.78 us (5%)
    all_gather x1, waiting for transfers between devices, local(): return lax.all_gather(mine * product_rows, 'view', axis=0, tiled=True)  40.3 us
    all_to_all x1, waiting for transfers between devices, local(): got = lax.all_to_all(rows, 'view', 0, 0)  17.3 us
    dot_general x18, matrix products, convolve(): jnp.dot(columns[shift_x:shift_x + rows_x].reshape(rows_x * rows_y, -1), b...  11.7 us
    all_to_all x1, starting transfers between devices, local(): got = lax.all_to_all(rows, 'view', 0, 0)  9.63 us
    ppermute x2, starting transfers between devices, with_halo(): lax.ppermute(tail, axis, [(i, (i + 1) % count) for i in range(ends)])  8.75 us
    slice x2, local copies, waits for them, and re-layouts, convolve(): columns[shift_x:shift_x + rows_x].reshape(rows_x * rows_y, -1)  6.38 us
    unnamed x17, local copies, waits for them, and re-layouts  4.82 us
    ppermute x2, starting transfers between devices, with_halo(): lax.ppermute(head, axis, [((i + 1) % count, i) for i in range(ends)])  2.58 us
  transfers between devices with their start and end apart: 7, of which 3 were waited for; matrix products, arithmetic and copies ran while one was open for 5% of the time, Pallas kernels for 0%

profile of v2, /device:TPU:1, one launch (start us, length us, event | category | flops | bytes accessed | tf_op | source)
XLA Modules:
  0.0 128.2 jit_solution(17272270914108477657)
XLA Ops:
  6.5 1.3 %convert_element_type.30 = bf16[16,128,128]{2,1,0:T(8,128)(2,1)S(1)} convert(f32[16,128,128]{2,1,0:T(8,128)} %param.4) | non-fusion elementwise | flops 262144 | bytes 1572864 | tf_op jit(solution)/shard_map/convert_element_type | solution.py:91
  7.9 4.0 %collective-permute-start = (bf16[4,128,128]{2,1,0:T(8,128)(2,1)S(1)}, bf16[4,128,128]{2,1,0:T(8,128)(2,1)S(1)}, u32[]{:S(2)}, u32[]{:S(2)}) collective-permute-start(bf16[4,128,128]{2,1,0:T(8,128)(2,1)S(1)} %get-tuple-element.44), channel_id=1, source_target_pairs={{0,1},{1,2},{2,3},{3,4},{4,5},{5,6},{6,7},{7,8},{8,9},{9,10},{10,1... | collective-permute-start | bytes 393224 | tf_op jit(solution)/shard_map/ppermute | solution.py:17
  11.8 1.3 %collective-permute-start.1 = (bf16[4,128,128]{2,1,0:T(8,128)(2,1)S(1)}, bf16[4,128,128]{2,1,0:T(8,128)(2,1)S(1)}, u32[]{:S(2)}, u32[]{:S(2)}) collective-permute-start(bf16[4,128,128]{2,1,0:T(8,128)(2,1)S(1)} %get-tuple-element.43), channel_id=1, source_target_pairs={{1,0},{2,1},{3,2},{4,3},{5,4},{6,5},{7,6},{8,7},{9,8},{10,9},{11,1... | collective-permute-start | bytes 393224 | tf_op jit(solution)/shard_map/ppermute | solution.py:19
  13.2 1.6 %fusion.30 = (f32[]{:T(128)}, f32[1,9,7,25]{3,0,2,1:T(1,128)S(1)}) fusion(f32[8,9,7,25]{3,0,2,1:T(8,128)} %param.6, s32[]{:T(128)S(6)} %select_n.62), kind=kLoop, calls=%fused_computation.73 | loop fusion | flops 1574 | bytes 12608 | tf_op jit(solution)/shard_map/reduce_sum | solution.py:95
  14.8 1.5 %fusion.5 = bf16[9,7,128,128]{3,1,2,0:T(8,128)(2,1)S(1)} fusion(f32[1,9,7,25]{3,0,2,1:T(1,128)S(1)} %get-tuple-element.6, f32[]{:T(128)} %get-tuple-element.5), kind=kOutput, calls=%fused_computation.4 | convolution fusion | flops 53873744 | bytes 2070688 | tf_op jit(solution)/shard_map/abt,tpz->abpz/dot_general | solution.py:57
  17.6 0.7 fusion.29
  19.9 3.2 %fusion.32 = (bf16[16,64,896]{2,1,0:T(8,128)(2,1)S(1)}, bf16[16,64,896]{2,1,0:T(8,128)(2,1)S(1)}, bf16[16,64,896]{2,1,0:T(8,128)(2,1)S(1)}, bf16[16,64,896]{2,1,...) fusion(bf16[24,64,896]{2,1,0:T(8,128)(2,1)S(1)} %slice_dynamic-, ...), kind=kLoop, calls=%fused_computation.75 | loop fusion | bytes 33030144 | tf_op jit(solution)/shard_map/slice | solution.py:72
  23.8 0.7 convolution_add_fusion.15
  24.4 0.6 convolution_add_fusion.14
  25.7 0.6 convolution_add_fusion.12
  28.4 0.7 convolution_add_fusion.8
  29.5 1.3 %collective-permute-start.2 = (bf16[16,3,128]{2,1,0:T(4,128)(2,1)S(1)}, bf16[16,3,128]{2,1,0:T(4,128)(2,1)S(1)}, u32[]{:S(2)}, u32[]{:S(2)}) collective-permute-start(bf16[16,3,128]{2,1,0:T(4,128)(2,1)S(1)} %slice_select_fusion), channel_id=1, source_target_pairs={{0,16},{16,0},{32,48},{48,32},{64,80},{80,64},{96,112},{112,96},{1... | collective-permute-start | bytes 36872 | tf_op jit(solution)/shard_map/ppermute | solution.py:33
  30.8 0.9 fusion.8
  31.8 1.3 %collective-permute-start.4 = (bf16[4,70,128]{2,1,0:T(8,128)(2,1)S(1)}, bf16[4,70,128]{2,1,0:T(8,128)(2,1)S(1)}, u32[]{:S(2)}, u32[]{:S(2)}) collective-permute-start(bf16[4,70,128]{2,1,0:T(8,128)(2,1)S(1)} %get-tuple-element.46), channel_id=1, source_target_pairs={{1,0},{2,1},{3,2},{4,3},{5,4},{6,5},{7,6},{8,7},{9,8},{10,9},{11,1... | collective-permute-start | bytes 215048 | tf_op jit(solution)/shard_map/ppermute | solution.py:19
  33.1 4.8 %collective-permute-start.3 = (bf16[4,70,128]{2,1,0:T(8,128)(2,1)S(1)}, bf16[4,70,128]{2,1,0:T(8,128)(2,1)S(1)}, u32[]{:S(2)}, u32[]{:S(2)}) collective-permute-start(bf16[4,70,128]{2,1,0:T(8,128)(2,1)S(1)} %get-tuple-element.45), channel_id=1, source_target_pairs={{0,1},{1,2},{2,3},{3,4},{4,5},{5,6},{6,7},{7,8},{8,9},{9,10},{10,1... | collective-permute-start | bytes 215048 | tf_op jit(solution)/shard_map/ppermute | solution.py:17
  40.3 3.2 %fusion.31 = (bf16[16,64,896]{2,1,0:T(8,128)(2,1)S(1)}, bf16[16,64,896]{2,1,0:T(8,128)(2,1)S(1)}, bf16[16,64,896]{2,1,0:T(8,128)(2,1)S(1)}, bf16[16,64,896]{2,1,...) fusion(bf16[24,64,896]{2,1,0:T(8,128)(2,1)S(1)} %slice_dynamic-, ...), kind=kLoop, calls=%fused_computation.74 | loop fusion | bytes 33030144 | tf_op jit(solution)/shard_map/slice | solution.py:72
  44.2 0.7 convolution_add_fusion.7
  44.8 0.6 convolution_add_fusion.6
  49.4 0.9 broadcast_select_fusion
  50.3 9.6 %all-to-all-start = ((f32[16,1,64,128]{3,2,1,0:T(8,128)}), f32[16,1,64,128]{3,2,1,0:T(8,128)S(1)}, u32[]{:S(2)}, u32[]{:S(2)}) async-start(f32[16,1,64,128]{3,2,1,0:T(8,128)} %broadcast_select_fusion), calls=%async_computation | async-start | bytes 1048576 | tf_op jit(solution)/shard_map/all_to_all | solution.py:119
  60.0 17.3 %all-to-all-done = f32[16,1,64,128]{3,2,1,0:T(8,128)S(1)} async-done(((f32[16,1,64,128]{3,2,1,0:T(8,128)}), f32[16,1,64,128]{3,2,1,0:T(8,128)S(1)}, u32[]{:S(2)}, u32[]{:S(2)}) %all-to-all-start) | async-done | bytes 524320 | tf_op jit(solution)/shard_map/all_to_all | solution.py:119
  77.3 1.5 %bitcast_multiply_fusion = f32[1,128,128]{2,1,0:T(8,128)} fusion(f32[16,128,128]{2,1,0:T(8,128)} %param.4, s32[]{:T(128)S(6)} %select_n.60, f32[1,128,128]{2,1,0:T(8,128)S(1)} %bitcast.144), kind=kLoop, calls=%fused_computation.59 | loop fusion | flops 16384 | bytes 196612 | tf_op jit(solution)/shard_map/mul | solution.py:124
  78.8 40.3 %all-gather.2.cloned.1.call-done = f32[16,128,128]{2,1,0:T(8,128)} async-done(((f32[1,128,128]{2,1,0:T(8,128)}), f32[16,128,128]{2,1,0:T(8,128)}) %all-gather.2.cloned.1.call-update) | async-done | bytes 1048592 | tf_op jit(solution)/shard_map/all_gather | solution.py:124
  119.1 2.3 %copy.70 = f32[16,128,128]{2,1,0:T(8,128)} copy(f32[16,128,128]{2,1,0:T(8,128)} %all-gather.2.cloned.1.call-done) | data formatting | bytes 2097152
  (70 shorter events, 13.5 us)
Async XLA Ops:
  7.9 10.5 %collective-permute-start = (bf16[4,128,128]{2,1,0:T(8,128)(2,1)S(1)}, bf16[4,128,128]{2,1,0:T(8,128)(2,1)S(1)}, u32[]{:S(2)}, u32[]{:S(2)}) collective-permute-start(bf16[4,128,128]{2,1,0:T(8,128)(2,1)S(1)} %get-tuple-element.44), channel_id=1, source_target_pairs={{0,1},{1,2},{2,3},{3,4},{4,5},{5,6},{6,7},{7,8},{8,9},{9,10},{10,1... | collective-permute-start | bytes 393224 | tf_op jit(solution)/shard_map/ppermute | solution.py:17
  11.8 6.6 %collective-permute-start.1 = (bf16[4,128,128]{2,1,0:T(8,128)(2,1)S(1)}, bf16[4,128,128]{2,1,0:T(8,128)(2,1)S(1)}, u32[]{:S(2)}, u32[]{:S(2)}) collective-permute-start(bf16[4,128,128]{2,1,0:T(8,128)(2,1)S(1)} %get-tuple-element.43), channel_id=1, source_target_pairs={{1,0},{2,1},{3,2},{4,3},{5,4},{6,5},{7,6},{8,7},{9,8},{10,9},{11,1... | collective-permute-start | bytes 393224 | tf_op jit(solution)/shard_map/ppermute | solution.py:19
  16.6 0.7 copy-start.1
  28.3 1.0 copy-start
  29.5 2.2 %collective-permute-start.2 = (bf16[16,3,128]{2,1,0:T(4,128)(2,1)S(1)}, bf16[16,3,128]{2,1,0:T(4,128)(2,1)S(1)}, u32[]{:S(2)}, u32[]{:S(2)}) collective-permute-start(bf16[16,3,128]{2,1,0:T(4,128)(2,1)S(1)} %slice_select_fusion), channel_id=1, source_target_pairs={{0,16},{16,0},{32,48},{48,32},{64,80},{80,64},{96,112},{112,96},{1... | collective-permute-start | bytes 36872 | tf_op jit(solution)/shard_map/ppermute | solution.py:33
  31.8 6.7 %collective-permute-start.4 = (bf16[4,70,128]{2,1,0:T(8,128)(2,1)S(1)}, bf16[4,70,128]{2,1,0:T(8,128)(2,1)S(1)}, u32[]{:S(2)}, u32[]{:S(2)}) collective-permute-start(bf16[4,70,128]{2,1,0:T(8,128)(2,1)S(1)} %get-tuple-element.46), channel_id=1, source_target_pairs={{1,0},{2,1},{3,2},{4,3},{5,4},{6,5},{7,6},{8,7},{9,8},{10,9},{11,1... | collective-permute-start | bytes 215048 | tf_op jit(solution)/shard_map/ppermute | solution.py:19
  33.1 6.0 %collective-permute-start.3 = (bf16[4,70,128]{2,1,0:T(8,128)(2,1)S(1)}, bf16[4,70,128]{2,1,0:T(8,128)(2,1)S(1)}, u32[]{:S(2)}, u32[]{:S(2)}) collective-permute-start(bf16[4,70,128]{2,1,0:T(8,128)(2,1)S(1)} %get-tuple-element.45), channel_id=1, source_target_pairs={{0,1},{1,2},{2,3},{3,4},{4,5},{5,6},{6,7},{7,8},{8,9},{9,10},{10,1... | collective-permute-start | bytes 215048 | tf_op jit(solution)/shard_map/ppermute | solution.py:17
  50.3 26.9 %all-to-all-start = ((f32[16,1,64,128]{3,2,1,0:T(8,128)}), f32[16,1,64,128]{3,2,1,0:T(8,128)S(1)}, u32[]{:S(2)}, u32[]{:S(2)}) async-start(f32[16,1,64,128]{3,2,1,0:T(8,128)} %broadcast_select_fusion), calls=%async_computation | async-start | bytes 1048576 | tf_op jit(solution)/shard_map/all_to_all | solution.py:119
  60.0 59.1 %all-gather.2.cloned.1.call-start = ((), (), s32[]{:S(2)}) async-start(), calls=%async_computation.1 | async-start | bytes 1114112 | tf_op jit(solution)/shard_map/all_gather | solution.py:124
Sparse Core Ops, SparseCore 0:
  78.9 40.0 all-gather.1

commit v3 on v2

--- a/solution.py
+++ b/solution.py
@@ -1,6 +1,10 @@
+import functools
+
 import jax
 import jax.numpy as jnp
 from jax import lax
+from jax.experimental import pallas as pl
+from jax.experimental.pallas import tpu as pltpu
 from jax.sharding import PartitionSpec as P
 
 BY = 32
@@ -42,6 +46,94 @@
     return lax.fori_loop(
         1, lax.axis_size(axis), lambda source, state: combine(state, take(source)), take(0)
     )
+
+
+def product_kernel(n, shares, factor_ref, est_ref, out_ref, held, send1, recv1, send2, recv2):
+    groups = n // shares
+    step, share_w, depth = held.shape[1:]
+    me = lax.axis_index("view")
+    view_id = me // shares
+    part = me % shares
+    mesh_kind = pl.DeviceIdType.MESH
+    outgoing = []
+    for d in range(1, groups):
+        target = (view_id + d) % groups
+        copy = pltpu.make_async_remote_copy(
+            src_ref=factor_ref.at[pl.ds(target * step, step)],
+            dst_ref=held.at[view_id],
+            send_sem=send1.at[d],
+            recv_sem=recv1.at[d],
+            device_id={"view": target * shares + part},
+            device_id_type=mesh_kind,
+        )
+        copy.start()
+        outgoing.append(copy)
+    acc = factor_ref[pl.ds(view_id * step, step)]
+    for d in range(1, groups):
+        source = (view_id - d + groups) % groups
+        pltpu.make_async_remote_copy(
+            src_ref=factor_ref.at[pl.ds(0, step)],
+            dst_ref=held.at[source],
+            send_sem=send1.at[d],
+            recv_sem=recv1.at[d],
+            device_id={"view": source * shares + part},
+            device_id_type=mesh_kind,
+        ).wait_recv()
+        acc = acc * held[source]
+    for copy in outgoing:
+        copy.wait_send()
+    rows = pl.ds(view_id * step, step)
+    cols = pl.ds(part * share_w, share_w)
+    out_ref[rows, cols, :] = acc * est_ref[rows, cols, :]
+    outgoing = []
+    for d in range(1, n):
+        target = (me + d) % n
+        copy = pltpu.make_async_remote_copy(
+            src_ref=out_ref.at[rows, cols],
+            dst_ref=out_ref.at[rows, cols],
+            send_sem=send2.at[d],
+            recv_sem=recv2.at[d],
+            device_id={"view": target},
+            device_id_type=mesh_kind,
+        )
+        copy.start()
+        outgoing.append(copy)
+    for d in range(1, n):
+        source = (me - d + n) % n
+        src_rows = pl.ds((source // shares) * step, step)
+        src_cols = pl.ds((source % shares) * share_w, share_w)
+        pltpu.make_async_remote_copy(
+            src_ref=out_ref.at[src_rows, src_cols],
+            dst_ref=out_ref.at[src_rows, src_cols],
+            send_sem=send2.at[d],
+            recv_sem=recv2.at[d],
+            device_id={"view": source},
+            device_id_type=mesh_kind,
+        ).wait_recv()
+    for copy in outgoing:
+        copy.wait_send()
+
+
+def product_gather(share_factor, estimate, shares):
+    n = lax.axis_size("view")
+    groups = n // shares
+    slab_x, share_w, depth = share_factor.shape
+    step = slab_x // groups
+    vmem = pl.BlockSpec(memory_space=pltpu.VMEM)
+    return pl.pallas_call(
+        functools.partial(product_kernel, n, shares),
+        out_shape=jax.ShapeDtypeStruct(estimate.shape, jnp.float32),
+        in_specs=[vmem, vmem],
+        out_specs=vmem,
+        scratch_shapes=[
+            pltpu.VMEM((groups, step, share_w, depth), jnp.float32),
+            pltpu.SemaphoreType.DMA((groups,)),
+            pltpu.SemaphoreType.DMA((groups,)),
+            pltpu.SemaphoreType.DMA((n,)),
+            pltpu.SemaphoreType.DMA((n,)),
+        ],
+        compiler_params=pltpu.CompilerParams(has_side_effects=True),
+    )(share_factor, estimate)
 
 
 def band_table(kernel, depth):
@@ -113,15 +205,7 @@
     quotient_rimmed = with_halo(extended, (("blk", 0),), rim_x)
     correction = convolve(quotient_rimmed, backward, slab_x, share_w)
     share_factor = jnp.where(cell_cover, correction, 1.0)
-    n_view = lax.axis_size("view")
-    step_x = slab_x // n_view
-    rows = share_factor.reshape(n_view, step_x, share_w, depth)
-    got = lax.all_to_all(rows, "view", 0, 0)
-    got = got.reshape(n_view // shares, shares, step_x, share_w, depth)
-    product_rows = jnp.prod(got, axis=0)
-    product_rows = jnp.transpose(product_rows, (1, 0, 2, 3)).reshape(step_x, width_y, depth)
-    mine = lax.dynamic_slice_in_dim(estimate, group * step_x, step_x, axis=0)
-    return lax.all_gather(mine * product_rows, "view", axis=0, tiled=True)
+    return product_gather(share_factor, estimate, shares)
 
 
 def solution(mesh):

time: 129 us -> 114 us (0.88)
  Pallas kernels: 0 us -> 66.2 us
  waiting for transfers between devices: 58.2 us -> 3.07 us
  between operations: 14 us -> 0.6 us
  starting transfers between devices: 22.3 us -> 12 us
  other arithmetic: 6.78 us -> 5.26 us
    pallas_call x0 -> x1, Pallas kernels: none -> 66.2 us  [product_gather(): pl.pallas_call(functools.partial(product_kernel, n, shares), out_shape=ja...]
    all_gather x1 -> x0, waiting for transfers between devices: 40.3 us -> none  [local(): return lax.all_gather(mine * product_rows, 'view', axis=0, tiled=True)]
    all_to_all x1 -> x0, waiting for transfers between devices: 17.3 us -> none  [local(): got = lax.all_to_all(rows, 'view', 0, 0)]
    all_to_all x1 -> x0, starting transfers between devices: 9.63 us -> none  [local(): got = lax.all_to_all(rows, 'view', 0, 0)]
    ppermute x2, waiting for transfers between devices: 0.01 us -> 3.06 us  [with_halo(): lax.ppermute(head, axis, [((i + 1) % count, i) for i in range(ends)])]
    mul x1 -> x0, other arithmetic: 1.49 us -> none  [local(): return lax.all_gather(mine * product_rows, 'view', axis=0, tiled=True)]
  transfers between devices with their start and end apart: 7 -> 5, of which waited for: 3 -> 1; matrix products, arithmetic and copies ran while one was open for 5% -> 5% of each run, Pallas kernels for 0% -> 0%
where the time goes in v3:
time: 114 us
  Pallas kernels  66.2 us (58%)
  matrix products  14 us (12%)
  local copies, waits for them, and re-layouts  12.9 us (11%)
  starting transfers between devices  12 us (11%)
  other arithmetic  5.26 us (5%)
  waiting for transfers between devices  3.07 us (3%)
    pallas_call x1, Pallas kernels, product_gather(): pl.pallas_call(functools.partial(product_kernel, n, shares), out_shape=ja...  66.2 us
    dot_general x18, matrix products, convolve(): jnp.dot(columns[shift_x:shift_x + rows_x].reshape(rows_x * rows_y, -1), b...  11.6 us
    ppermute x2, starting transfers between devices, with_halo(): lax.ppermute(tail, axis, [(i, (i + 1) % count) for i in range(ends)])  7.94 us
    slice x2, local copies, waits for them, and re-layouts, convolve(): columns[shift_x:shift_x + rows_x].reshape(rows_x * rows_y, -1)  6.38 us
    unnamed x17, local copies, waits for them, and re-layouts  4.83 us
    ppermute x2, waiting for transfers between devices, with_halo(): lax.ppermute(head, axis, [((i + 1) % count, i) for i in range(ends)])  3.06 us
    ppermute x2, starting transfers between devices, with_halo(): lax.ppermute(head, axis, [((i + 1) % count, i) for i in range(ends)])  2.76 us
    dot_general x2, matrix products, band_table(): jnp.einsum('abt,tpz->abpz', kernel, onehot, preferred_element_type=jnp.fl...  2.37 us
  transfers between devices with their start and end apart: 5, of which 1 were waited for; matrix products, arithmetic and copies ran while one was open for 5% of the time, Pallas kernels for 0%

profile of v3, /device:TPU:1, one launch (start us, length us, event | category | flops | bytes accessed | tf_op | source)
XLA Modules:
  0.0 114.1 jit_solution(15790567491973956357)
XLA Ops:
  0.0 1.3 %convert_element_type.30 = bf16[16,128,128]{2,1,0:T(8,128)(2,1)S(1)} convert(f32[16,128,128]{2,1,0:T(8,128)} %est_ref.1) | non-fusion elementwise | flops 262144 | bytes 1572864 | tf_op jit(solution)/shard_map/convert_element_type | solution.py:183
  1.3 4.0 %collective-permute-start = (bf16[4,128,128]{2,1,0:T(8,128)(2,1)S(1)}, bf16[4,128,128]{2,1,0:T(8,128)(2,1)S(1)}, u32[]{:S(2)}, u32[]{:S(2)}) collective-permute-start(bf16[4,128,128]{2,1,0:T(8,128)(2,1)S(1)} %get-tuple-element.44), channel_id=1, source_target_pairs={{0,1},{1,2},{2,3},{3,4},{4,5},{5,6},{6,7},{7,8},{8,9},{9,10},{10,1... | collective-permute-start | bytes 393224 | tf_op jit(solution)/shard_map/ppermute | solution.py:21
  5.3 1.3 %collective-permute-start.1 = (bf16[4,128,128]{2,1,0:T(8,128)(2,1)S(1)}, bf16[4,128,128]{2,1,0:T(8,128)(2,1)S(1)}, u32[]{:S(2)}, u32[]{:S(2)}) collective-permute-start(bf16[4,128,128]{2,1,0:T(8,128)(2,1)S(1)} %get-tuple-element.43), channel_id=1, source_target_pairs={{1,0},{2,1},{3,2},{4,3},{5,4},{6,5},{7,6},{8,7},{9,8},{10,9},{11,1... | collective-permute-start | bytes 393224 | tf_op jit(solution)/shard_map/ppermute | solution.py:23
  6.6 1.6 %fusion.30 = (f32[]{:T(128)}, f32[1,9,7,25]{3,0,2,1:T(1,128)S(1)}) fusion(f32[8,9,7,25]{3,0,2,1:T(8,128)} %param.6, s32[]{:T(128)S(6)} %select_n.51), kind=kLoop, calls=%fused_computation.71 | loop fusion | flops 1574 | bytes 12608 | tf_op jit(solution)/shard_map/reduce_sum | solution.py:187
  8.3 1.5 %fusion.5 = bf16[9,7,128,128]{3,1,2,0:T(8,128)(2,1)S(1)} fusion(f32[1,9,7,25]{3,0,2,1:T(1,128)S(1)} %get-tuple-element.6, f32[]{:T(128)} %get-tuple-element.5), kind=kOutput, calls=%fused_computation.4 | convolution fusion | flops 53873744 | bytes 2070688 | tf_op jit(solution)/shard_map/abt,tpz->abpz/dot_general | solution.py:149
  11.1 0.7 fusion.29
  13.4 3.2 %fusion.32 = (bf16[16,64,896]{2,1,0:T(8,128)(2,1)S(1)}, bf16[16,64,896]{2,1,0:T(8,128)(2,1)S(1)}, bf16[16,64,896]{2,1,0:T(8,128)(2,1)S(1)}, bf16[16,64,896]{2,1,...) fusion(bf16[24,64,896]{2,1,0:T(8,128)(2,1)S(1)} %slice_dynamic-, ...), kind=kLoop, calls=%fused_computation.73 | loop fusion | bytes 33030144 | tf_op jit(solution)/shard_map/slice | solution.py:164
  17.2 0.7 convolution_add_fusion.15
  17.9 0.6 convolution_add_fusion.14
  18.5 0.6 convolution_add_fusion.13
  19.2 0.6 convolution_add_fusion.12
  19.8 0.6 convolution_add_fusion.11
  20.5 0.6 convolution_add_fusion.10
  21.8 0.7 convolution_add_fusion.8
  22.9 1.3 %collective-permute-start.2 = (bf16[16,3,128]{2,1,0:T(4,128)(2,1)S(1)}, bf16[16,3,128]{2,1,0:T(4,128)(2,1)S(1)}, u32[]{:S(2)}, u32[]{:S(2)}) collective-permute-start(bf16[16,3,128]{2,1,0:T(4,128)(2,1)S(1)} %slice_select_fusion), channel_id=1, source_target_pairs={{0,16},{16,0},{32,48},{48,32},{64,80},{80,64},{96,112},{112,96},{1... | collective-permute-start | bytes 36872 | tf_op jit(solution)/shard_map/ppermute | solution.py:37
  24.3 0.9 fusion.8
  25.2 4.0 %collective-permute-start.3 = (bf16[4,70,128]{2,1,0:T(8,128)(2,1)S(1)}, bf16[4,70,128]{2,1,0:T(8,128)(2,1)S(1)}, u32[]{:S(2)}, u32[]{:S(2)}) collective-permute-start(bf16[4,70,128]{2,1,0:T(8,128)(2,1)S(1)} %get-tuple-element.45), channel_id=1, source_target_pairs={{0,1},{1,2},{2,3},{3,4},{4,5},{5,6},{6,7},{7,8},{8,9},{9,10},{10,1... | collective-permute-start | bytes 215048 | tf_op jit(solution)/shard_map/ppermute | solution.py:21
  29.2 1.5 %collective-permute-start.4 = (bf16[4,70,128]{2,1,0:T(8,128)(2,1)S(1)}, bf16[4,70,128]{2,1,0:T(8,128)(2,1)S(1)}, u32[]{:S(2)}, u32[]{:S(2)}) collective-permute-start(bf16[4,70,128]{2,1,0:T(8,128)(2,1)S(1)} %get-tuple-element.46), channel_id=1, source_target_pairs={{1,0},{2,1},{3,2},{4,3},{5,4},{6,5},{7,6},{8,7},{9,8},{10,9},{11,1... | collective-permute-start | bytes 215048 | tf_op jit(solution)/shard_map/ppermute | solution.py:23
  31.3 3.1 %collective-permute-done.4 = bf16[4,70,128]{2,1,0:T(8,128)(2,1)S(1)} collective-permute-done((bf16[4,70,128]{2,1,0:T(8,128)(2,1)S(1)}, bf16[4,70,128]{2,1,0:T(8,128)(2,1)S(1)}, u32[]{:S(2)}, u32[]{:S(2)}) %collective-permute-start.4) | collective-permute-done | bytes 71712 | tf_op jit(solution)/shard_map/ppermute | solution.py:23
  35.6 3.2 %fusion.31 = (bf16[16,64,896]{2,1,0:T(8,128)(2,1)S(1)}, bf16[16,64,896]{2,1,0:T(8,128)(2,1)S(1)}, bf16[16,64,896]{2,1,0:T(8,128)(2,1)S(1)}, bf16[16,64,896]{2,1,...) fusion(bf16[24,64,896]{2,1,0:T(8,128)(2,1)S(1)} %slice_dynamic-, ...), kind=kLoop, calls=%fused_computation.72 | loop fusion | bytes 33030144 | tf_op jit(solution)/shard_map/slice | solution.py:164
  39.4 0.7 convolution_add_fusion.7
  44.7 0.9 broadcast_select_fusion.factor_ref
  45.6 66.2 %shard_map.46 = f32[16,128,128]{2,1,0:T(8,128)} custom-call(f32[16,64,128]{2,1,0:T(8,128)} %broadcast_select_fusion.factor_ref, f32[16,128,128]{2,1,0:T(8,128)} %est_ref.1), custom_call_target="tpu_custom_call" | custom-call | tf_op jit(solution)/shard_map/pallas_call | solution.py:123
  111.8 2.3 %copy.50 = f32[16,128,128]{2,1,0:T(8,128)} copy(f32[16,128,128]{2,1,0:T(8,128)} %shard_map.46) | data formatting | bytes 2097152
  (64 shorter events, 11.4 us)
Async XLA Ops:
  1.3 10.5 %collective-permute-start = (bf16[4,128,128]{2,1,0:T(8,128)(2,1)S(1)}, bf16[4,128,128]{2,1,0:T(8,128)(2,1)S(1)}, u32[]{:S(2)}, u32[]{:S(2)}) collective-permute-start(bf16[4,128,128]{2,1,0:T(8,128)(2,1)S(1)} %get-tuple-element.44), channel_id=1, source_target_pairs={{0,1},{1,2},{2,3},{3,4},{4,5},{5,6},{6,7},{7,8},{8,9},{9,10},{10,1... | collective-permute-start | bytes 393224 | tf_op jit(solution)/shard_map/ppermute | solution.py:21
  5.3 6.6 %collective-permute-start.1 = (bf16[4,128,128]{2,1,0:T(8,128)(2,1)S(1)}, bf16[4,128,128]{2,1,0:T(8,128)(2,1)S(1)}, u32[]{:S(2)}, u32[]{:S(2)}) collective-permute-start(bf16[4,128,128]{2,1,0:T(8,128)(2,1)S(1)} %get-tuple-element.43), channel_id=1, source_target_pairs={{1,0},{2,1},{3,2},{4,3},{5,4},{6,5},{7,6},{8,7},{9,8},{10,9},{11,1... | collective-permute-start | bytes 393224 | tf_op jit(solution)/shard_map/ppermute | solution.py:23
  10.0 0.7 copy-start.1
  21.8 1.0 copy-start
  22.9 2.2 %collective-permute-start.2 = (bf16[16,3,128]{2,1,0:T(4,128)(2,1)S(1)}, bf16[16,3,128]{2,1,0:T(4,128)(2,1)S(1)}, u32[]{:S(2)}, u32[]{:S(2)}) collective-permute-start(bf16[16,3,128]{2,1,0:T(4,128)(2,1)S(1)} %slice_select_fusion), channel_id=1, source_target_pairs={{0,16},{16,0},{32,48},{48,32},{64,80},{80,64},{96,112},{112,96},{1... | collective-permute-start | bytes 36872 | tf_op jit(solution)/shard_map/ppermute | solution.py:37
  25.2 6.0 %collective-permute-start.3 = (bf16[4,70,128]{2,1,0:T(8,128)(2,1)S(1)}, bf16[4,70,128]{2,1,0:T(8,128)(2,1)S(1)}, u32[]{:S(2)}, u32[]{:S(2)}) collective-permute-start(bf16[4,70,128]{2,1,0:T(8,128)(2,1)S(1)} %get-tuple-element.45), channel_id=1, source_target_pairs={{0,1},{1,2},{2,3},{3,4},{4,5},{5,6},{6,7},{7,8},{8,9},{9,10},{10,1... | collective-permute-start | bytes 215048 | tf_op jit(solution)/shard_map/ppermute | solution.py:21
  29.2 5.1 %collective-permute-start.4 = (bf16[4,70,128]{2,1,0:T(8,128)(2,1)S(1)}, bf16[4,70,128]{2,1,0:T(8,128)(2,1)S(1)}, u32[]{:S(2)}, u32[]{:S(2)}) collective-permute-start(bf16[4,70,128]{2,1,0:T(8,128)(2,1)S(1)} %get-tuple-element.46), channel_id=1, source_target_pairs={{1,0},{2,1},{3,2},{4,3},{5,4},{6,5},{7,6},{8,7},{9,8},{10,9},{11,1... | collective-permute-start | bytes 215048 | tf_op jit(solution)/shard_map/ppermute | solution.py:23

commit v4 on v3

--- a/solution.py
+++ b/solution.py
@@ -86,28 +86,53 @@
     cols = pl.ds(part * share_w, share_w)
     out_ref[rows, cols, :] = acc * est_ref[rows, cols, :]
     outgoing = []
-    for d in range(1, n):
-        target = (me + d) % n
+    for d in range(1, groups):
+        target = (view_id + d) % groups
         copy = pltpu.make_async_remote_copy(
             src_ref=out_ref.at[rows, cols],
             dst_ref=out_ref.at[rows, cols],
             send_sem=send2.at[d],
             recv_sem=recv2.at[d],
-            device_id={"view": target},
+            device_id={"view": target * shares + part},
             device_id_type=mesh_kind,
         )
         copy.start()
         outgoing.append(copy)
-    for d in range(1, n):
-        source = (me - d + n) % n
-        src_rows = pl.ds((source // shares) * step, step)
-        src_cols = pl.ds((source % shares) * share_w, share_w)
+    for d in range(1, groups):
+        source = (view_id - d + groups) % groups
+        src_rows = pl.ds(source * step, step)
         pltpu.make_async_remote_copy(
-            src_ref=out_ref.at[src_rows, src_cols],
-            dst_ref=out_ref.at[src_rows, src_cols],
+            src_ref=out_ref.at[src_rows, cols],
+            dst_ref=out_ref.at[src_rows, cols],
             send_sem=send2.at[d],
             recv_sem=recv2.at[d],
-            device_id={"view": source},
+            device_id={"view": source * shares + part},
+            device_id_type=mesh_kind,
+        ).wait_recv()
+    for copy in outgoing:
+        copy.wait_send()
+    outgoing = []
+    for d in range(1, shares):
+        other = (part + d) % shares
+        copy = pltpu.make_async_remote_copy(
+            src_ref=out_ref.at[:, cols],
+            dst_ref=out_ref.at[:, cols],
+            send_sem=send2.at[groups + d],
+            recv_sem=recv2.at[groups + d],
+            device_id={"view": view_id * shares + other},
+            device_id_type=mesh_kind,
+        )
+        copy.start()
+        outgoing.append(copy)
+    for d in range(1, shares):
+        other = (part - d + shares) % shares
+        other_cols = pl.ds(other * share_w, share_w)
+        pltpu.make_async_remote_copy(
+            src_ref=out_ref.at[:, other_cols],
+            dst_ref=out_ref.at[:, other_cols],
+            send_sem=send2.at[groups + d],
+            recv_sem=recv2.at[groups + d],
+            device_id={"view": view_id * shares + other},
             device_id_type=mesh_kind,
         ).wait_recv()
     for copy in outgoing:
@@ -129,8 +154,8 @@
             pltpu.VMEM((groups, step, share_w, depth), jnp.float32),
             pltpu.SemaphoreType.DMA((groups,)),
             pltpu.SemaphoreType.DMA((groups,)),
-            pltpu.SemaphoreType.DMA((n,)),
-            pltpu.SemaphoreType.DMA((n,)),
+            pltpu.SemaphoreType.DMA((groups + shares,)),
+            pltpu.SemaphoreType.DMA((groups + shares,)),
         ],
         compiler_params=pltpu.CompilerParams(has_side_effects=True),
     )(share_factor, estimate)

time: 114 us -> 101 us (0.89)
  Pallas kernels: 66.2 us -> 52.7 us
    pallas_call x1, Pallas kernels: 66.2 us -> 52.7 us  [product_gather(): pl.pallas_call(functools.partial(product_kernel, n, shares), out_shape=ja...]
  transfers between devices with their start and end apart: 5 -> 5, of which waited for: 1 -> 1; matrix products, arithmetic and copies ran while one was open for 5% -> 6% of each run, Pallas kernels for 0% -> 0%
where the time goes in v4:
time: 101 us
  Pallas kernels  52.7 us (52%)
  matrix products  14 us (14%)
  local copies, waits for them, and re-layouts  12.9 us (13%)
  starting transfers between devices  12 us (12%)
  other arithmetic  5.26 us (5%)
  waiting for transfers between devices  3.07 us (3%)
    pallas_call x1, Pallas kernels, product_gather(): pl.pallas_call(functools.partial(product_kernel, n, shares), out_shape=ja...  52.7 us
    dot_general x18, matrix products, convolve(): jnp.dot(columns[shift_x:shift_x + rows_x].reshape(rows_x * rows_y, -1), b...  11.6 us
    ppermute x2, starting transfers between devices, with_halo(): lax.ppermute(tail, axis, [(i, (i + 1) % count) for i in range(ends)])  7.94 us
    slice x2, local copies, waits for them, and re-layouts, convolve(): columns[shift_x:shift_x + rows_x].reshape(rows_x * rows_y, -1)  6.38 us
    unnamed x17, local copies, waits for them, and re-layouts  4.83 us
    ppermute x2, waiting for transfers between devices, with_halo(): lax.ppermute(head, axis, [((i + 1) % count, i) for i in range(ends)])  3.06 us
    ppermute x2, starting transfers between devices, with_halo(): lax.ppermute(head, axis, [((i + 1) % count, i) for i in range(ends)])  2.76 us
    dot_general x2, matrix products, band_table(): jnp.einsum('abt,tpz->abpz', kernel, onehot, preferred_element_type=jnp.fl...  2.37 us
  transfers between devices with their start and end apart: 5, of which 1 were waited for; matrix products, arithmetic and copies ran while one was open for 6% of the time, Pallas kernels for 0%

profile of v4, /device:TPU:1, one launch (start us, length us, event | category | flops | bytes accessed | tf_op | source)
XLA Modules:
  0.0 100.5 jit_solution(4966054667372039335)
XLA Ops:
  0.0 1.3 %convert_element_type.30 = bf16[16,128,128]{2,1,0:T(8,128)(2,1)S(1)} convert(f32[16,128,128]{2,1,0:T(8,128)} %est_ref.1) | non-fusion elementwise | flops 262144 | bytes 1572864 | tf_op jit(solution)/shard_map/convert_element_type | solution.py:208
  1.3 4.0 %collective-permute-start = (bf16[4,128,128]{2,1,0:T(8,128)(2,1)S(1)}, bf16[4,128,128]{2,1,0:T(8,128)(2,1)S(1)}, u32[]{:S(2)}, u32[]{:S(2)}) collective-permute-start(bf16[4,128,128]{2,1,0:T(8,128)(2,1)S(1)} %get-tuple-element.44), channel_id=1, source_target_pairs={{0,1},{1,2},{2,3},{3,4},{4,5},{5,6},{6,7},{7,8},{8,9},{9,10},{10,1... | collective-permute-start | bytes 393224 | tf_op jit(solution)/shard_map/ppermute | solution.py:21
  5.3 1.3 %collective-permute-start.1 = (bf16[4,128,128]{2,1,0:T(8,128)(2,1)S(1)}, bf16[4,128,128]{2,1,0:T(8,128)(2,1)S(1)}, u32[]{:S(2)}, u32[]{:S(2)}) collective-permute-start(bf16[4,128,128]{2,1,0:T(8,128)(2,1)S(1)} %get-tuple-element.43), channel_id=1, source_target_pairs={{1,0},{2,1},{3,2},{4,3},{5,4},{6,5},{7,6},{8,7},{9,8},{10,9},{11,1... | collective-permute-start | bytes 393224 | tf_op jit(solution)/shard_map/ppermute | solution.py:23
  6.6 1.6 %fusion.30 = (f32[]{:T(128)}, f32[1,9,7,25]{3,0,2,1:T(1,128)S(1)}) fusion(f32[8,9,7,25]{3,0,2,1:T(8,128)} %param.6, s32[]{:T(128)S(6)} %select_n.51), kind=kLoop, calls=%fused_computation.71 | loop fusion | flops 1574 | bytes 12608 | tf_op jit(solution)/shard_map/reduce_sum | solution.py:212
  8.3 1.5 %fusion.5 = bf16[9,7,128,128]{3,1,2,0:T(8,128)(2,1)S(1)} fusion(f32[1,9,7,25]{3,0,2,1:T(1,128)S(1)} %get-tuple-element.6, f32[]{:T(128)} %get-tuple-element.5), kind=kOutput, calls=%fused_computation.4 | convolution fusion | flops 53873744 | bytes 2070688 | tf_op jit(solution)/shard_map/abt,tpz->abpz/dot_general | solution.py:174
  11.1 0.7 fusion.29
  13.4 3.2 %fusion.32 = (bf16[16,64,896]{2,1,0:T(8,128)(2,1)S(1)}, bf16[16,64,896]{2,1,0:T(8,128)(2,1)S(1)}, bf16[16,64,896]{2,1,0:T(8,128)(2,1)S(1)}, bf16[16,64,896]{2,1,...) fusion(bf16[24,64,896]{2,1,0:T(8,128)(2,1)S(1)} %slice_dynamic-, ...), kind=kLoop, calls=%fused_computation.73 | loop fusion | bytes 33030144 | tf_op jit(solution)/shard_map/slice | solution.py:189
  17.2 0.7 convolution_add_fusion.15
  17.9 0.6 convolution_add_fusion.14
  18.5 0.6 convolution_add_fusion.13
  19.2 0.6 convolution_add_fusion.12
  19.8 0.6 convolution_add_fusion.11
  20.5 0.6 convolution_add_fusion.10
  21.8 0.7 convolution_add_fusion.8
  22.9 1.3 %collective-permute-start.2 = (bf16[16,3,128]{2,1,0:T(4,128)(2,1)S(1)}, bf16[16,3,128]{2,1,0:T(4,128)(2,1)S(1)}, u32[]{:S(2)}, u32[]{:S(2)}) collective-permute-start(bf16[16,3,128]{2,1,0:T(4,128)(2,1)S(1)} %slice_select_fusion), channel_id=1, source_target_pairs={{0,16},{16,0},{32,48},{48,32},{64,80},{80,64},{96,112},{112,96},{1... | collective-permute-start | bytes 36872 | tf_op jit(solution)/shard_map/ppermute | solution.py:37
  24.3 0.9 fusion.8
  25.2 4.0 %collective-permute-start.3 = (bf16[4,70,128]{2,1,0:T(8,128)(2,1)S(1)}, bf16[4,70,128]{2,1,0:T(8,128)(2,1)S(1)}, u32[]{:S(2)}, u32[]{:S(2)}) collective-permute-start(bf16[4,70,128]{2,1,0:T(8,128)(2,1)S(1)} %get-tuple-element.45), channel_id=1, source_target_pairs={{0,1},{1,2},{2,3},{3,4},{4,5},{5,6},{6,7},{7,8},{8,9},{9,10},{10,1... | collective-permute-start | bytes 215048 | tf_op jit(solution)/shard_map/ppermute | solution.py:21
  29.2 1.5 %collective-permute-start.4 = (bf16[4,70,128]{2,1,0:T(8,128)(2,1)S(1)}, bf16[4,70,128]{2,1,0:T(8,128)(2,1)S(1)}, u32[]{:S(2)}, u32[]{:S(2)}) collective-permute-start(bf16[4,70,128]{2,1,0:T(8,128)(2,1)S(1)} %get-tuple-element.46), channel_id=1, source_target_pairs={{1,0},{2,1},{3,2},{4,3},{5,4},{6,5},{7,6},{8,7},{9,8},{10,9},{11,1... | collective-permute-start | bytes 215048 | tf_op jit(solution)/shard_map/ppermute | solution.py:23
  31.3 3.1 %collective-permute-done.4 = bf16[4,70,128]{2,1,0:T(8,128)(2,1)S(1)} collective-permute-done((bf16[4,70,128]{2,1,0:T(8,128)(2,1)S(1)}, bf16[4,70,128]{2,1,0:T(8,128)(2,1)S(1)}, u32[]{:S(2)}, u32[]{:S(2)}) %collective-permute-start.4) | collective-permute-done | bytes 71712 | tf_op jit(solution)/shard_map/ppermute | solution.py:23
  35.6 3.2 %fusion.31 = (bf16[16,64,896]{2,1,0:T(8,128)(2,1)S(1)}, bf16[16,64,896]{2,1,0:T(8,128)(2,1)S(1)}, bf16[16,64,896]{2,1,0:T(8,128)(2,1)S(1)}, bf16[16,64,896]{2,1,...) fusion(bf16[24,64,896]{2,1,0:T(8,128)(2,1)S(1)} %slice_dynamic-, ...), kind=kLoop, calls=%fused_computation.72 | loop fusion | bytes 33030144 | tf_op jit(solution)/shard_map/slice | solution.py:189
  39.4 0.7 convolution_add_fusion.7
  44.7 0.9 broadcast_select_fusion.factor_ref
  45.6 52.7 %shard_map.46 = f32[16,128,128]{2,1,0:T(8,128)} custom-call(f32[16,64,128]{2,1,0:T(8,128)} %broadcast_select_fusion.factor_ref, f32[16,128,128]{2,1,0:T(8,128)} %est_ref.1), custom_call_target="tpu_custom_call" | custom-call | tf_op jit(solution)/shard_map/pallas_call | solution.py:148
  98.3 2.3 %copy.50 = f32[16,128,128]{2,1,0:T(8,128)} copy(f32[16,128,128]{2,1,0:T(8,128)} %shard_map.46) | data formatting | bytes 2097152
  (64 shorter events, 11.4 us)
Async XLA Ops:
  1.3 10.5 %collective-permute-start = (bf16[4,128,128]{2,1,0:T(8,128)(2,1)S(1)}, bf16[4,128,128]{2,1,0:T(8,128)(2,1)S(1)}, u32[]{:S(2)}, u32[]{:S(2)}) collective-permute-start(bf16[4,128,128]{2,1,0:T(8,128)(2,1)S(1)} %get-tuple-element.44), channel_id=1, source_target_pairs={{0,1},{1,2},{2,3},{3,4},{4,5},{5,6},{6,7},{7,8},{8,9},{9,10},{10,1... | collective-permute-start | bytes 393224 | tf_op jit(solution)/shard_map/ppermute | solution.py:21
  5.3 6.6 %collective-permute-start.1 = (bf16[4,128,128]{2,1,0:T(8,128)(2,1)S(1)}, bf16[4,128,128]{2,1,0:T(8,128)(2,1)S(1)}, u32[]{:S(2)}, u32[]{:S(2)}) collective-permute-start(bf16[4,128,128]{2,1,0:T(8,128)(2,1)S(1)} %get-tuple-element.43), channel_id=1, source_target_pairs={{1,0},{2,1},{3,2},{4,3},{5,4},{6,5},{7,6},{8,7},{9,8},{10,9},{11,1... | collective-permute-start | bytes 393224 | tf_op jit(solution)/shard_map/ppermute | solution.py:23
  10.0 0.7 copy-start.1
  21.8 1.0 copy-start
  22.9 2.2 %collective-permute-start.2 = (bf16[16,3,128]{2,1,0:T(4,128)(2,1)S(1)}, bf16[16,3,128]{2,1,0:T(4,128)(2,1)S(1)}, u32[]{:S(2)}, u32[]{:S(2)}) collective-permute-start(bf16[16,3,128]{2,1,0:T(4,128)(2,1)S(1)} %slice_select_fusion), channel_id=1, source_target_pairs={{0,16},{16,0},{32,48},{48,32},{64,80},{80,64},{96,112},{112,96},{1... | collective-permute-start | bytes 36872 | tf_op jit(solution)/shard_map/ppermute | solution.py:37
  25.2 6.0 %collective-permute-start.3 = (bf16[4,70,128]{2,1,0:T(8,128)(2,1)S(1)}, bf16[4,70,128]{2,1,0:T(8,128)(2,1)S(1)}, u32[]{:S(2)}, u32[]{:S(2)}) collective-permute-start(bf16[4,70,128]{2,1,0:T(8,128)(2,1)S(1)} %get-tuple-element.45), channel_id=1, source_target_pairs={{0,1},{1,2},{2,3},{3,4},{4,5},{5,6},{6,7},{7,8},{8,9},{9,10},{10,1... | collective-permute-start | bytes 215048 | tf_op jit(solution)/shard_map/ppermute | solution.py:21
  29.2 5.1 %collective-permute-start.4 = (bf16[4,70,128]{2,1,0:T(8,128)(2,1)S(1)}, bf16[4,70,128]{2,1,0:T(8,128)(2,1)S(1)}, u32[]{:S(2)}, u32[]{:S(2)}) collective-permute-start(bf16[4,70,128]{2,1,0:T(8,128)(2,1)S(1)} %get-tuple-element.46), channel_id=1, source_target_pairs={{1,0},{2,1},{3,2},{4,3},{5,4},{6,5},{7,6},{8,7},{9,8},{10,9},{11,1... | collective-permute-start | bytes 215048 | tf_op jit(solution)/shard_map/ppermute | solution.py:23

commit v5 on v4

--- a/solution.py
+++ b/solution.py
@@ -55,6 +55,18 @@
     view_id = me // shares
     part = me % shares
     mesh_kind = pl.DeviceIdType.MESH
+    barrier = pltpu.get_barrier_semaphore()
+    for d in range(1, groups):
+        pl.semaphore_signal(
+            barrier, inc=1, device_id={"view": ((view_id + d) % groups) * shares + part},
+            device_id_type=mesh_kind,
+        )
+    for d in range(1, shares):
+        pl.semaphore_signal(
+            barrier, inc=1, device_id={"view": view_id * shares + (part + d) % shares},
+            device_id_type=mesh_kind,
+        )
+    pl.semaphore_wait(barrier, groups + shares - 2)
     outgoing = []
     for d in range(1, groups):
         target = (view_id + d) % groups
@@ -157,7 +169,7 @@
             pltpu.SemaphoreType.DMA((groups + shares,)),
             pltpu.SemaphoreType.DMA((groups + shares,)),
         ],
-        compiler_params=pltpu.CompilerParams(has_side_effects=True),
+        compiler_params=pltpu.CompilerParams(collective_id=0, has_side_effects=True),
     )(share_factor, estimate)
 
 

time: 101 us -> 89.2 us (0.88)
  the two profiles are of different devices: /device:TPU:1 before, /device:TPU:71 now
where the time goes in v5:
time: 89.2 us; the launch traced here: 88.2 us
  Pallas kernels  36.9 us (41%)
  matrix products  14 us (16%)
  starting transfers between devices  13.6 us (15%)
  local copies, waits for them, and re-layouts  12.9 us (14%)
  other arithmetic  5.26 us (6%)
  waiting for transfers between devices  4.93 us (6%)
    pallas_call x1, Pallas kernels, product_gather(): pl.pallas_call(functools.partial(product_kernel, n, shares), out_shape=ja...  36.9 us
    dot_general x18, matrix products, convolve(): jnp.dot(columns[shift_x:shift_x + rows_x].reshape(rows_x * rows_y, -1), b...  11.6 us
    ppermute x2, starting transfers between devices, with_halo(): lax.ppermute(tail, axis, [(i, (i + 1) % count) for i in range(ends)])  7.11 us
    slice x2, local copies, waits for them, and re-layouts, convolve(): columns[shift_x:shift_x + rows_x].reshape(rows_x * rows_y, -1)  6.38 us
    ppermute x2, waiting for transfers between devices, with_halo(): lax.ppermute(head, axis, [((i + 1) % count, i) for i in range(ends)])  4.93 us
    unnamed x17, local copies, waits for them, and re-layouts  4.83 us
    ppermute x2, starting transfers between devices, with_halo(): lax.ppermute(head, axis, [((i + 1) % count, i) for i in range(ends)])  4.26 us
    dot_general x2, matrix products, band_table(): jnp.einsum('abt,tpz->abpz', kernel, onehot, preferred_element_type=jnp.fl...  2.37 us
  transfers between devices with their start and end apart: 5, of which 2 were waited for; matrix products, arithmetic and copies ran while one was open for 7% of the time, Pallas kernels for 0%

profile of v5, /device:TPU:71, one launch (start us, length us, event | category | flops | bytes accessed | tf_op | source)
XLA Modules:
  0.0 88.2 jit_solution(4772200252378183151)
XLA Ops:
  0.0 1.3 %convert_element_type.30 = bf16[16,128,128]{2,1,0:T(8,128)(2,1)S(1)} convert(f32[16,128,128]{2,1,0:T(8,128)} %est_ref.1) | non-fusion elementwise | flops 262144 | bytes 1572864 | tf_op jit(solution)/shard_map/convert_element_type | solution.py:220
  1.3 3.1 %collective-permute-start = (bf16[4,128,128]{2,1,0:T(8,128)(2,1)S(1)}, bf16[4,128,128]{2,1,0:T(8,128)(2,1)S(1)}, u32[]{:S(2)}, u32[]{:S(2)}) collective-permute-start(bf16[4,128,128]{2,1,0:T(8,128)(2,1)S(1)} %get-tuple-element.44), channel_id=1, source_target_pairs={{0,1},{1,2},{2,3},{3,4},{4,5},{5,6},{6,7},{7,8},{8,9},{9,10},{10,1... | collective-permute-start | bytes 393224 | tf_op jit(solution)/shard_map/ppermute | solution.py:21
  4.5 2.2 %collective-permute-start.1 = (bf16[4,128,128]{2,1,0:T(8,128)(2,1)S(1)}, bf16[4,128,128]{2,1,0:T(8,128)(2,1)S(1)}, u32[]{:S(2)}, u32[]{:S(2)}) collective-permute-start(bf16[4,128,128]{2,1,0:T(8,128)(2,1)S(1)} %get-tuple-element.43), channel_id=1, source_target_pairs={{1,0},{2,1},{3,2},{4,3},{5,4},{6,5},{7,6},{8,7},{9,8},{10,9},{11,1... | collective-permute-start | bytes 393224 | tf_op jit(solution)/shard_map/ppermute | solution.py:23
  6.7 1.6 %fusion.30 = (f32[]{:T(128)}, f32[1,9,7,25]{3,0,2,1:T(1,128)S(1)}) fusion(f32[8,9,7,25]{3,0,2,1:T(8,128)} %param.6, s32[]{:T(128)S(6)} %select_n.51), kind=kLoop, calls=%fused_computation.71 | loop fusion | flops 1574 | bytes 12608 | tf_op jit(solution)/shard_map/reduce_sum | solution.py:224
  8.3 1.5 %fusion.5 = bf16[9,7,128,128]{3,1,2,0:T(8,128)(2,1)S(1)} fusion(f32[1,9,7,25]{3,0,2,1:T(1,128)S(1)} %get-tuple-element.6, f32[]{:T(128)} %get-tuple-element.5), kind=kOutput, calls=%fused_computation.4 | convolution fusion | flops 53873744 | bytes 2070688 | tf_op jit(solution)/shard_map/abt,tpz->abpz/dot_general | solution.py:186
  11.1 0.7 fusion.29
  13.8 3.2 %fusion.32 = (bf16[16,64,896]{2,1,0:T(8,128)(2,1)S(1)}, bf16[16,64,896]{2,1,0:T(8,128)(2,1)S(1)}, bf16[16,64,896]{2,1,0:T(8,128)(2,1)S(1)}, bf16[16,64,896]{2,1,...) fusion(bf16[24,64,896]{2,1,0:T(8,128)(2,1)S(1)} %slice_dynamic-, ...), kind=kLoop, calls=%fused_computation.73 | loop fusion | bytes 33030144 | tf_op jit(solution)/shard_map/slice | solution.py:201
  17.6 0.7 convolution_add_fusion.15
  18.9 0.6 convolution_add_fusion.13
  19.6 0.6 convolution_add_fusion.12
  20.3 0.6 convolution_add_fusion.11
  20.9 0.6 convolution_add_fusion.10
  21.6 0.6 convolution_add_fusion.9
  22.2 0.7 convolution_add_fusion.8
  23.3 2.2 %collective-permute-start.2 = (bf16[16,3,128]{2,1,0:T(4,128)(2,1)S(1)}, bf16[16,3,128]{2,1,0:T(4,128)(2,1)S(1)}, u32[]{:S(2)}, u32[]{:S(2)}) collective-permute-start(bf16[16,3,128]{2,1,0:T(4,128)(2,1)S(1)} %slice_select_fusion), channel_id=1, source_target_pairs={{0,16},{16,0},{32,48},{48,32},{64,80},{80,64},{96,112},{112,96},{1... | collective-permute-start | bytes 36872 | tf_op jit(solution)/shard_map/ppermute | solution.py:37
  25.5 0.9 fusion.8
  26.5 4.0 %collective-permute-start.3 = (bf16[4,70,128]{2,1,0:T(8,128)(2,1)S(1)}, bf16[4,70,128]{2,1,0:T(8,128)(2,1)S(1)}, u32[]{:S(2)}, u32[]{:S(2)}) collective-permute-start(bf16[4,70,128]{2,1,0:T(8,128)(2,1)S(1)} %get-tuple-element.45), channel_id=1, source_target_pairs={{0,1},{1,2},{2,3},{3,4},{4,5},{5,6},{6,7},{7,8},{8,9},{9,10},{10,1... | collective-permute-start | bytes 215048 | tf_op jit(solution)/shard_map/ppermute | solution.py:21
  30.5 2.1 %collective-permute-start.4 = (bf16[4,70,128]{2,1,0:T(8,128)(2,1)S(1)}, bf16[4,70,128]{2,1,0:T(8,128)(2,1)S(1)}, u32[]{:S(2)}, u32[]{:S(2)}) collective-permute-start(bf16[4,70,128]{2,1,0:T(8,128)(2,1)S(1)} %get-tuple-element.46), channel_id=1, source_target_pairs={{1,0},{2,1},{3,2},{4,3},{5,4},{6,5},{7,6},{8,7},{9,8},{10,9},{11,1... | collective-permute-start | bytes 215048 | tf_op jit(solution)/shard_map/ppermute | solution.py:23
  33.2 4.5 %collective-permute-done.4 = bf16[4,70,128]{2,1,0:T(8,128)(2,1)S(1)} collective-permute-done((bf16[4,70,128]{2,1,0:T(8,128)(2,1)S(1)}, bf16[4,70,128]{2,1,0:T(8,128)(2,1)S(1)}, u32[]{:S(2)}, u32[]{:S(2)}) %collective-permute-start.4) | collective-permute-done | bytes 71712 | tf_op jit(solution)/shard_map/ppermute | solution.py:23
  39.0 3.2 %fusion.31 = (bf16[16,64,896]{2,1,0:T(8,128)(2,1)S(1)}, bf16[16,64,896]{2,1,0:T(8,128)(2,1)S(1)}, bf16[16,64,896]{2,1,0:T(8,128)(2,1)S(1)}, bf16[16,64,896]{2,1,...) fusion(bf16[24,64,896]{2,1,0:T(8,128)(2,1)S(1)} %slice_dynamic-, ...), kind=kLoop, calls=%fused_computation.72 | loop fusion | bytes 33030144 | tf_op jit(solution)/shard_map/slice | solution.py:201
  42.8 0.7 convolution_add_fusion.7
  48.0 0.9 %broadcast_select_fusion.factor_ref = f32[16,64,128]{2,1,0:T(8,128)} fusion(f32[16,64,128]{2,1,0:T(8,128)S(1)} %bitcast.115, pred[64]{0:T(512)(128)(4,1)S(1)} %broadcast_in_dim.27), kind=kLoop, calls=%fused_computation.54 | loop fusion | flops 131072 | bytes 1048640 | tf_op jit(solution)/shard_map/jit(_where)/select_n | solution.py:244
  49.0 36.9 %shard_map.46 = f32[16,128,128]{2,1,0:T(8,128)} custom-call(f32[16,64,128]{2,1,0:T(8,128)} %broadcast_select_fusion.factor_ref, f32[16,128,128]{2,1,0:T(8,128)} %est_ref.1), custom_call_target="tpu_custom_call" | custom-call | tf_op jit(solution)/shard_map/pallas_call | solution.py:160
  85.9 2.3 %copy.50 = f32[16,128,128]{2,1,0:T(8,128)} copy(f32[16,128,128]{2,1,0:T(8,128)} %shard_map.46) | data formatting | bytes 2097152
  (64 shorter events, 11.8 us)
Async XLA Ops:
  1.3 10.6 %collective-permute-start = (bf16[4,128,128]{2,1,0:T(8,128)(2,1)S(1)}, bf16[4,128,128]{2,1,0:T(8,128)(2,1)S(1)}, u32[]{:S(2)}, u32[]{:S(2)}) collective-permute-start(bf16[4,128,128]{2,1,0:T(8,128)(2,1)S(1)} %get-tuple-element.44), channel_id=1, source_target_pairs={{0,1},{1,2},{2,3},{3,4},{4,5},{5,6},{6,7},{7,8},{8,9},{9,10},{10,1... | collective-permute-start | bytes 393224 | tf_op jit(solution)/shard_map/ppermute | solution.py:21
  4.5 7.8 %collective-permute-start.1 = (bf16[4,128,128]{2,1,0:T(8,128)(2,1)S(1)}, bf16[4,128,128]{2,1,0:T(8,128)(2,1)S(1)}, u32[]{:S(2)}, u32[]{:S(2)}) collective-permute-start(bf16[4,128,128]{2,1,0:T(8,128)(2,1)S(1)} %get-tuple-element.43), channel_id=1, source_target_pairs={{1,0},{2,1},{3,2},{4,3},{5,4},{6,5},{7,6},{8,7},{9,8},{10,9},{11,1... | collective-permute-start | bytes 393224 | tf_op jit(solution)/shard_map/ppermute | solution.py:23
  10.1 0.7 copy-start.1
  22.2 1.0 %copy-start = (bf16[1,16,64,128]{3,2,1,0:T(8,128)(2,1)S(1)}, bf16[1,16,64,128]{3,2,1,0:T(8,128)(2,1)}, u32[]{:S(2)}) copy-start(bf16[1,16,64,128]{3,2,1,0:T(8,128)(2,1)} %param.5) | copy-start | bytes 786436
  23.3 3.1 %collective-permute-start.2 = (bf16[16,3,128]{2,1,0:T(4,128)(2,1)S(1)}, bf16[16,3,128]{2,1,0:T(4,128)(2,1)S(1)}, u32[]{:S(2)}, u32[]{:S(2)}) collective-permute-start(bf16[16,3,128]{2,1,0:T(4,128)(2,1)S(1)} %slice_select_fusion), channel_id=1, source_target_pairs={{0,16},{16,0},{32,48},{48,32},{64,80},{80,64},{96,112},{112,96},{1... | collective-permute-start | bytes 36872 | tf_op jit(solution)/shard_map/ppermute | solution.py:37
  26.5 6.7 %collective-permute-start.3 = (bf16[4,70,128]{2,1,0:T(8,128)(2,1)S(1)}, bf16[4,70,128]{2,1,0:T(8,128)(2,1)S(1)}, u32[]{:S(2)}, u32[]{:S(2)}) collective-permute-start(bf16[4,70,128]{2,1,0:T(8,128)(2,1)S(1)} %get-tuple-element.45), channel_id=1, source_target_pairs={{0,1},{1,2},{2,3},{3,4},{4,5},{5,6},{6,7},{7,8},{8,9},{9,10},{10,1... | collective-permute-start | bytes 215048 | tf_op jit(solution)/shard_map/ppermute | solution.py:21
  30.5 7.2 %collective-permute-start.4 = (bf16[4,70,128]{2,1,0:T(8,128)(2,1)S(1)}, bf16[4,70,128]{2,1,0:T(8,128)(2,1)S(1)}, u32[]{:S(2)}, u32[]{:S(2)}) collective-permute-start(bf16[4,70,128]{2,1,0:T(8,128)(2,1)S(1)} %get-tuple-element.46), channel_id=1, source_target_pairs={{1,0},{2,1},{3,2},{4,3},{5,4},{6,5},{7,6},{8,7},{9,8},{10,9},{11,1... | collective-permute-start | bytes 215048 | tf_op jit(solution)/shard_map/ppermute | solution.py:23

commit v6 on v5

--- a/solution.py
+++ b/solution.py
@@ -189,21 +189,31 @@
     return banded.reshape(taps_x, taps_y * depth, depth)
 
 
+def conv_kernel(tile_x, src_ref, band_ref, out_ref, cols_ref):
+    rows_x, rows_y, depth = out_ref.shape
+    taps_x = src_ref.shape[0] - rows_x + 1
+    taps_y = src_ref.shape[1] - rows_y + 1
+    for step_y in range(taps_y):
+        cols_ref[:, :, step_y * depth : (step_y + 1) * depth] = src_ref[:, step_y : step_y + rows_y, :]
+    for start in range(0, rows_x, tile_x):
+        acc = None
+        for shift_x in range(taps_x):
+            lhs = cols_ref[start + shift_x : start + shift_x + tile_x].reshape(tile_x * rows_y, -1)
+            part = jnp.dot(lhs, band_ref[shift_x], preferred_element_type=jnp.float32)
+            acc = part if acc is None else acc + part
+        out_ref[start : start + tile_x] = acc.reshape(tile_x, rows_y, depth)
+
+
 def convolve(padded_part, banded, rows_x, rows_y):
-    taps_x = padded_part.shape[0] - rows_x + 1
-    taps_y = padded_part.shape[1] - rows_y + 1
-    columns = jnp.concatenate(
-        [padded_part[:, step_y : step_y + rows_y, :] for step_y in range(taps_y)], axis=2
-    )
-    output = None
-    for shift_x in range(taps_x):
-        partial_sum = jnp.dot(
-            columns[shift_x : shift_x + rows_x].reshape(rows_x * rows_y, -1),
-            banded[shift_x],
-            preferred_element_type=jnp.float32,
-        )
-        output = partial_sum if output is None else output + partial_sum
-    return output.reshape(rows_x, rows_y, -1)
+    depth = padded_part.shape[2]
+    vmem = pl.BlockSpec(memory_space=pltpu.VMEM)
+    return pl.pallas_call(
+        functools.partial(conv_kernel, 4),
+        out_shape=jax.ShapeDtypeStruct((rows_x, rows_y, depth), jnp.float32),
+        in_specs=[vmem, vmem],
+        out_specs=vmem,
+        scratch_shapes=[pltpu.VMEM((padded_part.shape[0], rows_y, banded.shape[1]), jnp.bfloat16)],
+    )(padded_part, banded)
 
 
 def local(estimate, images, point_spread, covered):

time: 89.2 us -> 86.5 us (0.970)
  Pallas kernels: 36.9 us -> 51.1 us
  matrix products: 14 us -> 2.41 us
  local copies, waits for them, and re-layouts: 12.9 us -> 6.57 us
  other arithmetic: 5.26 us -> 8.99 us
  waiting for transfers between devices: 4.93 us -> 2.37 us
    pallas_call x0 -> x2, Pallas kernels: none -> 14.1 us  [convolve(): pl.pallas_call(functools.partial(conv_kernel, 4), out_shape=jax.ShapeDtyp...]
    dot_general x18 -> x0, matrix products: 11.6 us -> none  [convolve(): jnp.dot(columns[shift_x:shift_x + rows_x].reshape(rows_x * rows_y, -1), b...]
    slice x22 -> x0, local copies, waits for them, and re-layouts: 7.32 us -> none  [the longest x2 6.38 us: convolve(): columns[shift_x:shift_x + rows_x].reshape(rows_x * rows_y, -1)]
    convert_element_type x0 -> x2, local copies, waits for them, and re-layouts: none -> 3.85 us  [band_table(): jnp.einsum('abt,tpz->abpz', kernel, onehot, preferred_element_type=jnp.fl...]
    ppermute x2, waiting for transfers between devices: 4.93 us -> 2.35 us  [with_halo(): lax.ppermute(head, axis, [((i + 1) % count, i) for i in range(ends)])]
    unnamed x17 -> x5, local copies, waits for them, and re-layouts: 4.83 us -> 2.31 us
    concatenate x2, other arithmetic: 0.44 us -> 1.96 us  [with_halo(): jnp.concatenate([lax.ppermute(tail, axis, [(i, (i + 1) % count) for i in...]
    convert_element_type x1, other arithmetic: 0.14 us -> 1.21 us  [local(): jnp.where(cell_cover, image.astype(jnp.float32) / blurred, 0.0)]
  transfers between devices with their start and end apart: 5 -> 5, of which waited for: 2 -> 1; matrix products, arithmetic and copies ran while one was open for 7% -> 11% of each run, Pallas kernels for 0% -> 0%
where the time goes in v6:
time: 86.5 us; the launch traced here: 85.5 us
  Pallas kernels  51.1 us (59%)
  starting transfers between devices  13.9 us (16%)
  other arithmetic  8.99 us (10%)
  local copies, waits for them, and re-layouts  6.57 us (8%)
  matrix products  2.41 us (3%)
  waiting for transfers between devices  2.37 us (3%)
    pallas_call x1, Pallas kernels, product_gather(): pl.pallas_call(functools.partial(product_kernel, n, shares), out_shape=ja...  36.9 us
    pallas_call x2, Pallas kernels, convolve(): pl.pallas_call(functools.partial(conv_kernel, 4), out_shape=jax.ShapeDtyp...  14.1 us
    ppermute x2, starting transfers between devices, with_halo(): lax.ppermute(tail, axis, [(i, (i + 1) % count) for i in range(ends)])  7.44 us
    ppermute x2, starting transfers between devices, with_halo(): lax.ppermute(head, axis, [((i + 1) % count, i) for i in range(ends)])  4.26 us
    convert_element_type x2, local copies, waits for them, and re-layouts, band_table(): jnp.einsum('abt,tpz->abpz', kernel, onehot, preferred_element_type=jnp.fl...  3.85 us
    dot_general x2, matrix products, band_table(): jnp.einsum('abt,tpz->abpz', kernel, onehot, preferred_element_type=jnp.fl...  2.41 us
    ppermute x2, waiting for transfers between devices, with_halo(): lax.ppermute(head, axis, [((i + 1) % count, i) for i in range(ends)])  2.35 us
    unnamed x5, local copies, waits for them, and re-layouts  2.31 us
  transfers between devices with their start and end apart: 5, of which 1 were waited for; matrix products, arithmetic and copies ran while one was open for 11% of the time, Pallas kernels for 0%

profile of v6, /device:TPU:71, one launch (start us, length us, event | category | flops | bytes accessed | tf_op | source)
XLA Modules:
  0.0 85.5 jit_solution(3485566686254037510)
XLA Ops:
  0.0 1.3 %convert_element_type.30 = bf16[16,128,128]{2,1,0:T(8,128)(2,1)S(1)} convert(f32[16,128,128]{2,1,0:T(8,128)} %est_ref.1) | non-fusion elementwise | flops 262144 | bytes 1572864 | tf_op jit(solution)/shard_map/convert_element_type | solution.py:230
  1.3 3.1 %collective-permute-start = (bf16[4,128,128]{2,1,0:T(8,128)(2,1)S(1)}, bf16[4,128,128]{2,1,0:T(8,128)(2,1)S(1)}, u32[]{:S(2)}, u32[]{:S(2)}) collective-permute-start(bf16[4,128,128]{2,1,0:T(8,128)(2,1)S(1)} %get-tuple-element.8), channel_id=1, source_target_pairs={{0,1},{1,2},{2,3},{3,4},{4,5},{5,6},{6,7},{7,8},{8,9},{9,10},{10,1... | collective-permute-start | bytes 393224 | tf_op jit(solution)/shard_map/ppermute | solution.py:21
  4.5 2.2 %collective-permute-start.1 = (bf16[4,128,128]{2,1,0:T(8,128)(2,1)S(1)}, bf16[4,128,128]{2,1,0:T(8,128)(2,1)S(1)}, u32[]{:S(2)}, u32[]{:S(2)}) collective-permute-start(bf16[4,128,128]{2,1,0:T(8,128)(2,1)S(1)} %get-tuple-element.7), channel_id=1, source_target_pairs={{1,0},{2,1},{3,2},{4,3},{5,4},{6,5},{7,6},{8,7},{9,8},{10,9},{11,1... | collective-permute-start | bytes 393224 | tf_op jit(solution)/shard_map/ppermute | solution.py:23
  6.7 1.7 %fusion.30 = (f32[]{:T(128)}, f32[1,9,7,25]{3,0,2,1:T(1,128)S(1)}) fusion(f32[8,9,7,25]{3,0,2,1:T(8,128)} %param.6, s32[]{:T(128)S(6)} %select_n.51), kind=kLoop, calls=%fused_computation.41 | loop fusion | flops 1574 | bytes 12608 | tf_op jit(solution)/shard_map/reduce_sum | solution.py:234
  8.4 1.6 %fusion.5 = bf16[9,7,128,128]{3,1,2,0:T(8,128)(2,1)S(1)} fusion(f32[1,9,7,25]{3,0,2,1:T(1,128)S(1)} %get-tuple-element.6, f32[]{:T(128)} %get-tuple-element.5), kind=kOutput, calls=%fused_computation.4 | convolution fusion | flops 53873744 | bytes 2070688 | tf_op jit(solution)/shard_map/abt,tpz->abpz/dot_general | solution.py:186
  9.9 1.9 %copy.6 = bf16[9,7,128,128]{3,2,1,0:T(8,128)(2,1)} copy(bf16[9,7,128,128]{3,1,2,0:T(8,128)(2,1)S(1)} %fusion.5) | data formatting | bytes 4128768 | tf_op jit(solution)/shard_map/convert_element_type | solution.py:186
  12.0 0.1 dynamic-slice_reduce_fusion
  12.2 0.1 broadcast_in_dim.27
  12.3 1.1 %fusion.20.src_ref = bf16[24,70,128]{2,1,0:T(8,128)(2,1)} fusion(s32[]{:T(128)S(6)} %select_n.56, bf16[4,128,128]{2,1,0:T(8,128)(2,1)S(1)} %collective-permute-done, bf16[16,128,128]{2,1,0:T(8,128)(2,1)S(1)} %convert_element_type.30, bf16[4,128,128]{2,1,0:T(8,128)(2,1)S(1)} %collective-permute-done.1), kind=kLoop, calls=%fused_computation.20 | loop fusion | flops 2795520 | bytes 1217536 | tf_op jit(solution)/shard_map/concatenate | solution.py:19
  13.4 7.1 %shard_map.46 = f32[16,64,128]{2,1,0:T(8,128)} custom-call(bf16[24,70,128]{2,1,0:T(8,128)(2,1)} %fusion.20.src_ref, bf16[9,896,128]{2,1,0:T(8,128)(2,1)} %bitcast.25), custom_call_target="tpu_custom_call" | custom-call | tf_op jit(solution)/shard_map/pallas_call | solution.py:210
  20.5 1.2 %fusion.17 = bf16[16,64,128]{2,1,0:T(8,128)(2,1)S(1)} fusion(f32[16,64,128]{2,1,0:T(8,128)} %shard_map.46, bf16[1,16,64,128]{3,2,1,0:T(8,128)(2,1)S(1)} %copy-done, pred[64]{0:T(512)(128)(4,1)S(1)} %broadcast_in_dim.27), kind=kLoop, calls=%fused_computation.17 | loop fusion | flops 524288 | bytes 1048640 | tf_op jit(solution)/shard_map/convert_element_type | solution.py:245
  21.7 2.2 %collective-permute-start.2 = (bf16[16,3,128]{2,1,0:T(4,128)(2,1)S(1)}, bf16[16,3,128]{2,1,0:T(4,128)(2,1)S(1)}, u32[]{:S(2)}, u32[]{:S(2)}) collective-permute-start(bf16[16,3,128]{2,1,0:T(4,128)(2,1)S(1)} %slice_select_fusion), channel_id=1, source_target_pairs={{0,16},{16,0},{32,48},{48,32},{64,80},{80,64},{96,112},{112,96},{1... | collective-permute-start | bytes 36872 | tf_op jit(solution)/shard_map/ppermute | solution.py:37
  23.9 0.7 fusion.29
  24.6 0.1 rev.3
  24.8 4.3 %collective-permute-start.3 = (bf16[4,70,128]{2,1,0:T(8,128)(2,1)S(1)}, bf16[4,70,128]{2,1,0:T(8,128)(2,1)S(1)}, u32[]{:S(2)}, u32[]{:S(2)}) collective-permute-start(bf16[4,70,128]{2,1,0:T(8,128)(2,1)S(1)} %get-tuple-element.9), channel_id=1, source_target_pairs={{0,1},{1,2},{2,3},{3,4},{4,5},{5,6},{6,7},{7,8},{8,9},{9,10},{10,1... | collective-permute-start | bytes 215048 | tf_op jit(solution)/shard_map/ppermute | solution.py:21
  29.1 2.1 %collective-permute-start.4 = (bf16[4,70,128]{2,1,0:T(8,128)(2,1)S(1)}, bf16[4,70,128]{2,1,0:T(8,128)(2,1)S(1)}, u32[]{:S(2)}, u32[]{:S(2)}) collective-permute-start(bf16[4,70,128]{2,1,0:T(8,128)(2,1)S(1)} %get-tuple-element.10), channel_id=1, source_target_pairs={{1,0},{2,1},{3,2},{4,3},{5,4},{6,5},{7,6},{8,7},{9,8},{10,9},{11,1... | collective-permute-start | bytes 215048 | tf_op jit(solution)/shard_map/ppermute | solution.py:23
  31.3 0.9 %fusion.8 = bf16[9,7,128,128]{3,1,2,0:T(8,128)(2,1)S(1)} fusion(bf16[9,7,25]{2,1,0:T(8,128)(2,1)S(1)} %rev.3), kind=kOutput, calls=%fused_computation.5 | convolution fusion | flops 53870592 | bytes 2067534 | tf_op jit(solution)/shard_map/abt,tpz->abpz/dot_general | solution.py:186
  32.1 1.9 %copy.7 = bf16[9,7,128,128]{3,2,1,0:T(8,128)(2,1)} copy(bf16[9,7,128,128]{3,1,2,0:T(8,128)(2,1)S(1)} %fusion.8) | data formatting | bytes 4128768 | tf_op jit(solution)/shard_map/convert_element_type | solution.py:186
  34.1 2.3 %collective-permute-done.4 = bf16[4,70,128]{2,1,0:T(8,128)(2,1)S(1)} collective-permute-done((bf16[4,70,128]{2,1,0:T(8,128)(2,1)S(1)}, bf16[4,70,128]{2,1,0:T(8,128)(2,1)S(1)}, u32[]{:S(2)}, u32[]{:S(2)}) %collective-permute-start.4) | collective-permute-done | bytes 71712 | tf_op jit(solution)/shard_map/ppermute | solution.py:23
  36.4 0.9 %pad_maximum_fusion.src_ref = bf16[24,70,128]{2,1,0:T(8,128)(2,1)} fusion(bf16[4,70,128]{2,1,0:T(8,128)(2,1)S(1)} %collective-permute-done.4, bf16[16,3,128]{2,1,0:T(4,128)(2,1)S(1)} %get-tuple-element.12, bf16[16,64,128]{2,1,0:T(8,128)(2,1)S(1)} %fusion.17, bf16[16,3,128]{2,1,0:T(4,128)(2,1)S(1)} %get-tuple-element.11, ...), kind=kLoop, calls=%fused_computation.23 | loop fusion | flops 2150400 | bytes 860160 | tf_op jit(solution)/shard_map/concatenate | solution.py:19
  37.2 7.1 %shard_map.47 = f32[16,64,128]{2,1,0:T(8,128)} custom-call(bf16[24,70,128]{2,1,0:T(8,128)(2,1)} %pad_maximum_fusion.src_ref, bf16[9,896,128]{2,1,0:T(8,128)(2,1)} %bitcast.26), custom_call_target="tpu_custom_call" | custom-call | tf_op jit(solution)/shard_map/pallas_call | solution.py:210
  44.3 2.0 %broadcast_select_fusion.factor_ref = f32[16,64,128]{2,1,0:T(8,128)} fusion(f32[16,64,128]{2,1,0:T(8,128)} %shard_map.47, pred[64]{0:T(512)(128)(4,1)S(1)} %broadcast_in_dim.27), kind=kLoop, calls=%fused_computation.24 | loop fusion | flops 131072 | bytes 1048640 | tf_op jit(solution)/shard_map/jit(_where)/select_n | solution.py:254
  46.2 36.9 %shard_map.48 = f32[16,128,128]{2,1,0:T(8,128)} custom-call(f32[16,64,128]{2,1,0:T(8,128)} %broadcast_select_fusion.factor_ref, f32[16,128,128]{2,1,0:T(8,128)} %est_ref.1), custom_call_target="tpu_custom_call" | custom-call | tf_op jit(solution)/shard_map/pallas_call | solution.py:160
  83.2 2.3 %copy.21 = f32[16,128,128]{2,1,0:T(8,128)} copy(f32[16,128,128]{2,1,0:T(8,128)} %shard_map.48) | data formatting | bytes 2097152
  (14 shorter events, 0.3 us)
Async XLA Ops:
  1.3 10.9 %collective-permute-start = (bf16[4,128,128]{2,1,0:T(8,128)(2,1)S(1)}, bf16[4,128,128]{2,1,0:T(8,128)(2,1)S(1)}, u32[]{:S(2)}, u32[]{:S(2)}) collective-permute-start(bf16[4,128,128]{2,1,0:T(8,128)(2,1)S(1)} %get-tuple-element.8), channel_id=1, source_target_pairs={{0,1},{1,2},{2,3},{3,4},{4,5},{5,6},{6,7},{7,8},{8,9},{9,10},{10,1... | collective-permute-start | bytes 393224 | tf_op jit(solution)/shard_map/ppermute | solution.py:21
  4.5 7.8 %collective-permute-start.1 = (bf16[4,128,128]{2,1,0:T(8,128)(2,1)S(1)}, bf16[4,128,128]{2,1,0:T(8,128)(2,1)S(1)}, u32[]{:S(2)}, u32[]{:S(2)}) collective-permute-start(bf16[4,128,128]{2,1,0:T(8,128)(2,1)S(1)} %get-tuple-element.7), channel_id=1, source_target_pairs={{1,0},{2,1},{3,2},{4,3},{5,4},{6,5},{7,6},{8,7},{9,8},{10,9},{11,1... | collective-permute-start | bytes 393224 | tf_op jit(solution)/shard_map/ppermute | solution.py:23
  9.9 1.9 %copy-start.1 = (s32[8,1,4]{0,2,1:T(4,128)S(1)}, s32[8,1,4]{0,2,1:T(4,128)}, u32[]{:S(2)}) copy-start(s32[8,1,4]{0,2,1:T(4,128)} %param.7) | copy-start | bytes 388
  12.2 8.2 %copy-start = (bf16[1,16,64,128]{3,2,1,0:T(8,128)(2,1)S(1)}, bf16[1,16,64,128]{3,2,1,0:T(8,128)(2,1)}, u32[]{:S(2)}) copy-start(bf16[1,16,64,128]{3,2,1,0:T(8,128)(2,1)} %param.5) | copy-start | bytes 786436
  21.7 3.0 %collective-permute-start.2 = (bf16[16,3,128]{2,1,0:T(4,128)(2,1)S(1)}, bf16[16,3,128]{2,1,0:T(4,128)(2,1)S(1)}, u32[]{:S(2)}, u32[]{:S(2)}) collective-permute-start(bf16[16,3,128]{2,1,0:T(4,128)(2,1)S(1)} %slice_select_fusion), channel_id=1, source_target_pairs={{0,16},{16,0},{32,48},{48,32},{64,80},{80,64},{96,112},{112,96},{1... | collective-permute-start | bytes 36872 | tf_op jit(solution)/shard_map/ppermute | solution.py:37
  24.8 9.2 %collective-permute-start.3 = (bf16[4,70,128]{2,1,0:T(8,128)(2,1)S(1)}, bf16[4,70,128]{2,1,0:T(8,128)(2,1)S(1)}, u32[]{:S(2)}, u32[]{:S(2)}) collective-permute-start(bf16[4,70,128]{2,1,0:T(8,128)(2,1)S(1)} %get-tuple-element.9), channel_id=1, source_target_pairs={{0,1},{1,2},{2,3},{3,4},{4,5},{5,6},{6,7},{7,8},{8,9},{9,10},{10,1... | collective-permute-start | bytes 215048 | tf_op jit(solution)/shard_map/ppermute | solution.py:21
  29.1 7.2 %collective-permute-start.4 = (bf16[4,70,128]{2,1,0:T(8,128)(2,1)S(1)}, bf16[4,70,128]{2,1,0:T(8,128)(2,1)S(1)}, u32[]{:S(2)}, u32[]{:S(2)}) collective-permute-start(bf16[4,70,128]{2,1,0:T(8,128)(2,1)S(1)} %get-tuple-element.10), channel_id=1, source_target_pairs={{1,0},{2,1},{3,2},{4,3},{5,4},{6,5},{7,6},{8,7},{9,8},{10,9},{11,1... | collective-permute-start | bytes 215048 | tf_op jit(solution)/shard_map/ppermute | solution.py:23

commit v7 on v6

--- a/solution.py
+++ b/solution.py
@@ -48,9 +48,14 @@
     )
 
 
-def product_kernel(n, shares, factor_ref, est_ref, out_ref, held, send1, recv1, send2, recv2):
+def product_kernel(
+    n, shares, quot_ref, band_ref, cover_ref, est_ref, out_ref, cols_ref, factor_ref, held,
+    send1, recv1, send2, recv2,
+):
     groups = n // shares
     step, share_w, depth = held.shape[1:]
+    taps_x = band_ref.shape[0]
+    taps_y = quot_ref.shape[1] - share_w + 1
     me = lax.axis_index("view")
     view_id = me // shares
     part = me % shares
@@ -66,10 +71,25 @@
             barrier, inc=1, device_id={"view": view_id * shares + (part + d) % shares},
             device_id_type=mesh_kind,
         )
+    for step_y in range(taps_y):
+        cols_ref[:, :, step_y * depth : (step_y + 1) * depth] = quot_ref[:, step_y : step_y + share_w, :]
+    keep = cover_ref[...] > 0
+
+    def factor_rows(target):
+        acc = None
+        for shift_x in range(taps_x):
+            lhs = cols_ref[pl.ds(target * step + shift_x, step)].reshape(step * share_w, -1)
+            part_sum = jnp.dot(lhs, band_ref[shift_x], preferred_element_type=jnp.float32)
+            acc = part_sum if acc is None else acc + part_sum
+        acc = acc.reshape(step, share_w, depth)
+        factor_ref[pl.ds(target * step, step)] = jnp.where(keep[None], acc, 1.0)
+
+    factor_rows(view_id)
     pl.semaphore_wait(barrier, groups + shares - 2)
     outgoing = []
     for d in range(1, groups):
         target = (view_id + d) % groups
+        factor_rows(target)
         copy = pltpu.make_async_remote_copy(
             src_ref=factor_ref.at[pl.ds(target * step, step)],
             dst_ref=held.at[view_id],
@@ -151,18 +171,21 @@
         copy.wait_send()
 
 
-def product_gather(share_factor, estimate, shares):
+def product_gather(quotient_rimmed, banded, cover_plane, estimate, shares):
     n = lax.axis_size("view")
     groups = n // shares
-    slab_x, share_w, depth = share_factor.shape
+    slab_x, width_y, depth = estimate.shape
+    share_w = cover_plane.shape[0]
     step = slab_x // groups
     vmem = pl.BlockSpec(memory_space=pltpu.VMEM)
     return pl.pallas_call(
         functools.partial(product_kernel, n, shares),
         out_shape=jax.ShapeDtypeStruct(estimate.shape, jnp.float32),
-        in_specs=[vmem, vmem],
+        in_specs=[vmem] * 4,
         out_specs=vmem,
         scratch_shapes=[
+            pltpu.VMEM((quotient_rimmed.shape[0], share_w, banded.shape[1]), jnp.bfloat16),
+            pltpu.VMEM((slab_x, share_w, depth), jnp.float32),
             pltpu.VMEM((groups, step, share_w, depth), jnp.float32),
             pltpu.SemaphoreType.DMA((groups,)),
             pltpu.SemaphoreType.DMA((groups,)),
@@ -170,7 +193,7 @@
             pltpu.SemaphoreType.DMA((groups + shares,)),
         ],
         compiler_params=pltpu.CompilerParams(collective_id=0, has_side_effects=True),
-    )(share_factor, estimate)
+    )(quotient_rimmed, banded, cover_plane, estimate)
 
 
 def band_table(kernel, depth):
@@ -250,9 +273,8 @@
     upper_rim = jnp.where(part < shares - 1, partner, rim_zeros)
     extended = jnp.concatenate([lower_rim, quotient, upper_rim], axis=1)
     quotient_rimmed = with_halo(extended, (("blk", 0),), rim_x)
-    correction = convolve(quotient_rimmed, backward, slab_x, share_w)
-    share_factor = jnp.where(cell_cover, correction, 1.0)
-    return product_gather(share_factor, estimate, shares)
+    cover_plane = jnp.broadcast_to(cell_cover[0].astype(jnp.float32), (share_w, depth))
+    return product_gather(quotient_rimmed, backward, cover_plane, estimate, shares)
 
 
 def solution(mesh):

time: 86.5 us -> 82.5 us (0.954)
  Pallas kernels: 51.1 us -> 48.4 us
  other arithmetic: 8.99 us -> 7.04 us
    pallas_call x2 -> x1, Pallas kernels: 14.1 us -> 7.07 us  [convolve(): pl.pallas_call(functools.partial(conv_kernel, 4), out_shape=jax.ShapeDtyp...]
    pallas_call x1, Pallas kernels: 36.9 us -> 41.3 us  [product_gather(): pl.pallas_call(functools.partial(product_kernel, n, shares), out_shape=ja...]
    select_n x1 -> x0, other arithmetic: 1.96 us -> none  [local(): share_factor = jnp.where(cell_cover, correction, 1.0)]
where the time goes in v7:
time: 82.5 us; the launch traced here: 81.5 us
  Pallas kernels  48.4 us (59%)
  starting transfers between devices  13.9 us (17%)
  local copies, waits for them, and re-layouts  7.24 us (9%)
  other arithmetic  7.04 us (9%)
  matrix products  2.41 us (3%)
  waiting for transfers between devices  2.36 us (3%)
    pallas_call x1, Pallas kernels, product_gather(): pl.pallas_call(functools.partial(product_kernel, n, shares), out_shape=ja...  41.3 us
    ppermute x2, starting transfers between devices, with_halo(): lax.ppermute(tail, axis, [(i, (i + 1) % count) for i in range(ends)])  7.44 us
    pallas_call x1, Pallas kernels, convolve(): pl.pallas_call(functools.partial(conv_kernel, 4), out_shape=jax.ShapeDtyp...  7.07 us
    ppermute x2, starting transfers between devices, with_halo(): lax.ppermute(head, axis, [((i + 1) % count, i) for i in range(ends)])  4.26 us
    convert_element_type x2, local copies, waits for them, and re-layouts, band_table(): jnp.einsum('abt,tpz->abpz', kernel, onehot, preferred_element_type=jnp.fl...  3.85 us
    dot_general x2, matrix products, band_table(): jnp.einsum('abt,tpz->abpz', kernel, onehot, preferred_element_type=jnp.fl...  2.41 us
    ppermute x2, waiting for transfers between devices, with_halo(): lax.ppermute(head, axis, [((i + 1) % count, i) for i in range(ends)])  2.34 us
    unnamed x5, local copies, waits for them, and re-layouts  2.31 us
  transfers between devices with their start and end apart: 5, of which 1 were waited for; matrix products, arithmetic and copies ran while one was open for 11% of the time, Pallas kernels for 0%

profile of v7, /device:TPU:71, one launch (start us, length us, event | category | flops | bytes accessed | tf_op | source)
XLA Modules:
  0.0 81.5 jit_solution(15467443650397041001)
XLA Ops:
  0.0 1.3 %convert_element_type.38 = bf16[16,128,128]{2,1,0:T(8,128)(2,1)S(1)} convert(f32[16,128,128]{2,1,0:T(8,128)} %est_ref.1) | non-fusion elementwise | flops 262144 | bytes 1572864 | tf_op jit(solution)/shard_map/convert_element_type | solution.py:253
  1.3 3.1 %collective-permute-start = (bf16[4,128,128]{2,1,0:T(8,128)(2,1)S(1)}, bf16[4,128,128]{2,1,0:T(8,128)(2,1)S(1)}, u32[]{:S(2)}, u32[]{:S(2)}) collective-permute-start(bf16[4,128,128]{2,1,0:T(8,128)(2,1)S(1)} %get-tuple-element.8), channel_id=1, source_target_pairs={{0,1},{1,2},{2,3},{3,4},{4,5},{5,6},{6,7},{7,8},{8,9},{9,10},{10,1... | collective-permute-start | bytes 393224 | tf_op jit(solution)/shard_map/ppermute | solution.py:21
  4.5 2.2 %collective-permute-start.1 = (bf16[4,128,128]{2,1,0:T(8,128)(2,1)S(1)}, bf16[4,128,128]{2,1,0:T(8,128)(2,1)S(1)}, u32[]{:S(2)}, u32[]{:S(2)}) collective-permute-start(bf16[4,128,128]{2,1,0:T(8,128)(2,1)S(1)} %get-tuple-element.7), channel_id=1, source_target_pairs={{1,0},{2,1},{3,2},{4,3},{5,4},{6,5},{7,6},{8,7},{9,8},{10,9},{11,1... | collective-permute-start | bytes 393224 | tf_op jit(solution)/shard_map/ppermute | solution.py:23
  6.7 1.7 %fusion.30 = (f32[]{:T(128)}, f32[1,9,7,25]{3,0,2,1:T(1,128)S(1)}) fusion(f32[8,9,7,25]{3,0,2,1:T(8,128)} %param.6, s32[]{:T(128)S(6)} %select_n.51), kind=kLoop, calls=%fused_computation.40 | loop fusion | flops 1574 | bytes 12608 | tf_op jit(solution)/shard_map/reduce_sum | solution.py:257
  8.4 1.6 %fusion.5 = bf16[9,7,128,128]{3,1,2,0:T(8,128)(2,1)S(1)} fusion(f32[1,9,7,25]{3,0,2,1:T(1,128)S(1)} %get-tuple-element.6, f32[]{:T(128)} %get-tuple-element.5), kind=kOutput, calls=%fused_computation.4 | convolution fusion | flops 53873744 | bytes 2070688 | tf_op jit(solution)/shard_map/abt,tpz->abpz/dot_general | solution.py:209
  9.9 1.9 %copy.6 = bf16[9,7,128,128]{3,2,1,0:T(8,128)(2,1)} copy(bf16[9,7,128,128]{3,1,2,0:T(8,128)(2,1)S(1)} %fusion.5) | data formatting | bytes 4128768 | tf_op jit(solution)/shard_map/convert_element_type | solution.py:209
  12.0 0.1 dynamic-slice_reduce_fusion
  12.1 0.1 broadcast_in_dim.25
  12.2 0.1 broadcast_in_dim.26
  12.3 1.1 %fusion.20.src_ref = bf16[24,70,128]{2,1,0:T(8,128)(2,1)} fusion(s32[]{:T(128)S(6)} %select_n.53, bf16[4,128,128]{2,1,0:T(8,128)(2,1)S(1)} %collective-permute-done, bf16[16,128,128]{2,1,0:T(8,128)(2,1)S(1)} %convert_element_type.38, bf16[4,128,128]{2,1,0:T(8,128)(2,1)S(1)} %collective-permute-done.1), kind=kLoop, calls=%fused_computation.20 | loop fusion | flops 2795520 | bytes 1217536 | tf_op jit(solution)/shard_map/concatenate | solution.py:19
  13.4 7.1 %shard_map.46 = f32[16,64,128]{2,1,0:T(8,128)} custom-call(bf16[24,70,128]{2,1,0:T(8,128)(2,1)} %fusion.20.src_ref, bf16[9,896,128]{2,1,0:T(8,128)(2,1)} %bitcast.25), custom_call_target="tpu_custom_call" | custom-call | tf_op jit(solution)/shard_map/pallas_call | solution.py:233
  20.5 1.2 %fusion.17 = bf16[16,64,128]{2,1,0:T(8,128)(2,1)S(1)} fusion(f32[16,64,128]{2,1,0:T(8,128)} %shard_map.46, bf16[1,16,64,128]{3,2,1,0:T(8,128)(2,1)S(1)} %copy-done, pred[64]{0:T(512)(128)(4,1)S(1)} %broadcast_in_dim.26), kind=kLoop, calls=%fused_computation.17 | loop fusion | flops 524288 | bytes 1048640 | tf_op jit(solution)/shard_map/convert_element_type | solution.py:268
  21.7 2.2 %collective-permute-start.2 = (bf16[16,3,128]{2,1,0:T(4,128)(2,1)S(1)}, bf16[16,3,128]{2,1,0:T(4,128)(2,1)S(1)}, u32[]{:S(2)}, u32[]{:S(2)}) collective-permute-start(bf16[16,3,128]{2,1,0:T(4,128)(2,1)S(1)} %slice_select_fusion), channel_id=1, source_target_pairs={{0,16},{16,0},{32,48},{48,32},{64,80},{80,64},{96,112},{112,96},{1... | collective-permute-start | bytes 36872 | tf_op jit(solution)/shard_map/ppermute | solution.py:37
  23.9 0.7 fusion.29
  24.6 0.1 rev.3
  24.8 4.3 %collective-permute-start.3 = (bf16[4,70,128]{2,1,0:T(8,128)(2,1)S(1)}, bf16[4,70,128]{2,1,0:T(8,128)(2,1)S(1)}, u32[]{:S(2)}, u32[]{:S(2)}) collective-permute-start(bf16[4,70,128]{2,1,0:T(8,128)(2,1)S(1)} %get-tuple-element.9), channel_id=1, source_target_pairs={{0,1},{1,2},{2,3},{3,4},{4,5},{5,6},{6,7},{7,8},{8,9},{9,10},{10,1... | collective-permute-start | bytes 215048 | tf_op jit(solution)/shard_map/ppermute | solution.py:21
  29.1 2.1 %collective-permute-start.4 = (bf16[4,70,128]{2,1,0:T(8,128)(2,1)S(1)}, bf16[4,70,128]{2,1,0:T(8,128)(2,1)S(1)}, u32[]{:S(2)}, u32[]{:S(2)}) collective-permute-start(bf16[4,70,128]{2,1,0:T(8,128)(2,1)S(1)} %get-tuple-element.10), channel_id=1, source_target_pairs={{1,0},{2,1},{3,2},{4,3},{5,4},{6,5},{7,6},{8,7},{9,8},{10,9},{11,1... | collective-permute-start | bytes 215048 | tf_op jit(solution)/shard_map/ppermute | solution.py:23
  31.3 0.9 %fusion.8 = bf16[9,7,128,128]{3,1,2,0:T(8,128)(2,1)S(1)} fusion(bf16[9,7,25]{2,1,0:T(8,128)(2,1)S(1)} %rev.3), kind=kOutput, calls=%fused_computation.5 | convolution fusion | flops 53870592 | bytes 2067534 | tf_op jit(solution)/shard_map/abt,tpz->abpz/dot_general | solution.py:209
  32.1 1.9 %copy.7 = bf16[9,7,128,128]{3,2,1,0:T(8,128)(2,1)} copy(bf16[9,7,128,128]{3,1,2,0:T(8,128)(2,1)S(1)} %fusion.8) | data formatting | bytes 4128768 | tf_op jit(solution)/shard_map/convert_element_type | solution.py:209
  34.1 2.3 %collective-permute-done.4 = bf16[4,70,128]{2,1,0:T(8,128)(2,1)S(1)} collective-permute-done((bf16[4,70,128]{2,1,0:T(8,128)(2,1)S(1)}, bf16[4,70,128]{2,1,0:T(8,128)(2,1)S(1)}, u32[]{:S(2)}, u32[]{:S(2)}) %collective-permute-start.4) | collective-permute-done | bytes 71712 | tf_op jit(solution)/shard_map/ppermute | solution.py:23
  36.4 0.9 %pad_maximum_fusion.quot_ref = bf16[24,70,128]{2,1,0:T(8,128)(2,1)} fusion(bf16[4,70,128]{2,1,0:T(8,128)(2,1)S(1)} %collective-permute-done.4, bf16[16,3,128]{2,1,0:T(4,128)(2,1)S(1)} %get-tuple-element.12, bf16[16,64,128]{2,1,0:T(8,128)(2,1)S(1)} %fusion.17, bf16[16,3,128]{2,1,0:T(4,128)(2,1)S(1)} %get-tuple-element.11, ...), kind=kLoop, calls=%fused_computation.23 | loop fusion | flops 2150400 | bytes 860160 | tf_op jit(solution)/shard_map/concatenate | solution.py:19
  37.2 0.7 broadcast_in_dim.30.cover_ref
  37.9 41.3 %shard_map.47 = f32[16,128,128]{2,1,0:T(8,128)} custom-call(bf16[24,70,128]{2,1,0:T(8,128)(2,1)} %pad_maximum_fusion.quot_ref, bf16[9,896,128]{2,1,0:T(8,128)(2,1)} %bitcast.26, f32[64,128]{1,0:T(8,128)} %broadcast_in_dim.30.cover_ref, f32[16,128,128]{2,1,0:T(8,128)} %est_ref.1), custom_call_target="tpu_custom_call" | custom-call | tf_op jit(solution)/shard_map/pallas_call | solution.py:181
  79.2 2.3 %copy.21 = f32[16,128,128]{2,1,0:T(8,128)} copy(f32[16,128,128]{2,1,0:T(8,128)} %shard_map.47) | data formatting | bytes 2097152
  (14 shorter events, 0.3 us)
Async XLA Ops:
  1.3 10.9 %collective-permute-start = (bf16[4,128,128]{2,1,0:T(8,128)(2,1)S(1)}, bf16[4,128,128]{2,1,0:T(8,128)(2,1)S(1)}, u32[]{:S(2)}, u32[]{:S(2)}) collective-permute-start(bf16[4,128,128]{2,1,0:T(8,128)(2,1)S(1)} %get-tuple-element.8), channel_id=1, source_target_pairs={{0,1},{1,2},{2,3},{3,4},{4,5},{5,6},{6,7},{7,8},{8,9},{9,10},{10,1... | collective-permute-start | bytes 393224 | tf_op jit(solution)/shard_map/ppermute | solution.py:21
  4.5 7.8 %collective-permute-start.1 = (bf16[4,128,128]{2,1,0:T(8,128)(2,1)S(1)}, bf16[4,128,128]{2,1,0:T(8,128)(2,1)S(1)}, u32[]{:S(2)}, u32[]{:S(2)}) collective-permute-start(bf16[4,128,128]{2,1,0:T(8,128)(2,1)S(1)} %get-tuple-element.7), channel_id=1, source_target_pairs={{1,0},{2,1},{3,2},{4,3},{5,4},{6,5},{7,6},{8,7},{9,8},{10,9},{11,1... | collective-permute-start | bytes 393224 | tf_op jit(solution)/shard_map/ppermute | solution.py:23
  9.9 1.9 %copy-start.1 = (s32[8,1,4]{0,2,1:T(4,128)S(1)}, s32[8,1,4]{0,2,1:T(4,128)}, u32[]{:S(2)}) copy-start(s32[8,1,4]{0,2,1:T(4,128)} %param.7) | copy-start | bytes 388
  12.2 8.2 %copy-start = (bf16[1,16,64,128]{3,2,1,0:T(8,128)(2,1)S(1)}, bf16[1,16,64,128]{3,2,1,0:T(8,128)(2,1)}, u32[]{:S(2)}) copy-start(bf16[1,16,64,128]{3,2,1,0:T(8,128)(2,1)} %param.5) | copy-start | bytes 786436
  21.7 3.0 %collective-permute-start.2 = (bf16[16,3,128]{2,1,0:T(4,128)(2,1)S(1)}, bf16[16,3,128]{2,1,0:T(4,128)(2,1)S(1)}, u32[]{:S(2)}, u32[]{:S(2)}) collective-permute-start(bf16[16,3,128]{2,1,0:T(4,128)(2,1)S(1)} %slice_select_fusion), channel_id=1, source_target_pairs={{0,16},{16,0},{32,48},{48,32},{64,80},{80,64},{96,112},{112,96},{1... | collective-permute-start | bytes 36872 | tf_op jit(solution)/shard_map/ppermute | solution.py:37
  24.8 9.2 %collective-permute-start.3 = (bf16[4,70,128]{2,1,0:T(8,128)(2,1)S(1)}, bf16[4,70,128]{2,1,0:T(8,128)(2,1)S(1)}, u32[]{:S(2)}, u32[]{:S(2)}) collective-permute-start(bf16[4,70,128]{2,1,0:T(8,128)(2,1)S(1)} %get-tuple-element.9), channel_id=1, source_target_pairs={{0,1},{1,2},{2,3},{3,4},{4,5},{5,6},{6,7},{7,8},{8,9},{9,10},{10,1... | collective-permute-start | bytes 215048 | tf_op jit(solution)/shard_map/ppermute | solution.py:21
  29.1 7.2 %collective-permute-start.4 = (bf16[4,70,128]{2,1,0:T(8,128)(2,1)S(1)}, bf16[4,70,128]{2,1,0:T(8,128)(2,1)S(1)}, u32[]{:S(2)}, u32[]{:S(2)}) collective-permute-start(bf16[4,70,128]{2,1,0:T(8,128)(2,1)S(1)} %get-tuple-element.10), channel_id=1, source_target_pairs={{1,0},{2,1},{3,2},{4,3},{5,4},{6,5},{7,6},{8,7},{9,8},{10,9},{11,1... | collective-permute-start | bytes 215048 | tf_op jit(solution)/shard_map/ppermute | solution.py:23

commit v8 on v7

--- a/solution.py
+++ b/solution.py
@@ -196,6 +196,61 @@
     )(quotient_rimmed, banded, cover_plane, estimate)
 
 
+def halo_kernel(width, cells_ref, out_ref, send_sem, recv_sem):
+    n = lax.axis_size("blk")
+    me = lax.axis_index("blk")
+    rows = cells_ref.shape[0]
+    up = (me + 1) % n
+    down = (me + n - 1) % n
+    mesh_kind = pl.DeviceIdType.MESH
+    barrier = pltpu.get_barrier_semaphore()
+    for other in (up, down):
+        pl.semaphore_signal(barrier, inc=1, device_id={"blk": other}, device_id_type=mesh_kind)
+    pl.semaphore_wait(barrier, 2)
+    to_up = pltpu.make_async_remote_copy(
+        src_ref=cells_ref.at[pl.ds(rows - width, width)],
+        dst_ref=out_ref.at[pl.ds(0, width)],
+        send_sem=send_sem.at[0],
+        recv_sem=recv_sem.at[0],
+        device_id={"blk": up},
+        device_id_type=mesh_kind,
+    )
+    to_down = pltpu.make_async_remote_copy(
+        src_ref=cells_ref.at[pl.ds(0, width)],
+        dst_ref=out_ref.at[pl.ds(rows + width, width)],
+        send_sem=send_sem.at[1],
+        recv_sem=recv_sem.at[1],
+        device_id={"blk": down},
+        device_id_type=mesh_kind,
+    )
+    to_up.start()
+    to_down.start()
+    out_ref[pl.ds(width, rows)] = cells_ref[...]
+    to_up.wait()
+    to_down.wait()
+
+    @pl.when(me == 0)
+    def _():
+        out_ref[pl.ds(0, width)] = jnp.zeros((width,) + cells_ref.shape[1:], cells_ref.dtype)
+
+    @pl.when(me == n - 1)
+    def _():
+        out_ref[pl.ds(rows + width, width)] = jnp.zeros((width,) + cells_ref.shape[1:], cells_ref.dtype)
+
+
+def halo_exchange(cells, width, kernel_id):
+    vmem = pl.BlockSpec(memory_space=pltpu.VMEM)
+    shape = (cells.shape[0] + 2 * width,) + cells.shape[1:]
+    return pl.pallas_call(
+        functools.partial(halo_kernel, width),
+        out_shape=jax.ShapeDtypeStruct(shape, cells.dtype),
+        in_specs=[vmem],
+        out_specs=vmem,
+        scratch_shapes=[pltpu.SemaphoreType.DMA((2,)), pltpu.SemaphoreType.DMA((2,))],
+        compiler_params=pltpu.CompilerParams(collective_id=kernel_id, has_side_effects=True),
+    )(cells)
+
+
 def band_table(kernel, depth):
     taps_x, taps_y, taps_z = kernel.shape
     rim_z = (taps_z - 1) // 2
@@ -251,7 +306,7 @@
     part = group % shares
     y_start = part * share_w
     source = estimate.astype(jnp.bfloat16)
-    rimmed = with_halo(source, (("blk", 0),), rim_x)
+    rimmed = halo_exchange(source, rim_x, 1)
     padded = jnp.pad(rimmed, ((0, 0), (rim_y, rim_y), (0, 0)))
     spread = lax.dynamic_index_in_dim(point_spread, view_id, 0, keepdims=False)
     kernel = (spread / jnp.sum(spread)).astype(jnp.bfloat16)
@@ -272,7 +327,7 @@
     lower_rim = jnp.where(part > 0, partner, rim_zeros)
     upper_rim = jnp.where(part < shares - 1, partner, rim_zeros)
     extended = jnp.concatenate([lower_rim, quotient, upper_rim], axis=1)
-    quotient_rimmed = with_halo(extended, (("blk", 0),), rim_x)
+    quotient_rimmed = halo_exchange(extended, rim_x, 2)
     cover_plane = jnp.broadcast_to(cell_cover[0].astype(jnp.float32), (share_w, depth))
     return product_gather(quotient_rimmed, backward, cover_plane, estimate, shares)
 

time: 82.5 us -> 87.5 us (1.061)
  the two profiles are of different devices: /device:TPU:71 before, /device:TPU:65 now
where the time goes in v8:
time: 87.5 us; the launch traced here: 87.2 us
  Pallas kernels  68.5 us (78%)
  local copies, waits for them, and re-layouts  9.27 us (11%)
  other arithmetic  5.34 us (6%)
  matrix products  2.36 us (3%)
  starting transfers between devices  1.65 us (2%)
    pallas_call x1, Pallas kernels, product_gather(): pl.pallas_call(functools.partial(product_kernel, n, shares), out_shape=ja...  41.9 us
    pallas_call x2, Pallas kernels, halo_exchange(): pl.pallas_call(functools.partial(halo_kernel, width), out_shape=jax.Shape...  19.5 us
    pallas_call x1, Pallas kernels, convolve(): pl.pallas_call(functools.partial(conv_kernel, 4), out_shape=jax.ShapeDtyp...  7.07 us
    convert_element_type x2, local copies, waits for them, and re-layouts, band_table(): jnp.einsum('abt,tpz->abpz', kernel, onehot, preferred_element_type=jnp.fl...  3.9 us
    dot_general x2, matrix products, band_table(): jnp.einsum('abt,tpz->abpz', kernel, onehot, preferred_element_type=jnp.fl...  2.36 us
    unnamed x7, local copies, waits for them, and re-layouts  2.31 us
    dynamic_slice x1, local copies, waits for them, and re-layouts, local(): lax.dynamic_slice(padded, (0, y_start, 0), (slab_x + 2 * rim_x, share_w +...  1.98 us
  transfers between devices with their start and end apart: 1, of which 0 were waited for; matrix products, arithmetic and copies ran while one was open for 4% of the time, Pallas kernels for 0%

profile of v8, /device:TPU:65, one launch (start us, length us, event | category | flops | bytes accessed | tf_op | source)
XLA Modules:
  0.0 87.2 jit_solution(6805329719011767552)
XLA Ops:
  0.0 1.7 %fusion.22 = (f32[]{:T(128)}, f32[1,9,7,25]{3,0,2,1:T(1,128)S(1)}) fusion(f32[8,9,7,25]{3,0,2,1:T(8,128)} %param.6, s32[]{:T(128)S(6)} %select_n.51), kind=kLoop, calls=%fused_computation.26 | loop fusion | flops 1574 | bytes 12608 | tf_op jit(solution)/shard_map/reduce_sum | solution.py:312
  1.7 1.5 %fusion.5 = bf16[9,7,128,128]{3,1,2,0:T(8,128)(2,1)S(1)} fusion(f32[1,9,7,25]{3,0,2,1:T(1,128)S(1)} %get-tuple-element.6, f32[]{:T(128)} %get-tuple-element.5), kind=kOutput, calls=%fused_computation.4 | convolution fusion | flops 53873744 | bytes 2070688 | tf_op jit(solution)/shard_map/abt,tpz->abpz/dot_general | solution.py:264
  3.2 0.0 copy-start
  3.2 1.9 %copy.6 = bf16[9,7,128,128]{3,2,1,0:T(8,128)(2,1)} copy(bf16[9,7,128,128]{3,1,2,0:T(8,128)(2,1)S(1)} %fusion.5) | data formatting | bytes 4128768 | tf_op jit(solution)/shard_map/convert_element_type | solution.py:264
  5.1 0.9 %convert_element_type.38.cells_ref = bf16[16,128,128]{2,1,0:T(8,128)(2,1)} convert(f32[16,128,128]{2,1,0:T(8,128)S(1)} %copy-done) | non-fusion elementwise | flops 262144 | bytes 1572864 | tf_op jit(solution)/shard_map/convert_element_type | solution.py:308
  6.0 10.4 %shard_map.46 = bf16[24,128,128]{2,1,0:T(8,128)(2,1)} custom-call(bf16[16,128,128]{2,1,0:T(8,128)(2,1)} %convert_element_type.38.cells_ref), custom_call_target="tpu_custom_call" | custom-call | tf_op jit(solution)/shard_map/pallas_call | solution.py:244
  16.4 0.1 dynamic-slice_compare_fusion
  16.5 0.1 dynamic-slice_reduce_fusion
  16.6 0.1 broadcast_in_dim.25
  16.7 0.1 broadcast_in_dim.26
  16.8 2.0 %pad_dynamic-slice_fusion.src_ref = bf16[24,70,128]{2,1,0:T(8,128)(2,1)} fusion(s32[]{:T(128)S(6)} %select_n.53, bf16[24,128,128]{2,1,0:T(8,128)(2,1)} %shard_map.46), kind=kLoop, calls=%fused_computation.8 | loop fusion | bytes 1216516 | tf_op jit(solution)/shard_map/dynamic_slice | solution.py:319
  18.8 7.1 %shard_map.47 = f32[16,64,128]{2,1,0:T(8,128)} custom-call(bf16[24,70,128]{2,1,0:T(8,128)(2,1)} %pad_dynamic-slice_fusion.src_ref, bf16[9,896,128]{2,1,0:T(8,128)(2,1)} %bitcast.25), custom_call_target="tpu_custom_call" | custom-call | tf_op jit(solution)/shard_map/pallas_call | solution.py:288
  25.8 1.2 %fusion.14 = bf16[16,64,128]{2,1,0:T(8,128)(2,1)S(1)} fusion(f32[16,64,128]{2,1,0:T(8,128)} %shard_map.47, bf16[1,16,64,128]{3,2,1,0:T(8,128)(2,1)S(1)} %copy-done.1, pred[64]{0:T(512)(128)(4,1)S(1)} %broadcast_in_dim.26), kind=kLoop, calls=%fused_computation.11 | loop fusion | flops 524288 | bytes 1048640 | tf_op jit(solution)/shard_map/convert_element_type | solution.py:323
  27.1 1.7 %collective-permute-start = (bf16[16,3,128]{2,1,0:T(4,128)(2,1)S(1)}, bf16[16,3,128]{2,1,0:T(4,128)(2,1)S(1)}, u32[]{:S(2)}, u32[]{:S(2)}) collective-permute-start(bf16[16,3,128]{2,1,0:T(4,128)(2,1)S(1)} %slice_select_fusion), channel_id=1, source_target_pairs={{0,16},{16,0},{32,48},{48,32},{64,80},{80,64},{96,112},{112,96},{1... | collective-permute-start | bytes 36872 | tf_op jit(solution)/shard_map/ppermute | solution.py:37
  28.7 0.6 fusion.21
  29.4 0.1 rev.3
  29.5 0.9 fusion.8
  30.4 1.9 %copy.7 = bf16[9,7,128,128]{3,2,1,0:T(8,128)(2,1)} copy(bf16[9,7,128,128]{3,1,2,0:T(8,128)(2,1)S(1)} %fusion.8) | data formatting | bytes 4128768 | tf_op jit(solution)/shard_map/convert_element_type | solution.py:264
  32.3 0.0 collective-permute-done
  32.3 0.8 pad_maximum_fusion.cells_ref
  33.2 9.2 %shard_map.48.quot_ref = bf16[24,70,128]{2,1,0:T(8,128)(2,1)} custom-call(bf16[16,70,128]{2,1,0:T(8,128)(2,1)} %pad_maximum_fusion.cells_ref), custom_call_target="tpu_custom_call" | custom-call | tf_op jit(solution)/shard_map/pallas_call | solution.py:244
  42.3 0.7 broadcast_in_dim.30.cover_ref
  43.0 41.9 %shard_map.49 = f32[16,128,128]{2,1,0:T(8,128)} custom-call(bf16[24,70,128]{2,1,0:T(8,128)(2,1)} %shard_map.48.quot_ref, bf16[9,896,128]{2,1,0:T(8,128)(2,1)} %bitcast.26, f32[64,128]{1,0:T(8,128)} %broadcast_in_dim.30.cover_ref, f32[16,128,128]{2,1,0:T(8,128)} %est_ref.1), custom_call_target="tpu_custom_call" | custom-call | tf_op jit(solution)/shard_map/pallas_call | solution.py:181
  84.9 2.3 %copy.21 = f32[16,128,128]{2,1,0:T(8,128)} copy(f32[16,128,128]{2,1,0:T(8,128)} %shard_map.49) | data formatting | bytes 2097152
  (8 shorter events, 0.1 us)
Async XLA Ops:
  3.2 2.0 %copy-start = (f32[16,128,128]{2,1,0:T(8,128)S(1)}, f32[16,128,128]{2,1,0:T(8,128)}, u32[]{:S(2)}) copy-start(f32[16,128,128]{2,1,0:T(8,128)} %est_ref.1) | copy-start | bytes 3145732
  5.1 11.3 %copy-start.2 = (s32[8,1,4]{0,2,1:T(4,128)S(1)}, s32[8,1,4]{0,2,1:T(4,128)}, u32[]{:S(2)}) copy-start(s32[8,1,4]{0,2,1:T(4,128)} %param.7) | copy-start | bytes 388
  16.8 9.0 %copy-start.1 = (bf16[1,16,64,128]{3,2,1,0:T(8,128)(2,1)S(1)}, bf16[1,16,64,128]{3,2,1,0:T(8,128)(2,1)}, u32[]{:S(2)}) copy-start(bf16[1,16,64,128]{3,2,1,0:T(8,128)(2,1)} %param.5) | copy-start | bytes 786436
  27.1 5.2 %collective-permute-start = (bf16[16,3,128]{2,1,0:T(4,128)(2,1)S(1)}, bf16[16,3,128]{2,1,0:T(4,128)(2,1)S(1)}, u32[]{:S(2)}, u32[]{:S(2)}) collective-permute-start(bf16[16,3,128]{2,1,0:T(4,128)(2,1)S(1)} %slice_select_fusion), channel_id=1, source_target_pairs={{0,16},{16,0},{32,48},{48,32},{64,80},{80,64},{96,112},{112,96},{1... | collective-permute-start | bytes 36872 | tf_op jit(solution)/shard_map/ppermute | solution.py:37

commit v9 on v7

--- a/solution.py
+++ b/solution.py
@@ -196,8 +196,8 @@
     )(quotient_rimmed, banded, cover_plane, estimate)
 
 
-def band_table(kernel, depth):
-    taps_x, taps_y, taps_z = kernel.shape
+def band_tables(kernels, depth):
+    count, taps_x, taps_y, taps_z = kernels.shape
     rim_z = (taps_z - 1) // 2
     shape_three = (taps_z, depth, depth)
     offset = lax.broadcasted_iota(jnp.int32, shape_three, 1) - lax.broadcasted_iota(
@@ -206,10 +206,12 @@
     onehot = (offset + rim_z == lax.broadcasted_iota(jnp.int32, shape_three, 0)).astype(
         jnp.bfloat16
     )
-    banded = jnp.einsum("abt,tpz->abpz", kernel, onehot, preferred_element_type=jnp.float32).astype(
-        jnp.bfloat16
-    )
-    return banded.reshape(taps_x, taps_y * depth, depth)
+    banded = jnp.dot(
+        kernels.reshape(count * taps_x * taps_y, taps_z),
+        onehot.reshape(taps_z, depth * depth),
+        preferred_element_type=jnp.float32,
+    ).astype(jnp.bfloat16)
+    return banded.reshape(count, taps_x, taps_y * depth, depth)
 
 
 def conv_kernel(tile_x, src_ref, band_ref, out_ref, cols_ref):
@@ -253,10 +255,10 @@
     source = estimate.astype(jnp.bfloat16)
     rimmed = with_halo(source, (("blk", 0),), rim_x)
     padded = jnp.pad(rimmed, ((0, 0), (rim_y, rim_y), (0, 0)))
-    spread = lax.dynamic_index_in_dim(point_spread, view_id, 0, keepdims=False)
-    kernel = (spread / jnp.sum(spread)).astype(jnp.bfloat16)
-    forward = band_table(kernel, depth)
-    backward = band_table(kernel[::-1, ::-1, ::-1], depth)
+    flat = point_spread.reshape(view_count, taps_x * taps_y * taps_z)
+    spread = lax.dynamic_index_in_dim(flat, view_id, 0, keepdims=False)
+    kernel = (spread / jnp.sum(spread)).astype(jnp.bfloat16).reshape(taps_x, taps_y, taps_z)
+    forward, backward = band_tables(jnp.stack([kernel, kernel[::-1, ::-1, ::-1]]), depth)
     coverage_row = lax.dynamic_index_in_dim(covered[:, 0, :], view_id, 0, keepdims=False) > 0
     share_cover = lax.dynamic_slice_in_dim(coverage_row, part * share_blocks, share_blocks)
     cell_cover = jnp.repeat(share_cover, BY)[None, :, None]

time: 82.5 us -> 87.4 us (1.059)
  local copies, waits for them, and re-layouts: 7.24 us -> 13.3 us
  matrix products: 2.41 us -> 1.24 us
  waiting for transfers between devices: 2.36 us -> 3.4 us
    another operation x0 -> x3, local copies, waits for them, and re-layouts: none -> 8.83 us  [local(): forward, backward = band_tables(jnp.stack([kernel, kernel[::-1, ::-1, ::-...]
    convert_element_type x2, local copies, waits for them, and re-layouts: 3.85 us -> 0.3 us  [local(): (spread / jnp.sum(spread)).astype(jnp.bfloat16)]
    dot_general x2 -> x1, matrix products: 2.41 us -> 1.24 us  [band_tables(): jnp.dot(kernels.reshape(count * taps_x * taps_y, taps_z), onehot.reshape(...]
    reduce_sum x1, other arithmetic: 1.7 us -> 0.62 us  [local(): jnp.sum(spread)]
    ppermute x2, starting transfers between devices: 7.44 us -> 8.35 us  [with_halo(): lax.ppermute(tail, axis, [(i, (i + 1) % count) for i in range(ends)])]
    unnamed x5 -> x10, local copies, waits for them, and re-layouts: 2.31 us -> 2.91 us
  transfers between devices with their start and end apart: 5 -> 5, of which waited for: 1 -> 2; matrix products, arithmetic and copies ran while one was open for 11% -> 15% of each run, Pallas kernels for 0% -> 0%
where the time goes in v9:
time: 87.4 us; the launch traced here: 86.7 us
  Pallas kernels  48.4 us (55%)
  starting transfers between devices  13.9 us (16%)
  local copies, waits for them, and re-layouts  13.3 us (15%)
  other arithmetic  6.26 us (7%)
  waiting for transfers between devices  3.4 us (4%)
  matrix products  1.24 us (1%)
    pallas_call x1, Pallas kernels, product_gather(): pl.pallas_call(functools.partial(product_kernel, n, shares), out_shape=ja...  41.3 us
    another operation x3, local copies, waits for them, and re-layouts, local(): forward, backward = band_tables(jnp.stack([kernel, kernel[::-1, ::-1, ::-...  8.83 us
    ppermute x2, starting transfers between devices, with_halo(): lax.ppermute(tail, axis, [(i, (i + 1) % count) for i in range(ends)])  8.35 us
    pallas_call x1, Pallas kernels, convolve(): pl.pallas_call(functools.partial(conv_kernel, 4), out_shape=jax.ShapeDtyp...  7.07 us
    ppermute x2, starting transfers between devices, with_halo(): lax.ppermute(head, axis, [((i + 1) % count, i) for i in range(ends)])  4.26 us
    unnamed x10, local copies, waits for them, and re-layouts  2.91 us
    ppermute x2, waiting for transfers between devices, with_halo(): lax.ppermute(head, axis, [((i + 1) % count, i) for i in range(ends)])  2.56 us
    concatenate x2, other arithmetic, with_halo(): jnp.concatenate([lax.ppermute(tail, axis, [(i, (i + 1) % count) for i in...  1.97 us
  transfers between devices with their start and end apart: 5, of which 2 were waited for; matrix products, arithmetic and copies ran while one was open for 15% of the time, Pallas kernels for 0%

profile of v9, /device:TPU:71, one launch (start us, length us, event | category | flops | bytes accessed | tf_op | source)
XLA Modules:
  0.0 86.7 jit_solution(4477739637155122349)
XLA Ops:
  0.0 1.4 %convert_element_type.45 = bf16[16,128,128]{2,1,0:T(8,128)(2,1)S(1)} convert(f32[16,128,128]{2,1,0:T(8,128)} %est_ref.1) | non-fusion elementwise | flops 262144 | bytes 1572864 | tf_op jit(solution)/shard_map/convert_element_type | solution.py:255
  1.4 3.1 %collective-permute-start = (bf16[4,128,128]{2,1,0:T(8,128)(2,1)S(1)}, bf16[4,128,128]{2,1,0:T(8,128)(2,1)S(1)}, u32[]{:S(2)}, u32[]{:S(2)}) collective-permute-start(bf16[4,128,128]{2,1,0:T(8,128)(2,1)S(1)} %get-tuple-element.8), channel_id=1, source_target_pairs={{0,1},{1,2},{2,3},{3,4},{4,5},{5,6},{6,7},{7,8},{8,9},{9,10},{10,1... | collective-permute-start | bytes 393224 | tf_op jit(solution)/shard_map/ppermute | solution.py:21
  4.5 2.2 %collective-permute-start.1 = (bf16[4,128,128]{2,1,0:T(8,128)(2,1)S(1)}, bf16[4,128,128]{2,1,0:T(8,128)(2,1)S(1)}, u32[]{:S(2)}, u32[]{:S(2)}) collective-permute-start(bf16[4,128,128]{2,1,0:T(8,128)(2,1)S(1)} %get-tuple-element.7), channel_id=1, source_target_pairs={{1,0},{2,1},{3,2},{4,3},{5,4},{6,5},{7,6},{8,7},{9,8},{10,9},{11,1... | collective-permute-start | bytes 393224 | tf_op jit(solution)/shard_map/ppermute | solution.py:23
  6.9 0.6 dynamic-slice_reduce_fusion
  7.5 0.7 convert_reduce_fusion
  8.4 0.1 convert_element_type.47
  8.7 0.2 iota_compare_fusion
  9.0 0.5 copy.6
  9.5 1.2 %convolution_convert_fusion = bf16[126,16384]{1,0:T(8,128)(2,1)S(1)} fusion(bf16[126,25]{1,0:T(8,128)(2,1)S(1)} %reshape.87, pred[25,16384]{1,0:T(8,128)(4,1)S(1)} %bitcast.9), kind=kOutput, calls=%fused_computation | convolution fusion | flops 105283584 | bytes 4544668 | tf_op jit(solution)/shard_map/dot_general | solution.py:209
  10.7 1.9 %fusion.10 = (bf16[63,16384]{1,0:T(8,128)(2,1)S(1)}, bf16[63,16384]{1,0:T(8,128)(2,1)}) fusion(bf16[126,16384]{1,0:T(8,128)(2,1)S(1)} %convolution_convert_fusion), kind=kLoop, calls=%fused_computation.30 | loop fusion | bytes 8257536 | tf_op jit(solution)/shard_map/unstack | solution.py:261
  12.6 4.4 %unstack.13.band_ref = bf16[9,896,128]{2,1,0:T(8,128)(2,1)} reshape(bf16[63,16384]{1,0:T(8,128)(2,1)} %get-tuple-element.6) | data formatting | bytes 4128768 | tf_op jit(solution)/shard_map/unstack | solution.py:261
  17.4 1.1 %fusion.7.src_ref = bf16[24,70,128]{2,1,0:T(8,128)(2,1)} fusion(s32[]{:T(128)S(6)} %select_n.53, bf16[4,128,128]{2,1,0:T(8,128)(2,1)S(1)} %collective-permute-done, bf16[16,128,128]{2,1,0:T(8,128)(2,1)S(1)} %convert_element_type.45, bf16[4,128,128]{2,1,0:T(8,128)(2,1)S(1)} %collective-permute-done.1), kind=kLoop, calls=%fused_computation.14 | loop fusion | flops 2795520 | bytes 1217536 | tf_op jit(solution)/shard_map/concatenate | solution.py:19
  18.5 7.1 %shard_map.46 = f32[16,64,128]{2,1,0:T(8,128)} custom-call(bf16[24,70,128]{2,1,0:T(8,128)(2,1)} %fusion.7.src_ref, bf16[9,896,128]{2,1,0:T(8,128)(2,1)} %unstack.13.band_ref), custom_call_target="tpu_custom_call" | custom-call | tf_op jit(solution)/shard_map/pallas_call | solution.py:235
  25.6 1.2 %fusion.4 = bf16[16,64,128]{2,1,0:T(8,128)(2,1)S(1)} fusion(f32[16,64,128]{2,1,0:T(8,128)} %shard_map.46, bf16[1,16,64,128]{3,2,1,0:T(8,128)(2,1)S(1)} %copy-done, pred[64]{0:T(512)(128)(4,1)S(1)} %broadcast_in_dim.26), kind=kLoop, calls=%fused_computation.11 | loop fusion | flops 524288 | bytes 1048640 | tf_op jit(solution)/shard_map/convert_element_type | solution.py:270
  26.9 1.3 %collective-permute-start.2 = (bf16[16,3,128]{2,1,0:T(4,128)(2,1)S(1)}, bf16[16,3,128]{2,1,0:T(4,128)(2,1)S(1)}, u32[]{:S(2)}, u32[]{:S(2)}) collective-permute-start(bf16[16,3,128]{2,1,0:T(4,128)(2,1)S(1)} %slice_select_fusion), channel_id=1, source_target_pairs={{0,16},{16,0},{32,48},{48,32},{64,80},{80,64},{96,112},{112,96},{1... | collective-permute-start | bytes 36872 | tf_op jit(solution)/shard_map/ppermute | solution.py:37
  28.2 0.8 collective-permute-done.2
  29.1 5.2 %collective-permute-start.3 = (bf16[4,70,128]{2,1,0:T(8,128)(2,1)S(1)}, bf16[4,70,128]{2,1,0:T(8,128)(2,1)S(1)}, u32[]{:S(2)}, u32[]{:S(2)}) collective-permute-start(bf16[4,70,128]{2,1,0:T(8,128)(2,1)S(1)} %get-tuple-element.9), channel_id=1, source_target_pairs={{0,1},{1,2},{2,3},{3,4},{4,5},{5,6},{6,7},{7,8},{8,9},{9,10},{10,1... | collective-permute-start | bytes 215048 | tf_op jit(solution)/shard_map/ppermute | solution.py:21
  34.3 2.1 %collective-permute-start.4 = (bf16[4,70,128]{2,1,0:T(8,128)(2,1)S(1)}, bf16[4,70,128]{2,1,0:T(8,128)(2,1)S(1)}, u32[]{:S(2)}, u32[]{:S(2)}) collective-permute-start(bf16[4,70,128]{2,1,0:T(8,128)(2,1)S(1)} %get-tuple-element.10), channel_id=1, source_target_pairs={{1,0},{2,1},{3,2},{4,3},{5,4},{6,5},{7,6},{8,7},{9,8},{10,9},{11,1... | collective-permute-start | bytes 215048 | tf_op jit(solution)/shard_map/ppermute | solution.py:23
  36.5 2.5 %unstack.15.band_ref = bf16[9,896,128]{2,1,0:T(8,128)(2,1)} reshape(bf16[63,16384]{1,0:T(8,128)(2,1)S(1)} %get-tuple-element.5) | data formatting | bytes 4128768 | tf_op jit(solution)/shard_map/unstack | solution.py:261
  39.0 2.6 %collective-permute-done.4 = bf16[4,70,128]{2,1,0:T(8,128)(2,1)S(1)} collective-permute-done((bf16[4,70,128]{2,1,0:T(8,128)(2,1)S(1)}, bf16[4,70,128]{2,1,0:T(8,128)(2,1)S(1)}, u32[]{:S(2)}, u32[]{:S(2)}) %collective-permute-start.4) | collective-permute-done | bytes 71712 | tf_op jit(solution)/shard_map/ppermute | solution.py:23
  41.5 0.9 pad_maximum_fusion.quot_ref
  42.4 0.7 broadcast_in_dim.30.cover_ref
  43.1 41.3 %shard_map.47 = f32[16,128,128]{2,1,0:T(8,128)} custom-call(bf16[24,70,128]{2,1,0:T(8,128)(2,1)} %pad_maximum_fusion.quot_ref, bf16[9,896,128]{2,1,0:T(8,128)(2,1)} %unstack.15.band_ref, f32[64,128]{1,0:T(8,128)} %broadcast_in_dim.30.cover_ref, f32[16,128,128]{2,1,0:T(8,128)} %est_ref.1), custom_call_target="tpu_custom_call" | custom-call | tf_op jit(solution)/shard_map/pallas_call | solution.py:181
  84.4 2.3 %copy.8 = f32[16,128,128]{2,1,0:T(8,128)} copy(f32[16,128,128]{2,1,0:T(8,128)} %shard_map.47) | data formatting | bytes 2097152
  (26 shorter events, 1.1 us)
Async XLA Ops:
  0.0 6.7 %copy-start.1 = (f32[8,9,7,25]{3,0,2,1:T(8,128)S(1)}, f32[8,9,7,25]{3,0,2,1:T(8,128)}, u32[]{:S(2)}) copy-start(f32[8,9,7,25]{3,0,2,1:T(8,128)} %param.6) | copy-start | bytes 151204
  1.4 16.0 %collective-permute-start = (bf16[4,128,128]{2,1,0:T(8,128)(2,1)S(1)}, bf16[4,128,128]{2,1,0:T(8,128)(2,1)S(1)}, u32[]{:S(2)}, u32[]{:S(2)}) collective-permute-start(bf16[4,128,128]{2,1,0:T(8,128)(2,1)S(1)} %get-tuple-element.8), channel_id=1, source_target_pairs={{0,1},{1,2},{2,3},{3,4},{4,5},{5,6},{6,7},{7,8},{8,9},{9,10},{10,1... | collective-permute-start | bytes 393224 | tf_op jit(solution)/shard_map/ppermute | solution.py:21
  4.5 12.9 %collective-permute-start.1 = (bf16[4,128,128]{2,1,0:T(8,128)(2,1)S(1)}, bf16[4,128,128]{2,1,0:T(8,128)(2,1)S(1)}, u32[]{:S(2)}, u32[]{:S(2)}) collective-permute-start(bf16[4,128,128]{2,1,0:T(8,128)(2,1)S(1)} %get-tuple-element.7), channel_id=1, source_target_pairs={{1,0},{2,1},{3,2},{4,3},{5,4},{6,5},{7,6},{8,7},{9,8},{10,9},{11,1... | collective-permute-start | bytes 393224 | tf_op jit(solution)/shard_map/ppermute | solution.py:23
  12.6 4.5 %copy-start.2 = (s32[8,1,4]{0,2,1:T(4,128)S(1)}, s32[8,1,4]{0,2,1:T(4,128)}, u32[]{:S(2)}) copy-start(s32[8,1,4]{0,2,1:T(4,128)} %param.7) | copy-start | bytes 388
  17.4 8.2 %copy-start = (bf16[1,16,64,128]{3,2,1,0:T(8,128)(2,1)S(1)}, bf16[1,16,64,128]{3,2,1,0:T(8,128)(2,1)}, u32[]{:S(2)}) copy-start(bf16[1,16,64,128]{3,2,1,0:T(8,128)(2,1)} %param.5) | copy-start | bytes 786436
  26.9 2.2 %collective-permute-start.2 = (bf16[16,3,128]{2,1,0:T(4,128)(2,1)S(1)}, bf16[16,3,128]{2,1,0:T(4,128)(2,1)S(1)}, u32[]{:S(2)}, u32[]{:S(2)}) collective-permute-start(bf16[16,3,128]{2,1,0:T(4,128)(2,1)S(1)} %slice_select_fusion), channel_id=1, source_target_pairs={{0,16},{16,0},{32,48},{48,32},{64,80},{80,64},{96,112},{112,96},{1... | collective-permute-start | bytes 36872 | tf_op jit(solution)/shard_map/ppermute | solution.py:37
  29.1 9.9 %collective-permute-start.3 = (bf16[4,70,128]{2,1,0:T(8,128)(2,1)S(1)}, bf16[4,70,128]{2,1,0:T(8,128)(2,1)S(1)}, u32[]{:S(2)}, u32[]{:S(2)}) collective-permute-start(bf16[4,70,128]{2,1,0:T(8,128)(2,1)S(1)} %get-tuple-element.9), channel_id=1, source_target_pairs={{0,1},{1,2},{2,3},{3,4},{4,5},{5,6},{6,7},{7,8},{8,9},{9,10},{10,1... | collective-permute-start | bytes 215048 | tf_op jit(solution)/shard_map/ppermute | solution.py:21
  34.3 7.2 %collective-permute-start.4 = (bf16[4,70,128]{2,1,0:T(8,128)(2,1)S(1)}, bf16[4,70,128]{2,1,0:T(8,128)(2,1)S(1)}, u32[]{:S(2)}, u32[]{:S(2)}) collective-permute-start(bf16[4,70,128]{2,1,0:T(8,128)(2,1)S(1)} %get-tuple-element.10), channel_id=1, source_target_pairs={{1,0},{2,1},{3,2},{4,3},{5,4},{6,5},{7,6},{8,7},{9,8},{10,9},{11,1... | collective-permute-start | bytes 215048 | tf_op jit(solution)/shard_map/ppermute | solution.py:23

commit v10 on v7

--- a/solution.py
+++ b/solution.py
@@ -212,31 +212,34 @@
     return banded.reshape(taps_x, taps_y * depth, depth)
 
 
-def conv_kernel(tile_x, src_ref, band_ref, out_ref, cols_ref):
+def conv_kernel(tile_x, src_ref, band_ref, image_ref, cover_ref, out_ref, cols_ref):
     rows_x, rows_y, depth = out_ref.shape
     taps_x = src_ref.shape[0] - rows_x + 1
     taps_y = src_ref.shape[1] - rows_y + 1
     for step_y in range(taps_y):
         cols_ref[:, :, step_y * depth : (step_y + 1) * depth] = src_ref[:, step_y : step_y + rows_y, :]
+    keep = cover_ref[...] > 0
     for start in range(0, rows_x, tile_x):
         acc = None
         for shift_x in range(taps_x):
             lhs = cols_ref[start + shift_x : start + shift_x + tile_x].reshape(tile_x * rows_y, -1)
             part = jnp.dot(lhs, band_ref[shift_x], preferred_element_type=jnp.float32)
             acc = part if acc is None else acc + part
-        out_ref[start : start + tile_x] = acc.reshape(tile_x, rows_y, depth)
-
-
-def convolve(padded_part, banded, rows_x, rows_y):
-    depth = padded_part.shape[2]
+        blurred = acc.reshape(tile_x, rows_y, depth)
+        ratio = image_ref[start : start + tile_x].astype(jnp.float32) / blurred
+        out_ref[start : start + tile_x] = jnp.where(keep[None], ratio, 0.0).astype(out_ref.dtype)
+
+
+def quotient_of(padded_part, banded, image, cover_plane):
+    rows_x, rows_y, depth = image.shape
     vmem = pl.BlockSpec(memory_space=pltpu.VMEM)
     return pl.pallas_call(
         functools.partial(conv_kernel, 4),
-        out_shape=jax.ShapeDtypeStruct((rows_x, rows_y, depth), jnp.float32),
-        in_specs=[vmem, vmem],
+        out_shape=jax.ShapeDtypeStruct((rows_x, rows_y, depth), jnp.bfloat16),
+        in_specs=[vmem] * 4,
         out_specs=vmem,
         scratch_shapes=[pltpu.VMEM((padded_part.shape[0], rows_y, banded.shape[1]), jnp.bfloat16)],
-    )(padded_part, banded)
+    )(padded_part, banded, image, cover_plane)
 
 
 def local(estimate, images, point_spread, covered):
@@ -264,8 +267,8 @@
     region = lax.dynamic_slice(
         padded, (0, y_start, 0), (slab_x + 2 * rim_x, share_w + 2 * rim_y, depth)
     )
-    blurred = convolve(region, forward, slab_x, share_w)
-    quotient = jnp.where(cell_cover, image.astype(jnp.float32) / blurred, 0.0).astype(jnp.bfloat16)
+    cover_plane = jnp.broadcast_to(cell_cover[0].astype(jnp.float32), (share_w, depth))
+    quotient = quotient_of(region, forward, image, cover_plane)
     rim_zeros = jnp.zeros((slab_x, rim_y, depth), jnp.bfloat16)
     edge_rows = jnp.where(part == 0, quotient[:, share_w - rim_y :, :], quotient[:, :rim_y, :])
     partner = swapped(edge_rows, "view", 0)
@@ -273,7 +276,6 @@
     upper_rim = jnp.where(part < shares - 1, partner, rim_zeros)
     extended = jnp.concatenate([lower_rim, quotient, upper_rim], axis=1)
     quotient_rimmed = with_halo(extended, (("blk", 0),), rim_x)
-    cover_plane = jnp.broadcast_to(cell_cover[0].astype(jnp.float32), (share_w, depth))
     return product_gather(quotient_rimmed, backward, cover_plane, estimate, shares)
 
 

time: 82.5 us -> 82.9 us (level)
    convert_element_type x1 -> x0, other arithmetic: 1.21 us -> none  [local(): jnp.where(cell_cover, image.astype(jnp.float32) / blurred, 0.0)]
    slice x1, other arithmetic: 0.05 us -> 0.93 us  [with_halo(): lax.slice_in_dim(cells, cells.shape[dim] - width, cells.shape[dim], axis=...]
  transfers between devices with their start and end apart: 5 -> 5, of which waited for: 1 -> 2; matrix products, arithmetic and copies ran while one was open for 11% -> 11% of each run, Pallas kernels for 0% -> 0%
where the time goes in v10:
time: 82.9 us; the launch traced here: 81.8 us
  Pallas kernels  48.3 us (58%)
  starting transfers between devices  13.9 us (17%)
  other arithmetic  7.58 us (9%)
  local copies, waits for them, and re-layouts  7.12 us (9%)
  matrix products  2.4 us (3%)
  waiting for transfers between devices  2.4 us (3%)
    pallas_call x1, Pallas kernels, product_gather(): pl.pallas_call(functools.partial(product_kernel, n, shares), out_shape=ja...  41.4 us
    ppermute x2, starting transfers between devices, with_halo(): lax.ppermute(tail, axis, [(i, (i + 1) % count) for i in range(ends)])  7.41 us
    pallas_call x1, Pallas kernels, quotient_of(): pl.pallas_call(functools.partial(conv_kernel, 4), out_shape=jax.ShapeDtyp...  6.98 us
    ppermute x2, starting transfers between devices, with_halo(): lax.ppermute(head, axis, [((i + 1) % count, i) for i in range(ends)])  4.26 us
    convert_element_type x2, local copies, waits for them, and re-layouts, band_table(): jnp.einsum('abt,tpz->abpz', kernel, onehot, preferred_element_type=jnp.fl...  3.85 us
    dot_general x2, matrix products, band_table(): jnp.einsum('abt,tpz->abpz', kernel, onehot, preferred_element_type=jnp.fl...  2.4 us
    ppermute x2, waiting for transfers between devices, with_halo(): lax.ppermute(head, axis, [((i + 1) % count, i) for i in range(ends)])  2.37 us
    unnamed x5, local copies, waits for them, and re-layouts  2.31 us
  transfers between devices with their start and end apart: 5, of which 2 were waited for; matrix products, arithmetic and copies ran while one was open for 11% of the time, Pallas kernels for 0%

profile of v10, /device:TPU:71, one launch (start us, length us, event | category | flops | bytes accessed | tf_op | source)
XLA Modules:
  0.0 81.8 jit_solution(16598162670110091145)
XLA Ops:
  0.0 1.3 %convert_element_type.34 = bf16[16,128,128]{2,1,0:T(8,128)(2,1)S(1)} convert(f32[16,128,128]{2,1,0:T(8,128)} %est_ref.1) | non-fusion elementwise | flops 262144 | bytes 1572864 | tf_op jit(solution)/shard_map/convert_element_type | solution.py:256
  1.3 3.1 %collective-permute-start = (bf16[4,128,128]{2,1,0:T(8,128)(2,1)S(1)}, bf16[4,128,128]{2,1,0:T(8,128)(2,1)S(1)}, u32[]{:S(2)}, u32[]{:S(2)}) collective-permute-start(bf16[4,128,128]{2,1,0:T(8,128)(2,1)S(1)} %get-tuple-element.8), channel_id=1, source_target_pairs={{0,1},{1,2},{2,3},{3,4},{4,5},{5,6},{6,7},{7,8},{8,9},{9,10},{10,1... | collective-permute-start | bytes 393224 | tf_op jit(solution)/shard_map/ppermute | solution.py:21
  4.5 2.2 %collective-permute-start.1 = (bf16[4,128,128]{2,1,0:T(8,128)(2,1)S(1)}, bf16[4,128,128]{2,1,0:T(8,128)(2,1)S(1)}, u32[]{:S(2)}, u32[]{:S(2)}) collective-permute-start(bf16[4,128,128]{2,1,0:T(8,128)(2,1)S(1)} %get-tuple-element.7), channel_id=1, source_target_pairs={{1,0},{2,1},{3,2},{4,3},{5,4},{6,5},{7,6},{8,7},{9,8},{10,9},{11,1... | collective-permute-start | bytes 393224 | tf_op jit(solution)/shard_map/ppermute | solution.py:23
  6.7 1.7 %fusion.29 = (f32[]{:T(128)}, f32[1,9,7,25]{3,0,2,1:T(1,128)S(1)}) fusion(f32[8,9,7,25]{3,0,2,1:T(8,128)} %param.6, s32[]{:T(128)S(6)} %select_n.48), kind=kLoop, calls=%fused_computation.38 | loop fusion | flops 1574 | bytes 12608 | tf_op jit(solution)/shard_map/reduce_sum | solution.py:260
  8.4 1.5 %fusion.5 = bf16[9,7,128,128]{3,1,2,0:T(8,128)(2,1)S(1)} fusion(f32[1,9,7,25]{3,0,2,1:T(1,128)S(1)} %get-tuple-element.6, f32[]{:T(128)} %get-tuple-element.5), kind=kOutput, calls=%fused_computation.4 | convolution fusion | flops 53873744 | bytes 2070688 | tf_op jit(solution)/shard_map/abt,tpz->abpz/dot_general | solution.py:209
  9.9 1.9 %copy.6 = bf16[9,7,128,128]{3,2,1,0:T(8,128)(2,1)} copy(bf16[9,7,128,128]{3,1,2,0:T(8,128)(2,1)S(1)} %fusion.5) | data formatting | bytes 4128768 | tf_op jit(solution)/shard_map/convert_element_type | solution.py:209
  11.9 0.1 fusion.24
  12.1 0.1 convert_element_type.40
  12.3 1.1 %fusion.18.src_ref = bf16[24,70,128]{2,1,0:T(8,128)(2,1)} fusion(s32[]{:T(128)S(6)} %select_n.46, bf16[4,128,128]{2,1,0:T(8,128)(2,1)S(1)} %collective-permute-done, bf16[16,128,128]{2,1,0:T(8,128)(2,1)S(1)} %convert_element_type.34, bf16[4,128,128]{2,1,0:T(8,128)(2,1)S(1)} %collective-permute-done.1), kind=kLoop, calls=%fused_computation.17 | loop fusion | flops 2795520 | bytes 1217536 | tf_op jit(solution)/shard_map/concatenate | solution.py:19
  13.4 0.7 broadcast_in_dim.12.cover_ref
  14.1 7.0 %shard_map.46 = bf16[16,64,128]{2,1,0:T(8,128)(2,1)} custom-call(bf16[24,70,128]{2,1,0:T(8,128)(2,1)} %fusion.18.src_ref, bf16[9,896,128]{2,1,0:T(8,128)(2,1)} %bitcast.23, bf16[16,64,128]{2,1,0:T(8,128)(2,1)} %bitcast.25, f32[64,128]{1,0:T(8,128)} %broadcast_in_dim.12.cover_ref), custom_call_target="tpu_custom_call" | custom-call | tf_op jit(solution)/shard_map/pallas_call | solution.py:236
  21.0 0.8 slice_select_fusion
  21.8 2.2 %collective-permute-start.2 = (bf16[16,3,128]{2,1,0:T(4,128)(2,1)S(1)}, bf16[16,3,128]{2,1,0:T(4,128)(2,1)S(1)}, u32[]{:S(2)}, u32[]{:S(2)}) collective-permute-start(bf16[16,3,128]{2,1,0:T(4,128)(2,1)S(1)} %slice_select_fusion), channel_id=1, source_target_pairs={{0,16},{16,0},{32,48},{48,32},{64,80},{80,64},{96,112},{112,96},{1... | collective-permute-start | bytes 36872 | tf_op jit(solution)/shard_map/ppermute | solution.py:37
  24.0 0.7 fusion.28
  24.7 0.1 rev.3
  24.9 0.9 %pad_maximum_fusion.3 = (bf16[4,70,128]{2,1,0:T(8,128)(2,1)S(1)}, bf16[4,70,128]{2,1,0:T(8,128)(2,1)S(1)}) fusion(bf16[16,3,128]{2,1,0:T(4,128)(2,1)S(1)} %get-tuple-element.12, bf16[16,64,128]{2,1,0:T(8,128)(2,1)} %shard_map.46, bf16[16,3,128]{2,1,0:T(4,128)(2,1)S(1)} %get-tuple-element.11), kind=kLoop, calls=%fused_computation.23 | loop fusion | flops 430080 | bytes 430080 | tf_op jit(solution)/shard_map/slice | solution.py:18
  25.8 4.3 %collective-permute-start.3 = (bf16[4,70,128]{2,1,0:T(8,128)(2,1)S(1)}, bf16[4,70,128]{2,1,0:T(8,128)(2,1)S(1)}, u32[]{:S(2)}, u32[]{:S(2)}) collective-permute-start(bf16[4,70,128]{2,1,0:T(8,128)(2,1)S(1)} %get-tuple-element.9), channel_id=1, source_target_pairs={{0,1},{1,2},{2,3},{3,4},{4,5},{5,6},{6,7},{7,8},{8,9},{9,10},{10,1... | collective-permute-start | bytes 215048 | tf_op jit(solution)/shard_map/ppermute | solution.py:21
  30.1 2.1 %collective-permute-start.4 = (bf16[4,70,128]{2,1,0:T(8,128)(2,1)S(1)}, bf16[4,70,128]{2,1,0:T(8,128)(2,1)S(1)}, u32[]{:S(2)}, u32[]{:S(2)}) collective-permute-start(bf16[4,70,128]{2,1,0:T(8,128)(2,1)S(1)} %get-tuple-element.10), channel_id=1, source_target_pairs={{1,0},{2,1},{3,2},{4,3},{5,4},{6,5},{7,6},{8,7},{9,8},{10,9},{11,1... | collective-permute-start | bytes 215048 | tf_op jit(solution)/shard_map/ppermute | solution.py:23
  32.2 0.9 %fusion.8 = bf16[9,7,128,128]{3,1,2,0:T(8,128)(2,1)S(1)} fusion(bf16[9,7,25]{2,1,0:T(8,128)(2,1)S(1)} %rev.3), kind=kOutput, calls=%fused_computation.5 | convolution fusion | flops 53870592 | bytes 2067534 | tf_op jit(solution)/shard_map/abt,tpz->abpz/dot_general | solution.py:209
  33.1 1.9 %copy.7 = bf16[9,7,128,128]{3,2,1,0:T(8,128)(2,1)} copy(bf16[9,7,128,128]{3,1,2,0:T(8,128)(2,1)S(1)} %fusion.8) | data formatting | bytes 4128768 | tf_op jit(solution)/shard_map/convert_element_type | solution.py:209
  35.0 2.3 %collective-permute-done.4 = bf16[4,70,128]{2,1,0:T(8,128)(2,1)S(1)} collective-permute-done((bf16[4,70,128]{2,1,0:T(8,128)(2,1)S(1)}, bf16[4,70,128]{2,1,0:T(8,128)(2,1)S(1)}, u32[]{:S(2)}, u32[]{:S(2)}) %collective-permute-start.4) | collective-permute-done | bytes 71712 | tf_op jit(solution)/shard_map/ppermute | solution.py:23
  37.3 0.9 %pad_maximum_fusion.quot_ref = bf16[24,70,128]{2,1,0:T(8,128)(2,1)} fusion(bf16[4,70,128]{2,1,0:T(8,128)(2,1)S(1)} %collective-permute-done.4, bf16[16,3,128]{2,1,0:T(4,128)(2,1)S(1)} %get-tuple-element.12, bf16[16,64,128]{2,1,0:T(8,128)(2,1)S(1)} %copy-done, bf16[16,3,128]{2,1,0:T(4,128)(2,1)S(1)} %get-tuple-element.11, ...), kind=kLoop, calls=%fused_computation.20 | loop fusion | flops 2150400 | bytes 860160 | tf_op jit(solution)/shard_map/concatenate | solution.py:19
  38.2 41.4 %shard_map.47 = f32[16,128,128]{2,1,0:T(8,128)} custom-call(bf16[24,70,128]{2,1,0:T(8,128)(2,1)} %pad_maximum_fusion.quot_ref, bf16[9,896,128]{2,1,0:T(8,128)(2,1)} %bitcast.24, f32[64,128]{1,0:T(8,128)} %broadcast_in_dim.12.cover_ref, f32[16,128,128]{2,1,0:T(8,128)} %est_ref.1), custom_call_target="tpu_custom_call" | custom-call | tf_op jit(solution)/shard_map/pallas_call | solution.py:181
  79.6 2.3 %copy.21 = f32[16,128,128]{2,1,0:T(8,128)} copy(f32[16,128,128]{2,1,0:T(8,128)} %shard_map.47) | data formatting | bytes 2097152
  (12 shorter events, 0.3 us)
Async XLA Ops:
  1.3 10.9 %collective-permute-start = (bf16[4,128,128]{2,1,0:T(8,128)(2,1)S(1)}, bf16[4,128,128]{2,1,0:T(8,128)(2,1)S(1)}, u32[]{:S(2)}, u32[]{:S(2)}) collective-permute-start(bf16[4,128,128]{2,1,0:T(8,128)(2,1)S(1)} %get-tuple-element.8), channel_id=1, source_target_pairs={{0,1},{1,2},{2,3},{3,4},{4,5},{5,6},{6,7},{7,8},{8,9},{9,10},{10,1... | collective-permute-start | bytes 393224 | tf_op jit(solution)/shard_map/ppermute | solution.py:21
  4.5 7.8 %collective-permute-start.1 = (bf16[4,128,128]{2,1,0:T(8,128)(2,1)S(1)}, bf16[4,128,128]{2,1,0:T(8,128)(2,1)S(1)}, u32[]{:S(2)}, u32[]{:S(2)}) collective-permute-start(bf16[4,128,128]{2,1,0:T(8,128)(2,1)S(1)} %get-tuple-element.7), channel_id=1, source_target_pairs={{1,0},{2,1},{3,2},{4,3},{5,4},{6,5},{7,6},{8,7},{9,8},{10,9},{11,1... | collective-permute-start | bytes 393224 | tf_op jit(solution)/shard_map/ppermute | solution.py:23
  9.9 1.9 %copy-start.1 = (s32[8,1,4]{0,2,1:T(4,128)S(1)}, s32[8,1,4]{0,2,1:T(4,128)}, u32[]{:S(2)}) copy-start(s32[8,1,4]{0,2,1:T(4,128)} %param.7) | copy-start | bytes 388
  21.8 3.0 %collective-permute-start.2 = (bf16[16,3,128]{2,1,0:T(4,128)(2,1)S(1)}, bf16[16,3,128]{2,1,0:T(4,128)(2,1)S(1)}, u32[]{:S(2)}, u32[]{:S(2)}) collective-permute-start(bf16[16,3,128]{2,1,0:T(4,128)(2,1)S(1)} %slice_select_fusion), channel_id=1, source_target_pairs={{0,16},{16,0},{32,48},{48,32},{64,80},{80,64},{96,112},{112,96},{1... | collective-permute-start | bytes 36872 | tf_op jit(solution)/shard_map/ppermute | solution.py:37
  25.8 9.2 %collective-permute-start.3 = (bf16[4,70,128]{2,1,0:T(8,128)(2,1)S(1)}, bf16[4,70,128]{2,1,0:T(8,128)(2,1)S(1)}, u32[]{:S(2)}, u32[]{:S(2)}) collective-permute-start(bf16[4,70,128]{2,1,0:T(8,128)(2,1)S(1)} %get-tuple-element.9), channel_id=1, source_target_pairs={{0,1},{1,2},{2,3},{3,4},{4,5},{5,6},{6,7},{7,8},{8,9},{9,10},{10,1... | collective-permute-start | bytes 215048 | tf_op jit(solution)/shard_map/ppermute | solution.py:21
  30.1 7.2 %collective-permute-start.4 = (bf16[4,70,128]{2,1,0:T(8,128)(2,1)S(1)}, bf16[4,70,128]{2,1,0:T(8,128)(2,1)S(1)}, u32[]{:S(2)}, u32[]{:S(2)}) collective-permute-start(bf16[4,70,128]{2,1,0:T(8,128)(2,1)S(1)} %get-tuple-element.10), channel_id=1, source_target_pairs={{1,0},{2,1},{3,2},{4,3},{5,4},{6,5},{7,6},{8,7},{9,8},{10,9},{11,1... | collective-permute-start | bytes 215048 | tf_op jit(solution)/shard_map/ppermute | solution.py:23
  33.1 4.2 %copy-start = (bf16[16,64,128]{2,1,0:T(8,128)(2,1)S(1)}, bf16[16,64,128]{2,1,0:T(8,128)(2,1)}, u32[]{:S(2)}) copy-start(bf16[16,64,128]{2,1,0:T(8,128)(2,1)} %shard_map.46) | copy-start | bytes 786436

commit v11 on v10

--- a/solution.py
+++ b/solution.py
@@ -49,16 +49,21 @@
 
 
 def product_kernel(
-    n, shares, quot_ref, band_ref, cover_ref, est_ref, out_ref, cols_ref, factor_ref, held,
-    send1, recv1, send2, recv2,
+    n, shares, width, quot_ref, band_ref, cover_ref, est_ref, out_ref, ext_ref, cols_ref, factor_ref,
+    held, send1, recv1, send2, recv2, send_halo, recv_halo,
 ):
     groups = n // shares
     step, share_w, depth = held.shape[1:]
     taps_x = band_ref.shape[0]
     taps_y = quot_ref.shape[1] - share_w + 1
+    rows = quot_ref.shape[0]
     me = lax.axis_index("view")
     view_id = me // shares
     part = me % shares
+    layers = lax.axis_size("blk")
+    layer = lax.axis_index("blk")
+    up = (layer + 1) % layers
+    down = (layer + layers - 1) % layers
     mesh_kind = pl.DeviceIdType.MESH
     barrier = pltpu.get_barrier_semaphore()
     for d in range(1, groups):
@@ -71,8 +76,17 @@
             barrier, inc=1, device_id={"view": view_id * shares + (part + d) % shares},
             device_id_type=mesh_kind,
         )
-    for step_y in range(taps_y):
-        cols_ref[:, :, step_y * depth : (step_y + 1) * depth] = quot_ref[:, step_y : step_y + share_w, :]
+    for other in (up, down):
+        pl.semaphore_signal(barrier, inc=1, device_id={"blk": other}, device_id_type=mesh_kind)
+    ext_ref[pl.ds(width, rows)] = quot_ref[...]
+
+    def build_columns(first, count):
+        for step_y in range(taps_y):
+            cols_ref[pl.ds(first, count), :, step_y * depth : (step_y + 1) * depth] = ext_ref[
+                pl.ds(first, count), step_y : step_y + share_w, :
+            ]
+
+    build_columns(width, rows)
     keep = cover_ref[...] > 0
 
     def factor_rows(target):
@@ -84,45 +98,91 @@
         acc = acc.reshape(step, share_w, depth)
         factor_ref[pl.ds(target * step, step)] = jnp.where(keep[None], acc, 1.0)
 
-    factor_rows(view_id)
-    pl.semaphore_wait(barrier, groups + shares - 2)
+    pl.semaphore_wait(barrier, groups + shares)
+    to_up = pltpu.make_async_remote_copy(
+        src_ref=quot_ref.at[pl.ds(rows - width, width)],
+        dst_ref=ext_ref.at[pl.ds(0, width)],
+        send_sem=send_halo.at[0],
+        recv_sem=recv_halo.at[0],
+        device_id={"blk": up},
+        device_id_type=mesh_kind,
+    )
+    to_down = pltpu.make_async_remote_copy(
+        src_ref=quot_ref.at[pl.ds(0, width)],
+        dst_ref=ext_ref.at[pl.ds(rows + width, width)],
+        send_sem=send_halo.at[1],
+        recv_sem=recv_halo.at[1],
+        device_id={"blk": down},
+        device_id_type=mesh_kind,
+    )
+    to_up.start()
+    to_down.start()
+    reach = width // step
+    inner = list(range(reach, groups - reach))
+    outer = list(range(reach)) + list(range(groups - reach, groups))
     outgoing = []
-    for d in range(1, groups):
-        target = (view_id + d) % groups
+
+    def send_chunk(target):
         factor_rows(target)
         copy = pltpu.make_async_remote_copy(
             src_ref=factor_ref.at[pl.ds(target * step, step)],
             dst_ref=held.at[view_id],
-            send_sem=send1.at[d],
-            recv_sem=recv1.at[d],
+            send_sem=send1.at[target],
+            recv_sem=recv1.at[view_id],
             device_id={"view": target * shares + part},
             device_id_type=mesh_kind,
         )
-        copy.start()
-        outgoing.append(copy)
+
+        @pl.when(target != view_id)
+        def _():
+            copy.start()
+
+        outgoing.append((target, copy))
+
+    for target in inner:
+        send_chunk(target)
+    to_up.wait()
+    to_down.wait()
+
+    @pl.when(layer == 0)
+    def _():
+        ext_ref[pl.ds(0, width)] = jnp.zeros((width,) + quot_ref.shape[1:], quot_ref.dtype)
+
+    @pl.when(layer == layers - 1)
+    def _():
+        ext_ref[pl.ds(rows + width, width)] = jnp.zeros((width,) + quot_ref.shape[1:], quot_ref.dtype)
+
+    build_columns(0, width)
+    build_columns(rows + width, width)
+    for target in outer:
+        send_chunk(target)
     acc = factor_ref[pl.ds(view_id * step, step)]
     for d in range(1, groups):
         source = (view_id - d + groups) % groups
         pltpu.make_async_remote_copy(
             src_ref=factor_ref.at[pl.ds(0, step)],
             dst_ref=held.at[source],
-            send_sem=send1.at[d],
-            recv_sem=recv1.at[d],
+            send_sem=send1.at[source],
+            recv_sem=recv1.at[source],
             device_id={"view": source * shares + part},
             device_id_type=mesh_kind,
         ).wait_recv()
         acc = acc * held[source]
-    for copy in outgoing:
-        copy.wait_send()
-    rows = pl.ds(view_id * step, step)
+    for target, copy in outgoing:
+
+        @pl.when(target != view_id)
+        def _():
+            copy.wait_send()
+
+    mine = pl.ds(view_id * step, step)
     cols = pl.ds(part * share_w, share_w)
-    out_ref[rows, cols, :] = acc * est_ref[rows, cols, :]
+    out_ref[mine, cols, :] = acc * est_ref[mine, cols, :]
     outgoing = []
     for d in range(1, groups):
         target = (view_id + d) % groups
         copy = pltpu.make_async_remote_copy(
-            src_ref=out_ref.at[rows, cols],
-            dst_ref=out_ref.at[rows, cols],
+            src_ref=out_ref.at[mine, cols],
+            dst_ref=out_ref.at[mine, cols],
             send_sem=send2.at[d],
             recv_sem=recv2.at[d],
             device_id={"view": target * shares + part},
@@ -171,29 +231,33 @@
         copy.wait_send()
 
 
-def product_gather(quotient_rimmed, banded, cover_plane, estimate, shares):
+def product_gather(extended, banded, cover_plane, estimate, shares, width):
     n = lax.axis_size("view")
     groups = n // shares
     slab_x, width_y, depth = estimate.shape
     share_w = cover_plane.shape[0]
     step = slab_x // groups
+    padded_rows = extended.shape[0] + 2 * width
     vmem = pl.BlockSpec(memory_space=pltpu.VMEM)
     return pl.pallas_call(
-        functools.partial(product_kernel, n, shares),
+        functools.partial(product_kernel, n, shares, width),
         out_shape=jax.ShapeDtypeStruct(estimate.shape, jnp.float32),
         in_specs=[vmem] * 4,
         out_specs=vmem,
         scratch_shapes=[
-            pltpu.VMEM((quotient_rimmed.shape[0], share_w, banded.shape[1]), jnp.bfloat16),
+            pltpu.VMEM((padded_rows,) + extended.shape[1:], extended.dtype),
+            pltpu.VMEM((padded_rows, share_w, banded.shape[1]), jnp.bfloat16),
             pltpu.VMEM((slab_x, share_w, depth), jnp.float32),
             pltpu.VMEM((groups, step, share_w, depth), jnp.float32),
             pltpu.SemaphoreType.DMA((groups,)),
             pltpu.SemaphoreType.DMA((groups,)),
             pltpu.SemaphoreType.DMA((groups + shares,)),
             pltpu.SemaphoreType.DMA((groups + shares,)),
+            pltpu.SemaphoreType.DMA((2,)),
+            pltpu.SemaphoreType.DMA((2,)),
         ],
         compiler_params=pltpu.CompilerParams(collective_id=0, has_side_effects=True),
-    )(quotient_rimmed, banded, cover_plane, estimate)
+    )(extended, banded, cover_plane, estimate)
 
 
 def band_table(kernel, depth):
@@ -275,8 +339,7 @@
     lower_rim = jnp.where(part > 0, partner, rim_zeros)
     upper_rim = jnp.where(part < shares - 1, partner, rim_zeros)
     extended = jnp.concatenate([lower_rim, quotient, upper_rim], axis=1)
-    quotient_rimmed = with_halo(extended, (("blk", 0),), rim_x)
-    return product_gather(quotient_rimmed, backward, cover_plane, estimate, shares)
+    return product_gather(extended, backward, cover_plane, estimate, shares, rim_x)
 
 
 def solution(mesh):

time: 82.9 us -> 80.6 us (0.972)
  the two profiles are of different devices: /device:TPU:71 before, /device:TPU:1 now
where the time goes in v11:
time: 80.6 us; the launch traced here: 80.2 us
  Pallas kernels  57.6 us (71%)
  local copies, waits for them, and re-layouts  7.15 us (9%)
  other arithmetic  6.5 us (8%)
  starting transfers between devices  6.47 us (8%)
  matrix products  2.37 us (3%)
    pallas_call x1, Pallas kernels, product_gather(): pl.pallas_call(functools.partial(product_kernel, n, shares, width), out_s...  50.6 us
    pallas_call x1, Pallas kernels, quotient_of(): pl.pallas_call(functools.partial(conv_kernel, 4), out_shape=jax.ShapeDtyp...  7 us
    ppermute x1, starting transfers between devices, with_halo(): lax.ppermute(tail, axis, [(i, (i + 1) % count) for i in range(ends)])  3.95 us
    convert_element_type x2, local copies, waits for them, and re-layouts, band_table(): jnp.einsum('abt,tpz->abpz', kernel, onehot, preferred_element_type=jnp.fl...  3.88 us
    dot_general x2, matrix products, band_table(): jnp.einsum('abt,tpz->abpz', kernel, onehot, preferred_element_type=jnp.fl...  2.37 us
    unnamed x5, local copies, waits for them, and re-layouts  2.31 us
    reduce_sum x1, other arithmetic, local(): kernel = (spread / jnp.sum(spread)).astype(jnp.bfloat16)  1.63 us
  transfers between devices with their start and end apart: 3, of which 0 were waited for; matrix products, arithmetic and copies ran while one was open for 11% of the time, Pallas kernels for 0%

profile of v11, /device:TPU:1, one launch (start us, length us, event | category | flops | bytes accessed | tf_op | source)
XLA Modules:
  0.0 80.2 jit_solution(12864619277830322821)
XLA Ops:
  0.0 1.3 %convert_element_type.34 = bf16[16,128,128]{2,1,0:T(8,128)(2,1)S(1)} convert(f32[16,128,128]{2,1,0:T(8,128)} %est_ref.1) | non-fusion elementwise | flops 262144 | bytes 1572864 | tf_op jit(solution)/shard_map/convert_element_type | solution.py:320
  1.3 4.0 %collective-permute-start = (bf16[4,128,128]{2,1,0:T(8,128)(2,1)S(1)}, bf16[4,128,128]{2,1,0:T(8,128)(2,1)S(1)}, u32[]{:S(2)}, u32[]{:S(2)}) collective-permute-start(bf16[4,128,128]{2,1,0:T(8,128)(2,1)S(1)} %get-tuple-element.8), channel_id=1, source_target_pairs={{0,1},{1,2},{2,3},{3,4},{4,5},{5,6},{6,7},{7,8},{8,9},{9,10},{10,1... | collective-permute-start | bytes 393224 | tf_op jit(solution)/shard_map/ppermute | solution.py:21
  5.3 1.3 %collective-permute-start.1 = (bf16[4,128,128]{2,1,0:T(8,128)(2,1)S(1)}, bf16[4,128,128]{2,1,0:T(8,128)(2,1)S(1)}, u32[]{:S(2)}, u32[]{:S(2)}) collective-permute-start(bf16[4,128,128]{2,1,0:T(8,128)(2,1)S(1)} %get-tuple-element.7), channel_id=1, source_target_pairs={{1,0},{2,1},{3,2},{4,3},{5,4},{6,5},{7,6},{8,7},{9,8},{10,9},{11,1... | collective-permute-start | bytes 393224 | tf_op jit(solution)/shard_map/ppermute | solution.py:23
  6.6 1.6 %fusion.29 = (f32[]{:T(128)}, f32[1,9,7,25]{3,0,2,1:T(1,128)S(1)}) fusion(f32[8,9,7,25]{3,0,2,1:T(8,128)} %param.6, s32[]{:T(128)S(6)} %select_n.48), kind=kLoop, calls=%fused_computation.35 | loop fusion | flops 1574 | bytes 12608 | tf_op jit(solution)/shard_map/reduce_sum | solution.py:324
  8.3 1.5 %fusion.5 = bf16[9,7,128,128]{3,1,2,0:T(8,128)(2,1)S(1)} fusion(f32[1,9,7,25]{3,0,2,1:T(1,128)S(1)} %get-tuple-element.6, f32[]{:T(128)} %get-tuple-element.5), kind=kOutput, calls=%fused_computation.4 | convolution fusion | flops 53873744 | bytes 2070688 | tf_op jit(solution)/shard_map/abt,tpz->abpz/dot_general | solution.py:273
  9.8 0.0 copy-start.1
  9.8 1.9 %copy.6 = bf16[9,7,128,128]{3,2,1,0:T(8,128)(2,1)} copy(bf16[9,7,128,128]{3,1,2,0:T(8,128)(2,1)S(1)} %fusion.5) | data formatting | bytes 4128768 | tf_op jit(solution)/shard_map/convert_element_type | solution.py:273
  11.7 0.1 dynamic-slice_compare_fusion
  11.8 0.1 fusion.24
  11.9 0.1 broadcast_in_dim.11
  12.0 0.1 convert_element_type.40
  12.1 0.7 fusion.28
  12.7 0.1 rev.3
  12.9 0.0 collective-permute-done
  12.9 1.1 %fusion.18.src_ref = bf16[24,70,128]{2,1,0:T(8,128)(2,1)} fusion(s32[]{:T(128)S(6)} %select_n.46, bf16[4,128,128]{2,1,0:T(8,128)(2,1)S(1)} %collective-permute-done, bf16[16,128,128]{2,1,0:T(8,128)(2,1)S(1)} %convert_element_type.34, bf16[4,128,128]{2,1,0:T(8,128)(2,1)S(1)} %collective-permute-done.1), kind=kLoop, calls=%fused_computation.17 | loop fusion | flops 2795520 | bytes 1217536 | tf_op jit(solution)/shard_map/concatenate | solution.py:19
  14.0 0.7 broadcast_in_dim.12.cover_ref
  14.7 7.0 %shard_map.46 = bf16[16,64,128]{2,1,0:T(8,128)(2,1)} custom-call(bf16[24,70,128]{2,1,0:T(8,128)(2,1)} %fusion.18.src_ref, bf16[9,896,128]{2,1,0:T(8,128)(2,1)} %bitcast.23, bf16[16,64,128]{2,1,0:T(8,128)(2,1)} %bitcast.25, f32[64,128]{1,0:T(8,128)} %broadcast_in_dim.12.cover_ref), custom_call_target="tpu_custom_call" | custom-call | tf_op jit(solution)/shard_map/pallas_call | solution.py:300
  21.7 0.8 slice_select_fusion
  22.5 1.2 %collective-permute-start.2 = (bf16[16,3,128]{2,1,0:T(4,128)(2,1)S(1)}, bf16[16,3,128]{2,1,0:T(4,128)(2,1)S(1)}, u32[]{:S(2)}, u32[]{:S(2)}) collective-permute-start(bf16[16,3,128]{2,1,0:T(4,128)(2,1)S(1)} %slice_select_fusion), channel_id=1, source_target_pairs={{0,16},{16,0},{32,48},{48,32},{64,80},{80,64},{96,112},{112,96},{1... | collective-permute-start | bytes 36872 | tf_op jit(solution)/shard_map/ppermute | solution.py:37
  23.7 0.9 %fusion.8 = bf16[9,7,128,128]{3,1,2,0:T(8,128)(2,1)S(1)} fusion(bf16[9,7,25]{2,1,0:T(8,128)(2,1)S(1)} %rev.3), kind=kOutput, calls=%fused_computation.5 | convolution fusion | flops 53870592 | bytes 2067534 | tf_op jit(solution)/shard_map/abt,tpz->abpz/dot_general | solution.py:273
  24.6 1.9 %copy.7 = bf16[9,7,128,128]{3,2,1,0:T(8,128)(2,1)} copy(bf16[9,7,128,128]{3,1,2,0:T(8,128)(2,1)S(1)} %fusion.8) | data formatting | bytes 4128768 | tf_op jit(solution)/shard_map/convert_element_type | solution.py:273
  26.5 0.8 %pad_maximum_fusion.quot_ref = bf16[16,70,128]{2,1,0:T(8,128)(2,1)} fusion(bf16[16,3,128]{2,1,0:T(4,128)(2,1)S(1)} %get-tuple-element.10, bf16[16,64,128]{2,1,0:T(8,128)(2,1)S(1)} %copy-done, bf16[16,3,128]{2,1,0:T(4,128)(2,1)S(1)} %get-tuple-element.9), kind=kLoop, calls=%fused_computation.20 | loop fusion | flops 860160 | bytes 573440 | tf_op jit(solution)/shard_map/concatenate | solution.py:341
  27.3 50.6 %shard_map.47 = f32[16,128,128]{2,1,0:T(8,128)} custom-call(bf16[16,70,128]{2,1,0:T(8,128)(2,1)} %pad_maximum_fusion.quot_ref, bf16[9,896,128]{2,1,0:T(8,128)(2,1)} %bitcast.24, f32[64,128]{1,0:T(8,128)} %broadcast_in_dim.12.cover_ref, f32[16,128,128]{2,1,0:T(8,128)} %est_ref.1), custom_call_target="tpu_custom_call" | custom-call | tf_op jit(solution)/shard_map/pallas_call | solution.py:242
  77.9 2.3 %copy.21 = f32[16,128,128]{2,1,0:T(8,128)} copy(f32[16,128,128]{2,1,0:T(8,128)} %shard_map.47) | data formatting | bytes 2097152
  (7 shorter events, 0.0 us)
Async XLA Ops:
  1.3 11.5 %collective-permute-start = (bf16[4,128,128]{2,1,0:T(8,128)(2,1)S(1)}, bf16[4,128,128]{2,1,0:T(8,128)(2,1)S(1)}, u32[]{:S(2)}, u32[]{:S(2)}) collective-permute-start(bf16[4,128,128]{2,1,0:T(8,128)(2,1)S(1)} %get-tuple-element.8), channel_id=1, source_target_pairs={{0,1},{1,2},{2,3},{3,4},{4,5},{5,6},{6,7},{7,8},{8,9},{9,10},{10,1... | collective-permute-start | bytes 393224 | tf_op jit(solution)/shard_map/ppermute | solution.py:21
  5.3 7.6 %collective-permute-start.1 = (bf16[4,128,128]{2,1,0:T(8,128)(2,1)S(1)}, bf16[4,128,128]{2,1,0:T(8,128)(2,1)S(1)}, u32[]{:S(2)}, u32[]{:S(2)}) collective-permute-start(bf16[4,128,128]{2,1,0:T(8,128)(2,1)S(1)} %get-tuple-element.7), channel_id=1, source_target_pairs={{1,0},{2,1},{3,2},{4,3},{5,4},{6,5},{7,6},{8,7},{9,8},{10,9},{11,1... | collective-permute-start | bytes 393224 | tf_op jit(solution)/shard_map/ppermute | solution.py:23
  9.8 2.0 %copy-start.1 = (s32[8,1,4]{0,2,1:T(4,128)S(1)}, s32[8,1,4]{0,2,1:T(4,128)}, u32[]{:S(2)}) copy-start(s32[8,1,4]{0,2,1:T(4,128)} %param.7) | copy-start | bytes 388
  22.5 4.1 %collective-permute-start.2 = (bf16[16,3,128]{2,1,0:T(4,128)(2,1)S(1)}, bf16[16,3,128]{2,1,0:T(4,128)(2,1)S(1)}, u32[]{:S(2)}, u32[]{:S(2)}) collective-permute-start(bf16[16,3,128]{2,1,0:T(4,128)(2,1)S(1)} %slice_select_fusion), channel_id=1, source_target_pairs={{0,16},{16,0},{32,48},{48,32},{64,80},{80,64},{96,112},{112,96},{1... | collective-permute-start | bytes 36872 | tf_op jit(solution)/shard_map/ppermute | solution.py:37
  24.6 2.0 %copy-start = (bf16[16,64,128]{2,1,0:T(8,128)(2,1)S(1)}, bf16[16,64,128]{2,1,0:T(8,128)(2,1)}, u32[]{:S(2)}) copy-start(bf16[16,64,128]{2,1,0:T(8,128)(2,1)} %shard_map.46) | copy-start | bytes 786436

commit v12 on v11

--- a/solution.py
+++ b/solution.py
@@ -76,8 +76,17 @@
             barrier, inc=1, device_id={"view": view_id * shares + (part + d) % shares},
             device_id_type=mesh_kind,
         )
-    for other in (up, down):
-        pl.semaphore_signal(barrier, inc=1, device_id={"blk": other}, device_id_type=mesh_kind)
+    has_up = layer < layers - 1
+    has_down = layer > 0
+
+    @pl.when(has_up)
+    def _():
+        pl.semaphore_signal(barrier, inc=1, device_id={"blk": up}, device_id_type=mesh_kind)
+
+    @pl.when(has_down)
+    def _():
+        pl.semaphore_signal(barrier, inc=1, device_id={"blk": down}, device_id_type=mesh_kind)
+
     ext_ref[pl.ds(width, rows)] = quot_ref[...]
 
     def build_columns(first, count):
@@ -98,7 +107,9 @@
         acc = acc.reshape(step, share_w, depth)
         factor_ref[pl.ds(target * step, step)] = jnp.where(keep[None], acc, 1.0)
 
-    pl.semaphore_wait(barrier, groups + shares)
+    pl.semaphore_wait(
+        barrier, groups + shares - 2 + has_up.astype(jnp.int32) + has_down.astype(jnp.int32)
+    )
     to_up = pltpu.make_async_remote_copy(
         src_ref=quot_ref.at[pl.ds(rows - width, width)],
         dst_ref=ext_ref.at[pl.ds(0, width)],
@@ -115,8 +126,14 @@
         device_id={"blk": down},
         device_id_type=mesh_kind,
     )
-    to_up.start()
-    to_down.start()
+    @pl.when(has_up)
+    def _():
+        to_up.start()
+
+    @pl.when(has_down)
+    def _():
+        to_down.start()
+
     reach = width // step
     inner = list(range(reach, groups - reach))
     outer = list(range(reach)) + list(range(groups - reach, groups))
@@ -141,8 +158,15 @@
 
     for target in inner:
         send_chunk(target)
-    to_up.wait()
-    to_down.wait()
+    @pl.when(has_up)
+    def _():
+        to_up.wait_send()
+        to_down.wait_recv()
+
+    @pl.when(has_down)
+    def _():
+        to_down.wait_send()
+        to_up.wait_recv()
 
     @pl.when(layer == 0)
     def _():

time: 80.6 us -> 77 us (0.955)
  the two profiles are of different devices: /device:TPU:1 before, /device:TPU:71 now
where the time goes in v12:
time: 77 us; the launch traced here: 76.7 us
  Pallas kernels  53.7 us (70%)
  local copies, waits for them, and re-layouts  7.15 us (9%)
  starting transfers between devices  6.84 us (9%)
  other arithmetic  6.5 us (8%)
  matrix products  2.37 us (3%)
    pallas_call x1, Pallas kernels, product_gather(): pl.pallas_call(functools.partial(product_kernel, n, shares, width), out_s...  46.7 us
    pallas_call x1, Pallas kernels, quotient_of(): pl.pallas_call(functools.partial(conv_kernel, 4), out_shape=jax.ShapeDtyp...  7 us
    convert_element_type x2, local copies, waits for them, and re-layouts, band_table(): jnp.einsum('abt,tpz->abpz', kernel, onehot, preferred_element_type=jnp.fl...  3.88 us
    ppermute x1, starting transfers between devices, with_halo(): lax.ppermute(tail, axis, [(i, (i + 1) % count) for i in range(ends)])  3.12 us
    dot_general x2, matrix products, band_table(): jnp.einsum('abt,tpz->abpz', kernel, onehot, preferred_element_type=jnp.fl...  2.37 us
    unnamed x5, local copies, waits for them, and re-layouts  2.31 us
    ppermute x1, starting transfers between devices, with_halo(): lax.ppermute(head, axis, [((i + 1) % count, i) for i in range(ends)])  2.16 us
    reduce_sum x1, other arithmetic, local(): kernel = (spread / jnp.sum(spread)).astype(jnp.bfloat16)  1.63 us
  transfers between devices with their start and end apart: 3, of which 0 were waited for; matrix products, arithmetic and copies ran while one was open for 12% of the time, Pallas kernels for 0%

profile of v12, /device:TPU:71, one launch (start us, length us, event | category | flops | bytes accessed | tf_op | source)
XLA Modules:
  0.0 76.7 jit_solution(1480806391591893529)
XLA Ops:
  0.0 1.3 %convert_element_type.34 = bf16[16,128,128]{2,1,0:T(8,128)(2,1)S(1)} convert(f32[16,128,128]{2,1,0:T(8,128)} %est_ref.1) | non-fusion elementwise | flops 262144 | bytes 1572864 | tf_op jit(solution)/shard_map/convert_element_type | solution.py:344
  1.3 3.1 %collective-permute-start = (bf16[4,128,128]{2,1,0:T(8,128)(2,1)S(1)}, bf16[4,128,128]{2,1,0:T(8,128)(2,1)S(1)}, u32[]{:S(2)}, u32[]{:S(2)}) collective-permute-start(bf16[4,128,128]{2,1,0:T(8,128)(2,1)S(1)} %get-tuple-element.8), channel_id=1, source_target_pairs={{0,1},{1,2},{2,3},{3,4},{4,5},{5,6},{6,7},{7,8},{8,9},{9,10},{10,1... | collective-permute-start | bytes 393224 | tf_op jit(solution)/shard_map/ppermute | solution.py:21
  4.5 2.2 %collective-permute-start.1 = (bf16[4,128,128]{2,1,0:T(8,128)(2,1)S(1)}, bf16[4,128,128]{2,1,0:T(8,128)(2,1)S(1)}, u32[]{:S(2)}, u32[]{:S(2)}) collective-permute-start(bf16[4,128,128]{2,1,0:T(8,128)(2,1)S(1)} %get-tuple-element.7), channel_id=1, source_target_pairs={{1,0},{2,1},{3,2},{4,3},{5,4},{6,5},{7,6},{8,7},{9,8},{10,9},{11,1... | collective-permute-start | bytes 393224 | tf_op jit(solution)/shard_map/ppermute | solution.py:23
  6.7 1.6 %fusion.29 = (f32[]{:T(128)}, f32[1,9,7,25]{3,0,2,1:T(1,128)S(1)}) fusion(f32[8,9,7,25]{3,0,2,1:T(8,128)} %param.6, s32[]{:T(128)S(6)} %select_n.48), kind=kLoop, calls=%fused_computation.35 | loop fusion | flops 1574 | bytes 12608 | tf_op jit(solution)/shard_map/reduce_sum | solution.py:348
  8.3 1.5 %fusion.5 = bf16[9,7,128,128]{3,1,2,0:T(8,128)(2,1)S(1)} fusion(f32[1,9,7,25]{3,0,2,1:T(1,128)S(1)} %get-tuple-element.6, f32[]{:T(128)} %get-tuple-element.5), kind=kOutput, calls=%fused_computation.4 | convolution fusion | flops 53873744 | bytes 2070688 | tf_op jit(solution)/shard_map/abt,tpz->abpz/dot_general | solution.py:297
  9.8 0.0 copy-start.1
  9.8 1.9 %copy.6 = bf16[9,7,128,128]{3,2,1,0:T(8,128)(2,1)} copy(bf16[9,7,128,128]{3,1,2,0:T(8,128)(2,1)S(1)} %fusion.5) | data formatting | bytes 4128768 | tf_op jit(solution)/shard_map/convert_element_type | solution.py:297
  11.8 0.1 dynamic-slice_compare_fusion
  11.8 0.1 fusion.24
  12.0 0.1 broadcast_in_dim.11
  12.0 0.1 convert_element_type.40
  12.1 0.7 fusion.28
  12.8 0.1 rev.3
  12.9 0.0 collective-permute-done
  12.9 1.1 %fusion.18.src_ref = bf16[24,70,128]{2,1,0:T(8,128)(2,1)} fusion(s32[]{:T(128)S(6)} %select_n.46, bf16[4,128,128]{2,1,0:T(8,128)(2,1)S(1)} %collective-permute-done, bf16[16,128,128]{2,1,0:T(8,128)(2,1)S(1)} %convert_element_type.34, bf16[4,128,128]{2,1,0:T(8,128)(2,1)S(1)} %collective-permute-done.1), kind=kLoop, calls=%fused_computation.17 | loop fusion | flops 2795520 | bytes 1217536 | tf_op jit(solution)/shard_map/concatenate | solution.py:19
  14.0 0.7 broadcast_in_dim.12.cover_ref
  14.7 7.0 %shard_map.46 = bf16[16,64,128]{2,1,0:T(8,128)(2,1)} custom-call(bf16[24,70,128]{2,1,0:T(8,128)(2,1)} %fusion.18.src_ref, bf16[9,896,128]{2,1,0:T(8,128)(2,1)} %bitcast.23, bf16[16,64,128]{2,1,0:T(8,128)(2,1)} %bitcast.25, f32[64,128]{1,0:T(8,128)} %broadcast_in_dim.12.cover_ref), custom_call_target="tpu_custom_call" | custom-call | tf_op jit(solution)/shard_map/pallas_call | solution.py:324
  21.7 0.8 %slice_select_fusion = bf16[16,3,128]{2,1,0:T(4,128)(2,1)S(1)} fusion(bf16[16,64,128]{2,1,0:T(8,128)(2,1)} %shard_map.46, pred[]{:T(512)S(6)} %eq.11), kind=kLoop, calls=%fused_computation.25 | loop fusion | flops 6144 | bytes 36865 | tf_op jit(solution)/shard_map/jit(_where)/select_n | solution.py:361
  22.5 1.6 %collective-permute-start.2 = (bf16[16,3,128]{2,1,0:T(4,128)(2,1)S(1)}, bf16[16,3,128]{2,1,0:T(4,128)(2,1)S(1)}, u32[]{:S(2)}, u32[]{:S(2)}) collective-permute-start(bf16[16,3,128]{2,1,0:T(4,128)(2,1)S(1)} %slice_select_fusion), channel_id=1, source_target_pairs={{0,16},{16,0},{32,48},{48,32},{64,80},{80,64},{96,112},{112,96},{1... | collective-permute-start | bytes 36872 | tf_op jit(solution)/shard_map/ppermute | solution.py:37
  24.0 0.9 %fusion.8 = bf16[9,7,128,128]{3,1,2,0:T(8,128)(2,1)S(1)} fusion(bf16[9,7,25]{2,1,0:T(8,128)(2,1)S(1)} %rev.3), kind=kOutput, calls=%fused_computation.5 | convolution fusion | flops 53870592 | bytes 2067534 | tf_op jit(solution)/shard_map/abt,tpz->abpz/dot_general | solution.py:297
  24.9 1.9 %copy.7 = bf16[9,7,128,128]{3,2,1,0:T(8,128)(2,1)} copy(bf16[9,7,128,128]{3,1,2,0:T(8,128)(2,1)S(1)} %fusion.8) | data formatting | bytes 4128768 | tf_op jit(solution)/shard_map/convert_element_type | solution.py:297
  26.9 0.8 %pad_maximum_fusion.quot_ref = bf16[16,70,128]{2,1,0:T(8,128)(2,1)} fusion(bf16[16,3,128]{2,1,0:T(4,128)(2,1)S(1)} %get-tuple-element.10, bf16[16,64,128]{2,1,0:T(8,128)(2,1)S(1)} %copy-done, bf16[16,3,128]{2,1,0:T(4,128)(2,1)S(1)} %get-tuple-element.9), kind=kLoop, calls=%fused_computation.20 | loop fusion | flops 860160 | bytes 573440 | tf_op jit(solution)/shard_map/concatenate | solution.py:365
  27.7 46.7 %shard_map.47 = f32[16,128,128]{2,1,0:T(8,128)} custom-call(bf16[16,70,128]{2,1,0:T(8,128)(2,1)} %pad_maximum_fusion.quot_ref, bf16[9,896,128]{2,1,0:T(8,128)(2,1)} %bitcast.24, f32[64,128]{1,0:T(8,128)} %broadcast_in_dim.12.cover_ref, f32[16,128,128]{2,1,0:T(8,128)} %est_ref.1), custom_call_target="tpu_custom_call" | custom-call | tf_op jit(solution)/shard_map/pallas_call | solution.py:266
  74.4 2.3 %copy.21 = f32[16,128,128]{2,1,0:T(8,128)} copy(f32[16,128,128]{2,1,0:T(8,128)} %shard_map.47) | data formatting | bytes 2097152
  (7 shorter events, 0.0 us)
Async XLA Ops:
  1.3 11.6 %collective-permute-start = (bf16[4,128,128]{2,1,0:T(8,128)(2,1)S(1)}, bf16[4,128,128]{2,1,0:T(8,128)(2,1)S(1)}, u32[]{:S(2)}, u32[]{:S(2)}) collective-permute-start(bf16[4,128,128]{2,1,0:T(8,128)(2,1)S(1)} %get-tuple-element.8), channel_id=1, source_target_pairs={{0,1},{1,2},{2,3},{3,4},{4,5},{5,6},{6,7},{7,8},{8,9},{9,10},{10,1... | collective-permute-start | bytes 393224 | tf_op jit(solution)/shard_map/ppermute | solution.py:21
  4.5 8.4 %collective-permute-start.1 = (bf16[4,128,128]{2,1,0:T(8,128)(2,1)S(1)}, bf16[4,128,128]{2,1,0:T(8,128)(2,1)S(1)}, u32[]{:S(2)}, u32[]{:S(2)}) collective-permute-start(bf16[4,128,128]{2,1,0:T(8,128)(2,1)S(1)} %get-tuple-element.7), channel_id=1, source_target_pairs={{1,0},{2,1},{3,2},{4,3},{5,4},{6,5},{7,6},{8,7},{9,8},{10,9},{11,1... | collective-permute-start | bytes 393224 | tf_op jit(solution)/shard_map/ppermute | solution.py:23
  9.8 2.0 %copy-start.1 = (s32[8,1,4]{0,2,1:T(4,128)S(1)}, s32[8,1,4]{0,2,1:T(4,128)}, u32[]{:S(2)}) copy-start(s32[8,1,4]{0,2,1:T(4,128)} %param.7) | copy-start | bytes 388
  22.5 4.4 %collective-permute-start.2 = (bf16[16,3,128]{2,1,0:T(4,128)(2,1)S(1)}, bf16[16,3,128]{2,1,0:T(4,128)(2,1)S(1)}, u32[]{:S(2)}, u32[]{:S(2)}) collective-permute-start(bf16[16,3,128]{2,1,0:T(4,128)(2,1)S(1)} %slice_select_fusion), channel_id=1, source_target_pairs={{0,16},{16,0},{32,48},{48,32},{64,80},{80,64},{96,112},{112,96},{1... | collective-permute-start | bytes 36872 | tf_op jit(solution)/shard_map/ppermute | solution.py:37
  24.9 2.0 %copy-start = (bf16[16,64,128]{2,1,0:T(8,128)(2,1)S(1)}, bf16[16,64,128]{2,1,0:T(8,128)(2,1)}, u32[]{:S(2)}) copy-start(bf16[16,64,128]{2,1,0:T(8,128)(2,1)} %shard_map.46) | copy-start | bytes 786436

commit v13 on v12

--- a/solution.py
+++ b/solution.py
@@ -50,7 +50,7 @@
 
 def product_kernel(
     n, shares, width, quot_ref, band_ref, cover_ref, est_ref, out_ref, ext_ref, cols_ref, factor_ref,
-    held, send1, recv1, send2, recv2, send_halo, recv_halo,
+    held, send1, recv1, send2, recv2, send3, recv3, send_halo, recv_halo,
 ):
     groups = n // shares
     step, share_w, depth = held.shape[1:]
@@ -201,6 +201,9 @@
     mine = pl.ds(view_id * step, step)
     cols = pl.ds(part * share_w, share_w)
     out_ref[mine, cols, :] = acc * est_ref[mine, cols, :]
+    other = (part + 1) % shares
+    partner = view_id * shares + other
+    other_cols = pl.ds(other * share_w, share_w)
     outgoing = []
     for d in range(1, groups):
         target = (view_id + d) % groups
@@ -214,6 +217,20 @@
         )
         copy.start()
         outgoing.append(copy)
+
+    def forward(chunk):
+        copy = pltpu.make_async_remote_copy(
+            src_ref=out_ref.at[pl.ds(chunk * step, step), cols],
+            dst_ref=out_ref.at[pl.ds(chunk * step, step), cols],
+            send_sem=send3.at[chunk],
+            recv_sem=recv3.at[chunk],
+            device_id={"view": partner},
+            device_id_type=mesh_kind,
+        )
+        copy.start()
+        outgoing.append(copy)
+
+    forward(view_id)
     for d in range(1, groups):
         source = (view_id - d + groups) % groups
         src_rows = pl.ds(source * step, step)
@@ -225,30 +242,15 @@
             device_id={"view": source * shares + part},
             device_id_type=mesh_kind,
         ).wait_recv()
-    for copy in outgoing:
-        copy.wait_send()
-    outgoing = []
-    for d in range(1, shares):
-        other = (part + d) % shares
-        copy = pltpu.make_async_remote_copy(
-            src_ref=out_ref.at[:, cols],
-            dst_ref=out_ref.at[:, cols],
-            send_sem=send2.at[groups + d],
-            recv_sem=recv2.at[groups + d],
-            device_id={"view": view_id * shares + other},
-            device_id_type=mesh_kind,
-        )
-        copy.start()
-        outgoing.append(copy)
-    for d in range(1, shares):
-        other = (part - d + shares) % shares
-        other_cols = pl.ds(other * share_w, share_w)
+        forward(source)
+    for chunk in range(groups):
+        chunk_rows = pl.ds(chunk * step, step)
         pltpu.make_async_remote_copy(
-            src_ref=out_ref.at[:, other_cols],
-            dst_ref=out_ref.at[:, other_cols],
-            send_sem=send2.at[groups + d],
-            recv_sem=recv2.at[groups + d],
-            device_id={"view": view_id * shares + other},
+            src_ref=out_ref.at[chunk_rows, other_cols],
+            dst_ref=out_ref.at[chunk_rows, other_cols],
+            send_sem=send3.at[chunk],
+            recv_sem=recv3.at[chunk],
+            device_id={"view": partner},
             device_id_type=mesh_kind,
         ).wait_recv()
     for copy in outgoing:
@@ -275,8 +277,10 @@
             pltpu.VMEM((groups, step, share_w, depth), jnp.float32),
             pltpu.SemaphoreType.DMA((groups,)),
             pltpu.SemaphoreType.DMA((groups,)),
-            pltpu.SemaphoreType.DMA((groups + shares,)),
-            pltpu.SemaphoreType.DMA((groups + shares,)),
+            pltpu.SemaphoreType.DMA((groups,)),
+            pltpu.SemaphoreType.DMA((groups,)),
+            pltpu.SemaphoreType.DMA((groups,)),
+            pltpu.SemaphoreType.DMA((groups,)),
             pltpu.SemaphoreType.DMA((2,)),
             pltpu.SemaphoreType.DMA((2,)),
         ],

time: 77 us -> 76.9 us (level)
  no operation moved by 1% of the time
where the time goes in v13:
time: 76.9 us; the launch traced here: 76.5 us
  Pallas kernels  53.5 us (70%)
  local copies, waits for them, and re-layouts  7.15 us (9%)
  starting transfers between devices  6.84 us (9%)
  other arithmetic  6.5 us (8%)
  matrix products  2.37 us (3%)
    pallas_call x1, Pallas kernels, product_gather(): pl.pallas_call(functools.partial(product_kernel, n, shares, width), out_s...  46.5 us
    pallas_call x1, Pallas kernels, quotient_of(): pl.pallas_call(functools.partial(conv_kernel, 4), out_shape=jax.ShapeDtyp...  7 us
    convert_element_type x2, local copies, waits for them, and re-layouts, band_table(): jnp.einsum('abt,tpz->abpz', kernel, onehot, preferred_element_type=jnp.fl...  3.88 us
    ppermute x1, starting transfers between devices, with_halo(): lax.ppermute(tail, axis, [(i, (i + 1) % count) for i in range(ends)])  3.12 us
    dot_general x2, matrix products, band_table(): jnp.einsum('abt,tpz->abpz', kernel, onehot, preferred_element_type=jnp.fl...  2.37 us
    unnamed x5, local copies, waits for them, and re-layouts  2.31 us
    ppermute x1, starting transfers between devices, with_halo(): lax.ppermute(head, axis, [((i + 1) % count, i) for i in range(ends)])  2.16 us
    reduce_sum x1, other arithmetic, local(): kernel = (spread / jnp.sum(spread)).astype(jnp.bfloat16)  1.63 us
  transfers between devices with their start and end apart: 3, of which 0 were waited for; matrix products, arithmetic and copies ran while one was open for 12% of the time, Pallas kernels for 0%

profile of v13, /device:TPU:71, one launch (start us, length us, event | category | flops | bytes accessed | tf_op | source)
XLA Modules:
  0.0 76.5 jit_solution(15819920903228516577)
XLA Ops:
  0.0 1.3 %convert_element_type.34 = bf16[16,128,128]{2,1,0:T(8,128)(2,1)S(1)} convert(f32[16,128,128]{2,1,0:T(8,128)} %est_ref.1) | non-fusion elementwise | flops 262144 | bytes 1572864 | tf_op jit(solution)/shard_map/convert_element_type | solution.py:348
  1.3 3.1 %collective-permute-start = (bf16[4,128,128]{2,1,0:T(8,128)(2,1)S(1)}, bf16[4,128,128]{2,1,0:T(8,128)(2,1)S(1)}, u32[]{:S(2)}, u32[]{:S(2)}) collective-permute-start(bf16[4,128,128]{2,1,0:T(8,128)(2,1)S(1)} %get-tuple-element.8), channel_id=1, source_target_pairs={{0,1},{1,2},{2,3},{3,4},{4,5},{5,6},{6,7},{7,8},{8,9},{9,10},{10,1... | collective-permute-start | bytes 393224 | tf_op jit(solution)/shard_map/ppermute | solution.py:21
  4.5 2.2 %collective-permute-start.1 = (bf16[4,128,128]{2,1,0:T(8,128)(2,1)S(1)}, bf16[4,128,128]{2,1,0:T(8,128)(2,1)S(1)}, u32[]{:S(2)}, u32[]{:S(2)}) collective-permute-start(bf16[4,128,128]{2,1,0:T(8,128)(2,1)S(1)} %get-tuple-element.7), channel_id=1, source_target_pairs={{1,0},{2,1},{3,2},{4,3},{5,4},{6,5},{7,6},{8,7},{9,8},{10,9},{11,1... | collective-permute-start | bytes 393224 | tf_op jit(solution)/shard_map/ppermute | solution.py:23
  6.7 1.6 %fusion.29 = (f32[]{:T(128)}, f32[1,9,7,25]{3,0,2,1:T(1,128)S(1)}) fusion(f32[8,9,7,25]{3,0,2,1:T(8,128)} %param.6, s32[]{:T(128)S(6)} %select_n.48), kind=kLoop, calls=%fused_computation.35 | loop fusion | flops 1574 | bytes 12608 | tf_op jit(solution)/shard_map/reduce_sum | solution.py:352
  8.3 1.5 %fusion.5 = bf16[9,7,128,128]{3,1,2,0:T(8,128)(2,1)S(1)} fusion(f32[1,9,7,25]{3,0,2,1:T(1,128)S(1)} %get-tuple-element.6, f32[]{:T(128)} %get-tuple-element.5), kind=kOutput, calls=%fused_computation.4 | convolution fusion | flops 53873744 | bytes 2070688 | tf_op jit(solution)/shard_map/abt,tpz->abpz/dot_general | solution.py:301
  9.8 0.0 copy-start.1
  9.8 1.9 %copy.6 = bf16[9,7,128,128]{3,2,1,0:T(8,128)(2,1)} copy(bf16[9,7,128,128]{3,1,2,0:T(8,128)(2,1)S(1)} %fusion.5) | data formatting | bytes 4128768 | tf_op jit(solution)/shard_map/convert_element_type | solution.py:301
  11.8 0.1 dynamic-slice_compare_fusion
  11.8 0.1 fusion.24
  12.0 0.1 broadcast_in_dim.11
  12.0 0.1 convert_element_type.40
  12.1 0.7 fusion.28
  12.8 0.1 rev.3
  12.9 0.0 collective-permute-done
  12.9 1.1 %fusion.18.src_ref = bf16[24,70,128]{2,1,0:T(8,128)(2,1)} fusion(s32[]{:T(128)S(6)} %select_n.46, bf16[4,128,128]{2,1,0:T(8,128)(2,1)S(1)} %collective-permute-done, bf16[16,128,128]{2,1,0:T(8,128)(2,1)S(1)} %convert_element_type.34, bf16[4,128,128]{2,1,0:T(8,128)(2,1)S(1)} %collective-permute-done.1), kind=kLoop, calls=%fused_computation.17 | loop fusion | flops 2795520 | bytes 1217536 | tf_op jit(solution)/shard_map/concatenate | solution.py:19
  14.0 0.7 broadcast_in_dim.12.cover_ref
  14.7 7.0 %shard_map.46 = bf16[16,64,128]{2,1,0:T(8,128)(2,1)} custom-call(bf16[24,70,128]{2,1,0:T(8,128)(2,1)} %fusion.18.src_ref, bf16[9,896,128]{2,1,0:T(8,128)(2,1)} %bitcast.23, bf16[16,64,128]{2,1,0:T(8,128)(2,1)} %bitcast.25, f32[64,128]{1,0:T(8,128)} %broadcast_in_dim.12.cover_ref), custom_call_target="tpu_custom_call" | custom-call | tf_op jit(solution)/shard_map/pallas_call | solution.py:328
  21.7 0.8 %slice_select_fusion = bf16[16,3,128]{2,1,0:T(4,128)(2,1)S(1)} fusion(bf16[16,64,128]{2,1,0:T(8,128)(2,1)} %shard_map.46, pred[]{:T(512)S(6)} %eq.11), kind=kLoop, calls=%fused_computation.25 | loop fusion | flops 6144 | bytes 36865 | tf_op jit(solution)/shard_map/jit(_where)/select_n | solution.py:365
  22.5 1.6 %collective-permute-start.2 = (bf16[16,3,128]{2,1,0:T(4,128)(2,1)S(1)}, bf16[16,3,128]{2,1,0:T(4,128)(2,1)S(1)}, u32[]{:S(2)}, u32[]{:S(2)}) collective-permute-start(bf16[16,3,128]{2,1,0:T(4,128)(2,1)S(1)} %slice_select_fusion), channel_id=1, source_target_pairs={{0,16},{16,0},{32,48},{48,32},{64,80},{80,64},{96,112},{112,96},{1... | collective-permute-start | bytes 36872 | tf_op jit(solution)/shard_map/ppermute | solution.py:37
  24.0 0.9 %fusion.8 = bf16[9,7,128,128]{3,1,2,0:T(8,128)(2,1)S(1)} fusion(bf16[9,7,25]{2,1,0:T(8,128)(2,1)S(1)} %rev.3), kind=kOutput, calls=%fused_computation.5 | convolution fusion | flops 53870592 | bytes 2067534 | tf_op jit(solution)/shard_map/abt,tpz->abpz/dot_general | solution.py:301
  24.9 1.9 %copy.7 = bf16[9,7,128,128]{3,2,1,0:T(8,128)(2,1)} copy(bf16[9,7,128,128]{3,1,2,0:T(8,128)(2,1)S(1)} %fusion.8) | data formatting | bytes 4128768 | tf_op jit(solution)/shard_map/convert_element_type | solution.py:301
  26.9 0.8 %pad_maximum_fusion.quot_ref = bf16[16,70,128]{2,1,0:T(8,128)(2,1)} fusion(bf16[16,3,128]{2,1,0:T(4,128)(2,1)S(1)} %get-tuple-element.10, bf16[16,64,128]{2,1,0:T(8,128)(2,1)S(1)} %copy-done, bf16[16,3,128]{2,1,0:T(4,128)(2,1)S(1)} %get-tuple-element.9), kind=kLoop, calls=%fused_computation.20 | loop fusion | flops 860160 | bytes 573440 | tf_op jit(solution)/shard_map/concatenate | solution.py:369
  27.7 46.5 %shard_map.47 = f32[16,128,128]{2,1,0:T(8,128)} custom-call(bf16[16,70,128]{2,1,0:T(8,128)(2,1)} %pad_maximum_fusion.quot_ref, bf16[9,896,128]{2,1,0:T(8,128)(2,1)} %bitcast.24, f32[64,128]{1,0:T(8,128)} %broadcast_in_dim.12.cover_ref, f32[16,128,128]{2,1,0:T(8,128)} %est_ref.1), custom_call_target="tpu_custom_call" | custom-call | tf_op jit(solution)/shard_map/pallas_call | solution.py:268
  74.2 2.3 %copy.21 = f32[16,128,128]{2,1,0:T(8,128)} copy(f32[16,128,128]{2,1,0:T(8,128)} %shard_map.47) | data formatting | bytes 2097152
  (7 shorter events, 0.0 us)
Async XLA Ops:
  1.3 11.6 %collective-permute-start = (bf16[4,128,128]{2,1,0:T(8,128)(2,1)S(1)}, bf16[4,128,128]{2,1,0:T(8,128)(2,1)S(1)}, u32[]{:S(2)}, u32[]{:S(2)}) collective-permute-start(bf16[4,128,128]{2,1,0:T(8,128)(2,1)S(1)} %get-tuple-element.8), channel_id=1, source_target_pairs={{0,1},{1,2},{2,3},{3,4},{4,5},{5,6},{6,7},{7,8},{8,9},{9,10},{10,1... | collective-permute-start | bytes 393224 | tf_op jit(solution)/shard_map/ppermute | solution.py:21
  4.5 8.4 %collective-permute-start.1 = (bf16[4,128,128]{2,1,0:T(8,128)(2,1)S(1)}, bf16[4,128,128]{2,1,0:T(8,128)(2,1)S(1)}, u32[]{:S(2)}, u32[]{:S(2)}) collective-permute-start(bf16[4,128,128]{2,1,0:T(8,128)(2,1)S(1)} %get-tuple-element.7), channel_id=1, source_target_pairs={{1,0},{2,1},{3,2},{4,3},{5,4},{6,5},{7,6},{8,7},{9,8},{10,9},{11,1... | collective-permute-start | bytes 393224 | tf_op jit(solution)/shard_map/ppermute | solution.py:23
  9.8 2.0 %copy-start.1 = (s32[8,1,4]{0,2,1:T(4,128)S(1)}, s32[8,1,4]{0,2,1:T(4,128)}, u32[]{:S(2)}) copy-start(s32[8,1,4]{0,2,1:T(4,128)} %param.7) | copy-start | bytes 388
  22.5 4.4 %collective-permute-start.2 = (bf16[16,3,128]{2,1,0:T(4,128)(2,1)S(1)}, bf16[16,3,128]{2,1,0:T(4,128)(2,1)S(1)}, u32[]{:S(2)}, u32[]{:S(2)}) collective-permute-start(bf16[16,3,128]{2,1,0:T(4,128)(2,1)S(1)} %slice_select_fusion), channel_id=1, source_target_pairs={{0,16},{16,0},{32,48},{48,32},{64,80},{80,64},{96,112},{112,96},{1... | collective-permute-start | bytes 36872 | tf_op jit(solution)/shard_map/ppermute | solution.py:37
  24.9 2.0 %copy-start = (bf16[16,64,128]{2,1,0:T(8,128)(2,1)S(1)}, bf16[16,64,128]{2,1,0:T(8,128)(2,1)}, u32[]{:S(2)}) copy-start(bf16[16,64,128]{2,1,0:T(8,128)(2,1)} %shard_map.46) | copy-start | bytes 786436

commit v14 on v12

--- a/solution.py
+++ b/solution.py
@@ -49,7 +49,7 @@
 
 
 def product_kernel(
-    n, shares, width, quot_ref, band_ref, cover_ref, est_ref, out_ref, ext_ref, cols_ref, factor_ref,
+    n, shares, width, quot_ref, band_ref, cover_ref, out_ref, ext_ref, cols_ref, factor_ref,
     held, send1, recv1, send2, recv2, send_halo, recv_halo,
 ):
     groups = n // shares
@@ -200,7 +200,7 @@
 
     mine = pl.ds(view_id * step, step)
     cols = pl.ds(part * share_w, share_w)
-    out_ref[mine, cols, :] = acc * est_ref[mine, cols, :]
+    out_ref[mine, cols, :] = acc
     outgoing = []
     for d in range(1, groups):
         target = (view_id + d) % groups
@@ -266,7 +266,7 @@
     return pl.pallas_call(
         functools.partial(product_kernel, n, shares, width),
         out_shape=jax.ShapeDtypeStruct(estimate.shape, jnp.float32),
-        in_specs=[vmem] * 4,
+        in_specs=[vmem] * 3,
         out_specs=vmem,
         scratch_shapes=[
             pltpu.VMEM((padded_rows,) + extended.shape[1:], extended.dtype),
@@ -281,7 +281,7 @@
             pltpu.SemaphoreType.DMA((2,)),
         ],
         compiler_params=pltpu.CompilerParams(collective_id=0, has_side_effects=True),
-    )(extended, banded, cover_plane, estimate)
+    )(extended, banded, cover_plane)
 
 
 def band_table(kernel, depth):
@@ -363,7 +363,7 @@
     lower_rim = jnp.where(part > 0, partner, rim_zeros)
     upper_rim = jnp.where(part < shares - 1, partner, rim_zeros)
     extended = jnp.concatenate([lower_rim, quotient, upper_rim], axis=1)
-    return product_gather(extended, backward, cover_plane, estimate, shares, rim_x)
+    return estimate * product_gather(extended, backward, cover_plane, estimate, shares, rim_x)
 
 
 def solution(mesh):

time: 77 us -> 76.7 us (level)
  other arithmetic: 6.5 us -> 8.81 us
  local copies, waits for them, and re-layouts: 7.15 us -> 4.85 us
    mul x0 -> x1, other arithmetic: none -> 2.31 us  [local(): estimate * product_gather(extended, backward, cover_plane, estimate, shar...]
    unnamed x5 -> x6, local copies, waits for them, and re-layouts: 2.31 us -> 0.01 us
where the time goes in v14:
time: 76.7 us; the launch traced here: 76.3 us
  Pallas kernels  53.3 us (69%)
  other arithmetic  8.81 us (11%)
  starting transfers between devices  6.84 us (9%)
  local copies, waits for them, and re-layouts  4.85 us (6%)
  matrix products  2.37 us (3%)
    pallas_call x1, Pallas kernels, product_gather(): pl.pallas_call(functools.partial(product_kernel, n, shares, width), out_s...  46.3 us
    pallas_call x1, Pallas kernels, quotient_of(): pl.pallas_call(functools.partial(conv_kernel, 4), out_shape=jax.ShapeDtyp...  6.99 us
    convert_element_type x2, local copies, waits for them, and re-layouts, band_table(): jnp.einsum('abt,tpz->abpz', kernel, onehot, preferred_element_type=jnp.fl...  3.87 us
    ppermute x1, starting transfers between devices, with_halo(): lax.ppermute(tail, axis, [(i, (i + 1) % count) for i in range(ends)])  3.12 us
    dot_general x2, matrix products, band_table(): jnp.einsum('abt,tpz->abpz', kernel, onehot, preferred_element_type=jnp.fl...  2.37 us
    mul x1, other arithmetic, local(): estimate * product_gather(extended, backward, cover_plane, estimate, shar...  2.31 us
    ppermute x1, starting transfers between devices, with_halo(): lax.ppermute(head, axis, [((i + 1) % count, i) for i in range(ends)])  2.16 us
    reduce_sum x1, other arithmetic, local(): kernel = (spread / jnp.sum(spread)).astype(jnp.bfloat16)  1.63 us
  transfers between devices with their start and end apart: 3, of which 0 were waited for; matrix products, arithmetic and copies ran while one was open for 12% of the time, Pallas kernels for 0%

profile of v14, /device:TPU:71, one launch (start us, length us, event | category | flops | bytes accessed | tf_op | source)
XLA Modules:
  0.0 76.3 jit_solution(2793118879618092728)
XLA Ops:
  0.0 1.3 %convert_element_type.34 = bf16[16,128,128]{2,1,0:T(8,128)(2,1)S(1)} convert(f32[16,128,128]{2,1,0:T(8,128)} %param.4) | non-fusion elementwise | flops 262144 | bytes 1572864 | tf_op jit(solution)/shard_map/convert_element_type | solution.py:344
  1.3 3.1 %collective-permute-start = (bf16[4,128,128]{2,1,0:T(8,128)(2,1)S(1)}, bf16[4,128,128]{2,1,0:T(8,128)(2,1)S(1)}, u32[]{:S(2)}, u32[]{:S(2)}) collective-permute-start(bf16[4,128,128]{2,1,0:T(8,128)(2,1)S(1)} %get-tuple-element.8), channel_id=1, source_target_pairs={{0,1},{1,2},{2,3},{3,4},{4,5},{5,6},{6,7},{7,8},{8,9},{9,10},{10,1... | collective-permute-start | bytes 393224 | tf_op jit(solution)/shard_map/ppermute | solution.py:21
  4.5 2.2 %collective-permute-start.1 = (bf16[4,128,128]{2,1,0:T(8,128)(2,1)S(1)}, bf16[4,128,128]{2,1,0:T(8,128)(2,1)S(1)}, u32[]{:S(2)}, u32[]{:S(2)}) collective-permute-start(bf16[4,128,128]{2,1,0:T(8,128)(2,1)S(1)} %get-tuple-element.7), channel_id=1, source_target_pairs={{1,0},{2,1},{3,2},{4,3},{5,4},{6,5},{7,6},{8,7},{9,8},{10,9},{11,1... | collective-permute-start | bytes 393224 | tf_op jit(solution)/shard_map/ppermute | solution.py:23
  6.7 1.6 %fusion.29 = (f32[]{:T(128)}, f32[1,9,7,25]{3,0,2,1:T(1,128)S(1)}) fusion(f32[8,9,7,25]{3,0,2,1:T(8,128)} %param.6, s32[]{:T(128)S(6)} %select_n.48), kind=kLoop, calls=%fused_computation.35 | loop fusion | flops 1574 | bytes 12608 | tf_op jit(solution)/shard_map/reduce_sum | solution.py:348
  8.3 1.5 %fusion.5 = bf16[9,7,128,128]{3,1,2,0:T(8,128)(2,1)S(1)} fusion(f32[1,9,7,25]{3,0,2,1:T(1,128)S(1)} %get-tuple-element.6, f32[]{:T(128)} %get-tuple-element.5), kind=kOutput, calls=%fused_computation.4 | convolution fusion | flops 53873744 | bytes 2070688 | tf_op jit(solution)/shard_map/abt,tpz->abpz/dot_general | solution.py:297
  9.8 0.0 copy-start.2
  9.8 1.9 %copy.6 = bf16[9,7,128,128]{3,2,1,0:T(8,128)(2,1)} copy(bf16[9,7,128,128]{3,1,2,0:T(8,128)(2,1)S(1)} %fusion.5) | data formatting | bytes 4128768 | tf_op jit(solution)/shard_map/convert_element_type | solution.py:297
  11.8 0.1 dynamic-slice_compare_fusion
  11.8 0.1 fusion.24
  12.0 0.1 broadcast_in_dim.11
  12.0 0.1 convert_element_type.40
  12.1 0.7 fusion.28
  12.8 0.1 rev.3
  12.9 0.0 collective-permute-done
  12.9 1.1 %fusion.18.src_ref = bf16[24,70,128]{2,1,0:T(8,128)(2,1)} fusion(s32[]{:T(128)S(6)} %select_n.46, bf16[4,128,128]{2,1,0:T(8,128)(2,1)S(1)} %collective-permute-done, bf16[16,128,128]{2,1,0:T(8,128)(2,1)S(1)} %convert_element_type.34, bf16[4,128,128]{2,1,0:T(8,128)(2,1)S(1)} %collective-permute-done.1), kind=kLoop, calls=%fused_computation.17 | loop fusion | flops 2795520 | bytes 1217536 | tf_op jit(solution)/shard_map/concatenate | solution.py:19
  14.0 0.7 broadcast_in_dim.12.cover_ref
  14.7 7.0 %shard_map.46 = bf16[16,64,128]{2,1,0:T(8,128)(2,1)} custom-call(bf16[24,70,128]{2,1,0:T(8,128)(2,1)} %fusion.18.src_ref, bf16[9,896,128]{2,1,0:T(8,128)(2,1)} %bitcast.23, bf16[16,64,128]{2,1,0:T(8,128)(2,1)} %bitcast.25, f32[64,128]{1,0:T(8,128)} %broadcast_in_dim.12.cover_ref), custom_call_target="tpu_custom_call" | custom-call | tf_op jit(solution)/shard_map/pallas_call | solution.py:324
  21.7 0.8 %slice_select_fusion = bf16[16,3,128]{2,1,0:T(4,128)(2,1)S(1)} fusion(bf16[16,64,128]{2,1,0:T(8,128)(2,1)} %shard_map.46, pred[]{:T(512)S(6)} %eq.11), kind=kLoop, calls=%fused_computation.25 | loop fusion | flops 6144 | bytes 36865 | tf_op jit(solution)/shard_map/jit(_where)/select_n | solution.py:361
  22.5 1.6 %collective-permute-start.2 = (bf16[16,3,128]{2,1,0:T(4,128)(2,1)S(1)}, bf16[16,3,128]{2,1,0:T(4,128)(2,1)S(1)}, u32[]{:S(2)}, u32[]{:S(2)}) collective-permute-start(bf16[16,3,128]{2,1,0:T(4,128)(2,1)S(1)} %slice_select_fusion), channel_id=1, source_target_pairs={{0,16},{16,0},{32,48},{48,32},{64,80},{80,64},{96,112},{112,96},{1... | collective-permute-start | bytes 36872 | tf_op jit(solution)/shard_map/ppermute | solution.py:37
  24.0 0.9 %fusion.8 = bf16[9,7,128,128]{3,1,2,0:T(8,128)(2,1)S(1)} fusion(bf16[9,7,25]{2,1,0:T(8,128)(2,1)S(1)} %rev.3), kind=kOutput, calls=%fused_computation.5 | convolution fusion | flops 53870592 | bytes 2067534 | tf_op jit(solution)/shard_map/abt,tpz->abpz/dot_general | solution.py:297
  24.9 1.9 %copy.7 = bf16[9,7,128,128]{3,2,1,0:T(8,128)(2,1)} copy(bf16[9,7,128,128]{3,1,2,0:T(8,128)(2,1)S(1)} %fusion.8) | data formatting | bytes 4128768 | tf_op jit(solution)/shard_map/convert_element_type | solution.py:297
  26.9 0.8 %pad_maximum_fusion.quot_ref = bf16[16,70,128]{2,1,0:T(8,128)(2,1)} fusion(bf16[16,3,128]{2,1,0:T(4,128)(2,1)S(1)} %get-tuple-element.10, bf16[16,64,128]{2,1,0:T(8,128)(2,1)S(1)} %copy-done.1, bf16[16,3,128]{2,1,0:T(4,128)(2,1)S(1)} %get-tuple-element.9), kind=kLoop, calls=%fused_computation.20 | loop fusion | flops 860160 | bytes 573440 | tf_op jit(solution)/shard_map/concatenate | solution.py:365
  27.7 46.3 %shard_map.47 = f32[16,128,128]{2,1,0:T(8,128)} custom-call(bf16[16,70,128]{2,1,0:T(8,128)(2,1)} %pad_maximum_fusion.quot_ref, bf16[9,896,128]{2,1,0:T(8,128)(2,1)} %bitcast.24, f32[64,128]{1,0:T(8,128)} %broadcast_in_dim.12.cover_ref), custom_call_target="tpu_custom_call" | custom-call | tf_op jit(solution)/shard_map/pallas_call | solution.py:266
  74.0 2.3 %mul.11 = f32[16,128,128]{2,1,0:T(8,128)} multiply(f32[16,128,128]{2,1,0:T(8,128)S(1)} %copy-done, f32[16,128,128]{2,1,0:T(8,128)} %shard_map.47) | non-fusion elementwise | flops 262144 | bytes 3145728 | tf_op jit(solution)/shard_map/mul | solution.py:366
  (9 shorter events, 0.1 us)
Async XLA Ops:
  1.3 11.6 %collective-permute-start = (bf16[4,128,128]{2,1,0:T(8,128)(2,1)S(1)}, bf16[4,128,128]{2,1,0:T(8,128)(2,1)S(1)}, u32[]{:S(2)}, u32[]{:S(2)}) collective-permute-start(bf16[4,128,128]{2,1,0:T(8,128)(2,1)S(1)} %get-tuple-element.8), channel_id=1, source_target_pairs={{0,1},{1,2},{2,3},{3,4},{4,5},{5,6},{6,7},{7,8},{8,9},{9,10},{10,1... | collective-permute-start | bytes 393224 | tf_op jit(solution)/shard_map/ppermute | solution.py:21
  4.5 8.4 %collective-permute-start.1 = (bf16[4,128,128]{2,1,0:T(8,128)(2,1)S(1)}, bf16[4,128,128]{2,1,0:T(8,128)(2,1)S(1)}, u32[]{:S(2)}, u32[]{:S(2)}) collective-permute-start(bf16[4,128,128]{2,1,0:T(8,128)(2,1)S(1)} %get-tuple-element.7), channel_id=1, source_target_pairs={{1,0},{2,1},{3,2},{4,3},{5,4},{6,5},{7,6},{8,7},{9,8},{10,9},{11,1... | collective-permute-start | bytes 393224 | tf_op jit(solution)/shard_map/ppermute | solution.py:23
  9.8 1.9 %copy-start.2 = (s32[8,1,4]{0,2,1:T(4,128)S(1)}, s32[8,1,4]{0,2,1:T(4,128)}, u32[]{:S(2)}) copy-start(s32[8,1,4]{0,2,1:T(4,128)} %param.7) | copy-start | bytes 388
  22.5 4.4 %collective-permute-start.2 = (bf16[16,3,128]{2,1,0:T(4,128)(2,1)S(1)}, bf16[16,3,128]{2,1,0:T(4,128)(2,1)S(1)}, u32[]{:S(2)}, u32[]{:S(2)}) collective-permute-start(bf16[16,3,128]{2,1,0:T(4,128)(2,1)S(1)} %slice_select_fusion), channel_id=1, source_target_pairs={{0,16},{16,0},{32,48},{48,32},{64,80},{80,64},{96,112},{112,96},{1... | collective-permute-start | bytes 36872 | tf_op jit(solution)/shard_map/ppermute | solution.py:37
  24.9 2.0 %copy-start.1 = (bf16[16,64,128]{2,1,0:T(8,128)(2,1)S(1)}, bf16[16,64,128]{2,1,0:T(8,128)(2,1)}, u32[]{:S(2)}) copy-start(bf16[16,64,128]{2,1,0:T(8,128)(2,1)} %shard_map.46) | copy-start | bytes 786436
  26.9 47.1 %copy-start = (f32[16,128,128]{2,1,0:T(8,128)S(1)}, f32[16,128,128]{2,1,0:T(8,128)}, u32[]{:S(2)}) copy-start(f32[16,128,128]{2,1,0:T(8,128)} %param.4) | copy-start | bytes 3145732

commit v15 on v14

--- a/solution.py
+++ b/solution.py
@@ -342,8 +342,7 @@
     part = group % shares
     y_start = part * share_w
     source = estimate.astype(jnp.bfloat16)
-    rimmed = with_halo(source, (("blk", 0),), rim_x)
-    padded = jnp.pad(rimmed, ((0, 0), (rim_y, rim_y), (0, 0)))
+    padded = jnp.pad(source, ((0, 0), (rim_y, rim_y), (0, 0)))
     spread = lax.dynamic_index_in_dim(point_spread, view_id, 0, keepdims=False)
     kernel = (spread / jnp.sum(spread)).astype(jnp.bfloat16)
     forward = band_table(kernel, depth)
@@ -352,9 +351,8 @@
     share_cover = lax.dynamic_slice_in_dim(coverage_row, part * share_blocks, share_blocks)
     cell_cover = jnp.repeat(share_cover, BY)[None, :, None]
     image = images[0]
-    region = lax.dynamic_slice(
-        padded, (0, y_start, 0), (slab_x + 2 * rim_x, share_w + 2 * rim_y, depth)
-    )
+    local_region = lax.dynamic_slice(padded, (0, y_start, 0), (slab_x, share_w + 2 * rim_y, depth))
+    region = with_halo(local_region, (("blk", 0),), rim_x)
     cover_plane = jnp.broadcast_to(cell_cover[0].astype(jnp.float32), (share_w, depth))
     quotient = quotient_of(region, forward, image, cover_plane)
     rim_zeros = jnp.zeros((slab_x, rim_y, depth), jnp.bfloat16)

time: 76.7 us -> 76.3 us (level)
  no operation moved by 1% of the time
where the time goes in v15:
time: 76.3 us; the launch traced here: 75.6 us
  Pallas kernels  52.9 us (69%)
  other arithmetic  8.54 us (11%)
  starting transfers between devices  6.6 us (9%)
  local copies, waits for them, and re-layouts  4.99 us (7%)
  matrix products  2.37 us (3%)
    pallas_call x1, Pallas kernels, product_gather(): pl.pallas_call(functools.partial(product_kernel, n, shares, width), out_s...  46 us
    pallas_call x1, Pallas kernels, quotient_of(): pl.pallas_call(functools.partial(conv_kernel, 4), out_shape=jax.ShapeDtyp...  6.99 us
    convert_element_type x2, local copies, waits for them, and re-layouts, band_table(): jnp.einsum('abt,tpz->abpz', kernel, onehot, preferred_element_type=jnp.fl...  3.87 us
    ppermute x1, starting transfers between devices, with_halo(): lax.ppermute(tail, axis, [(i, (i + 1) % count) for i in range(ends)])  3.12 us
    dot_general x2, matrix products, band_table(): jnp.einsum('abt,tpz->abpz', kernel, onehot, preferred_element_type=jnp.fl...  2.37 us
    mul x1, other arithmetic, local(): estimate * product_gather(extended, backward, cover_plane, estimate, shar...  2.31 us
    ppermute x1, starting transfers between devices, with_halo(): lax.ppermute(head, axis, [((i + 1) % count, i) for i in range(ends)])  2.16 us
    reduce_sum x1, other arithmetic, local(): kernel = (spread / jnp.sum(spread)).astype(jnp.bfloat16)  1.63 us
  transfers between devices with their start and end apart: 3, of which 0 were waited for; matrix products, arithmetic and copies ran while one was open for 12% of the time, Pallas kernels for 0%

profile of v15, /device:TPU:71, one launch (start us, length us, event | category | flops | bytes accessed | tf_op | source)
XLA Modules:
  0.0 75.6 jit_solution(2177125447393469046)
XLA Ops:
  0.0 1.3 %convert_element_type.34 = bf16[16,128,128]{2,1,0:T(8,128)(2,1)S(1)} convert(f32[16,128,128]{2,1,0:T(8,128)} %param.4) | non-fusion elementwise | flops 262144 | bytes 1572864 | tf_op jit(solution)/shard_map/convert_element_type | solution.py:344
  1.3 0.1 pad_dynamic-slice_fusion.1
  1.4 3.1 %collective-permute-start = (bf16[4,70,128]{2,1,0:T(8,128)(2,1)S(1)}, bf16[4,70,128]{2,1,0:T(8,128)(2,1)S(1)}, u32[]{:S(2)}, u32[]{:S(2)}) collective-permute-start(bf16[4,70,128]{2,1,0:T(8,128)(2,1)S(1)} %get-tuple-element.7), channel_id=1, source_target_pairs={{0,1},{1,2},{2,3},{3,4},{4,5},{5,6},{6,7},{7,8},{8,9},{9,10},{10,1... | collective-permute-start | bytes 215048 | tf_op jit(solution)/shard_map/ppermute | solution.py:21
  4.5 2.2 %collective-permute-start.1 = (bf16[4,70,128]{2,1,0:T(8,128)(2,1)S(1)}, bf16[4,70,128]{2,1,0:T(8,128)(2,1)S(1)}, u32[]{:S(2)}, u32[]{:S(2)}) collective-permute-start(bf16[4,70,128]{2,1,0:T(8,128)(2,1)S(1)} %get-tuple-element.8), channel_id=1, source_target_pairs={{1,0},{2,1},{3,2},{4,3},{5,4},{6,5},{7,6},{8,7},{9,8},{10,9},{11,1... | collective-permute-start | bytes 215048 | tf_op jit(solution)/shard_map/ppermute | solution.py:23
  6.7 1.6 %fusion.21 = (f32[]{:T(128)}, f32[1,9,7,25]{3,0,2,1:T(1,128)S(1)}) fusion(f32[8,9,7,25]{3,0,2,1:T(8,128)} %param.6, s32[]{:T(128)S(6)} %select_n.48), kind=kLoop, calls=%fused_computation.27 | loop fusion | flops 1574 | bytes 12608 | tf_op jit(solution)/shard_map/reduce_sum | solution.py:347
  8.3 1.5 %fusion.5 = bf16[9,7,128,128]{3,1,2,0:T(8,128)(2,1)S(1)} fusion(f32[1,9,7,25]{3,0,2,1:T(1,128)S(1)} %get-tuple-element.6, f32[]{:T(128)} %get-tuple-element.5), kind=kOutput, calls=%fused_computation.4 | convolution fusion | flops 53873744 | bytes 2070688 | tf_op jit(solution)/shard_map/abt,tpz->abpz/dot_general | solution.py:297
  9.9 0.7 fusion.20
  10.5 1.9 %copy.6 = bf16[9,7,128,128]{3,2,1,0:T(8,128)(2,1)} copy(bf16[9,7,128,128]{3,1,2,0:T(8,128)(2,1)S(1)} %fusion.5) | data formatting | bytes 4128768 | tf_op jit(solution)/shard_map/convert_element_type | solution.py:297
  12.5 0.1 dynamic-slice_compare_fusion
  12.5 0.1 fusion.16
  12.7 0.1 broadcast_in_dim.11
  12.7 0.1 convert_element_type.40
  12.8 0.1 rev.3
  12.9 0.1 pad_dynamic-slice_fusion.2
  13.1 0.8 %pad_maximum_fusion.src_ref = bf16[24,70,128]{2,1,0:T(8,128)(2,1)} fusion(bf16[4,70,128]{2,1,0:T(8,128)(2,1)S(1)} %collective-permute-done.1, bf16[16,70,128]{2,1,0:T(8,128)(2,1)S(1)} %pad_dynamic-slice_fusion.2, bf16[4,70,128]{2,1,0:T(8,128)(2,1)S(1)} %collective-permute-done), kind=kLoop, calls=%fused_computation.11 | loop fusion | flops 430080 | bytes 860160 | tf_op jit(solution)/shard_map/concatenate | solution.py:19
  13.9 0.7 broadcast_in_dim.12.cover_ref
  14.6 7.0 %shard_map.46 = bf16[16,64,128]{2,1,0:T(8,128)(2,1)} custom-call(bf16[24,70,128]{2,1,0:T(8,128)(2,1)} %pad_maximum_fusion.src_ref, bf16[9,896,128]{2,1,0:T(8,128)(2,1)} %bitcast.23, bf16[16,64,128]{2,1,0:T(8,128)(2,1)} %bitcast.25, f32[64,128]{1,0:T(8,128)} %broadcast_in_dim.12.cover_ref), custom_call_target="tpu_custom_call" | custom-call | tf_op jit(solution)/shard_map/pallas_call | solution.py:324
  21.6 0.8 %slice_select_fusion = bf16[16,3,128]{2,1,0:T(4,128)(2,1)S(1)} fusion(bf16[16,64,128]{2,1,0:T(8,128)(2,1)} %shard_map.46, pred[]{:T(512)S(6)} %eq.11), kind=kLoop, calls=%fused_computation.17 | loop fusion | flops 6144 | bytes 36865 | tf_op jit(solution)/shard_map/jit(_where)/select_n | solution.py:359
  22.4 1.3 %collective-permute-start.2 = (bf16[16,3,128]{2,1,0:T(4,128)(2,1)S(1)}, bf16[16,3,128]{2,1,0:T(4,128)(2,1)S(1)}, u32[]{:S(2)}, u32[]{:S(2)}) collective-permute-start(bf16[16,3,128]{2,1,0:T(4,128)(2,1)S(1)} %slice_select_fusion), channel_id=1, source_target_pairs={{0,16},{16,0},{32,48},{48,32},{64,80},{80,64},{96,112},{112,96},{1... | collective-permute-start | bytes 36872 | tf_op jit(solution)/shard_map/ppermute | solution.py:37
  23.7 0.9 %fusion.8 = bf16[9,7,128,128]{3,1,2,0:T(8,128)(2,1)S(1)} fusion(bf16[9,7,25]{2,1,0:T(8,128)(2,1)S(1)} %rev.3), kind=kOutput, calls=%fused_computation.5 | convolution fusion | flops 53870592 | bytes 2067534 | tf_op jit(solution)/shard_map/abt,tpz->abpz/dot_general | solution.py:297
  24.6 1.9 %copy.7 = bf16[9,7,128,128]{3,2,1,0:T(8,128)(2,1)} copy(bf16[9,7,128,128]{3,1,2,0:T(8,128)(2,1)S(1)} %fusion.8) | data formatting | bytes 4128768 | tf_op jit(solution)/shard_map/convert_element_type | solution.py:297
  26.5 0.8 %pad_maximum_fusion.1.quot_ref = bf16[16,70,128]{2,1,0:T(8,128)(2,1)} fusion(bf16[16,3,128]{2,1,0:T(4,128)(2,1)S(1)} %get-tuple-element.10, bf16[16,64,128]{2,1,0:T(8,128)(2,1)S(1)} %copy-done.1, bf16[16,3,128]{2,1,0:T(4,128)(2,1)S(1)} %get-tuple-element.9), kind=kLoop, calls=%fused_computation.12 | loop fusion | flops 860160 | bytes 573440 | tf_op jit(solution)/shard_map/concatenate | solution.py:363
  27.3 46.0 %shard_map.47 = f32[16,128,128]{2,1,0:T(8,128)} custom-call(bf16[16,70,128]{2,1,0:T(8,128)(2,1)} %pad_maximum_fusion.1.quot_ref, bf16[9,896,128]{2,1,0:T(8,128)(2,1)} %bitcast.24, f32[64,128]{1,0:T(8,128)} %broadcast_in_dim.12.cover_ref), custom_call_target="tpu_custom_call" | custom-call | tf_op jit(solution)/shard_map/pallas_call | solution.py:266
  73.3 2.3 %mul.11 = f32[16,128,128]{2,1,0:T(8,128)} multiply(f32[16,128,128]{2,1,0:T(8,128)S(1)} %copy-done, f32[16,128,128]{2,1,0:T(8,128)} %shard_map.47) | non-fusion elementwise | flops 262144 | bytes 3145728 | tf_op jit(solution)/shard_map/mul | solution.py:364
  (10 shorter events, 0.0 us)
Async XLA Ops:
  1.4 11.7 %collective-permute-start = (bf16[4,70,128]{2,1,0:T(8,128)(2,1)S(1)}, bf16[4,70,128]{2,1,0:T(8,128)(2,1)S(1)}, u32[]{:S(2)}, u32[]{:S(2)}) collective-permute-start(bf16[4,70,128]{2,1,0:T(8,128)(2,1)S(1)} %get-tuple-element.7), channel_id=1, source_target_pairs={{0,1},{1,2},{2,3},{3,4},{4,5},{5,6},{6,7},{7,8},{8,9},{9,10},{10,1... | collective-permute-start | bytes 215048 | tf_op jit(solution)/shard_map/ppermute | solution.py:21
  4.5 8.5 %collective-permute-start.1 = (bf16[4,70,128]{2,1,0:T(8,128)(2,1)S(1)}, bf16[4,70,128]{2,1,0:T(8,128)(2,1)S(1)}, u32[]{:S(2)}, u32[]{:S(2)}) collective-permute-start(bf16[4,70,128]{2,1,0:T(8,128)(2,1)S(1)} %get-tuple-element.8), channel_id=1, source_target_pairs={{1,0},{2,1},{3,2},{4,3},{5,4},{6,5},{7,6},{8,7},{9,8},{10,9},{11,1... | collective-permute-start | bytes 215048 | tf_op jit(solution)/shard_map/ppermute | solution.py:23
  10.5 1.9 %copy-start.2 = (s32[8,1,4]{0,2,1:T(4,128)S(1)}, s32[8,1,4]{0,2,1:T(4,128)}, u32[]{:S(2)}) copy-start(s32[8,1,4]{0,2,1:T(4,128)} %param.7) | copy-start | bytes 388
  22.4 4.1 %collective-permute-start.2 = (bf16[16,3,128]{2,1,0:T(4,128)(2,1)S(1)}, bf16[16,3,128]{2,1,0:T(4,128)(2,1)S(1)}, u32[]{:S(2)}, u32[]{:S(2)}) collective-permute-start(bf16[16,3,128]{2,1,0:T(4,128)(2,1)S(1)} %slice_select_fusion), channel_id=1, source_target_pairs={{0,16},{16,0},{32,48},{48,32},{64,80},{80,64},{96,112},{112,96},{1... | collective-permute-start | bytes 36872 | tf_op jit(solution)/shard_map/ppermute | solution.py:37
  24.5 2.0 %copy-start.1 = (bf16[16,64,128]{2,1,0:T(8,128)(2,1)S(1)}, bf16[16,64,128]{2,1,0:T(8,128)(2,1)}, u32[]{:S(2)}) copy-start(bf16[16,64,128]{2,1,0:T(8,128)(2,1)} %shard_map.46) | copy-start | bytes 786436
  26.5 46.8 %copy-start = (f32[16,128,128]{2,1,0:T(8,128)S(1)}, f32[16,128,128]{2,1,0:T(8,128)}, u32[]{:S(2)}) copy-start(f32[16,128,128]{2,1,0:T(8,128)} %param.4) | copy-start | bytes 3145732

commit v16 on v14

--- a/solution.py
+++ b/solution.py
@@ -294,9 +294,11 @@
     onehot = (offset + rim_z == lax.broadcasted_iota(jnp.int32, shape_three, 0)).astype(
         jnp.bfloat16
     )
-    banded = jnp.einsum("abt,tpz->abpz", kernel, onehot, preferred_element_type=jnp.float32).astype(
-        jnp.bfloat16
-    )
+    banded = jnp.dot(
+        kernel.reshape(taps_x * taps_y, taps_z),
+        onehot.reshape(taps_z, depth * depth),
+        preferred_element_type=jnp.float32,
+    ).astype(jnp.bfloat16)
     return banded.reshape(taps_x, taps_y * depth, depth)
 
 

time: 76.7 us -> 79.1 us (1.031)
  other arithmetic: 8.81 us -> 10.6 us
  local copies, waits for them, and re-layouts: 4.85 us -> 6.61 us
  matrix products: 2.37 us -> 1.4 us
    reshape x0 -> x3, local copies, waits for them, and re-layouts: none -> 5.07 us  [the longest x2 5.05 us: band_table(): return banded.reshape(taps_x, taps_y * depth, depth)]
    convert_element_type x2 -> x1, local copies, waits for them, and re-layouts: 3.87 us -> 0.02 us  [local(): kernel = (spread / jnp.sum(spread)).astype(jnp.bfloat16)]
    dot_general x2, matrix products: 2.37 us -> 1.4 us  [band_table(): jnp.dot(kernel.reshape(taps_x * taps_y, taps_z), onehot.reshape(taps_z, d...]
    concatenate x1, other arithmetic: 1.1 us -> 1.98 us  [with_halo(): jnp.concatenate([lax.ppermute(tail, axis, [(i, (i + 1) % count) for i in...]
  transfers between devices with their start and end apart: 3 -> 3, of which waited for: 0 -> 0; matrix products, arithmetic and copies ran while one was open for 12% -> 14% of each run, Pallas kernels for 0% -> 0%
where the time goes in v16:
time: 79.1 us; the launch traced here: 78.4 us
  Pallas kernels  53 us (67%)
  other arithmetic  10.6 us (13%)
  local copies, waits for them, and re-layouts  6.61 us (8%)
  starting transfers between devices  6.61 us (8%)
  matrix products  1.4 us (2%)
    pallas_call x1, Pallas kernels, product_gather(): pl.pallas_call(functools.partial(product_kernel, n, shares, width), out_s...  46 us
    pallas_call x1, Pallas kernels, quotient_of(): pl.pallas_call(functools.partial(conv_kernel, 4), out_shape=jax.ShapeDtyp...  6.99 us
    reshape x2, local copies, waits for them, and re-layouts, band_table(): return banded.reshape(taps_x, taps_y * depth, depth)  5.05 us
    ppermute x1, starting transfers between devices, with_halo(): lax.ppermute(tail, axis, [(i, (i + 1) % count) for i in range(ends)])  3.12 us
    mul x1, other arithmetic, local(): estimate * product_gather(extended, backward, cover_plane, estimate, shar...  2.31 us
    ppermute x1, starting transfers between devices, with_halo(): lax.ppermute(head, axis, [((i + 1) % count, i) for i in range(ends)])  2.16 us
    concatenate x1, other arithmetic, with_halo(): jnp.concatenate([lax.ppermute(tail, axis, [(i, (i + 1) % count) for i in...  1.98 us
    reduce_sum x1, other arithmetic, local(): kernel = (spread / jnp.sum(spread)).astype(jnp.bfloat16)  1.63 us
  transfers between devices with their start and end apart: 3, of which 0 were waited for; matrix products, arithmetic and copies ran while one was open for 14% of the time, Pallas kernels for 0%

profile of v16, /device:TPU:71, one launch (start us, length us, event | category | flops | bytes accessed | tf_op | source)
XLA Modules:
  0.0 78.4 jit_solution(2125646497099240364)
XLA Ops:
  0.0 1.3 %convert_element_type.38 = bf16[16,128,128]{2,1,0:T(8,128)(2,1)S(1)} convert(f32[16,128,128]{2,1,0:T(8,128)} %param.4) | non-fusion elementwise | flops 262144 | bytes 1572864 | tf_op jit(solution)/shard_map/convert_element_type | solution.py:346
  1.3 3.1 %collective-permute-start = (bf16[4,128,128]{2,1,0:T(8,128)(2,1)S(1)}, bf16[4,128,128]{2,1,0:T(8,128)(2,1)}, u32[]{:S(2)}, u32[]{:S(2)}) collective-permute-start(bf16[4,128,128]{2,1,0:T(8,128)(2,1)S(1)} %get-tuple-element.8), channel_id=1, source_target_pairs={{0,1},{1,2},{2,3},{3,4},{4,5},{5,6},{6,7},{7,8},{8,9},{9,10},{10,1... | collective-permute-start | bytes 393224 | tf_op jit(solution)/shard_map/ppermute | solution.py:21
  4.5 2.2 %collective-permute-start.1 = (bf16[4,128,128]{2,1,0:T(8,128)(2,1)S(1)}, bf16[4,128,128]{2,1,0:T(8,128)(2,1)}, u32[]{:S(2)}, u32[]{:S(2)}) collective-permute-start(bf16[4,128,128]{2,1,0:T(8,128)(2,1)S(1)} %get-tuple-element.7), channel_id=1, source_target_pairs={{1,0},{2,1},{3,2},{4,3},{5,4},{6,5},{7,6},{8,7},{9,8},{10,9},{11,1... | collective-permute-start | bytes 393224 | tf_op jit(solution)/shard_map/ppermute | solution.py:23
  6.7 1.6 %fusion.10 = (f32[]{:T(128)}, f32[1,9,7,25]{3,0,2,1:T(1,128)S(1)}) fusion(f32[8,9,7,25]{3,0,2,1:T(8,128)} %param.6, s32[]{:T(128)S(6)} %select_n.48), kind=kLoop, calls=%fused_computation.26 | loop fusion | flops 1574 | bytes 12608 | tf_op jit(solution)/shard_map/reduce_sum | solution.py:350
  8.3 0.7 fusion.8
  9.0 0.2 iota_compare_fusion
  9.3 0.5 copy.8
  9.8 0.7 convolution_convert_fusion.1
  10.5 2.5 %reshape.99.band_ref = bf16[9,896,128]{2,1,0:T(8,128)(2,1)} reshape(bf16[63,16384]{1,0:T(8,128)(2,1)S(1)} %convolution_convert_fusion.1) | data formatting | bytes 4128768 | tf_op jit(solution)/shard_map/reshape | solution.py:302
  13.1 0.1 dynamic-slice_compare_fusion
  13.1 0.1 fusion.9
  13.3 0.1 convert_element_type.44
  13.4 0.7 fusion.16
  14.1 0.1 rev.3
  14.2 2.0 %fusion.5.src_ref = bf16[24,70,128]{2,1,0:T(8,128)(2,1)} fusion(s32[]{:T(128)S(6)} %select_n.46, bf16[4,128,128]{2,1,0:T(8,128)(2,1)} %collective-permute-done, bf16[16,128,128]{2,1,0:T(8,128)(2,1)S(1)} %convert_element_type.38, bf16[4,128,128]{2,1,0:T(8,128)(2,1)} %collective-permute-done.1), kind=kLoop, calls=%fused_computation.12 | loop fusion | flops 2795520 | bytes 1217536 | tf_op jit(solution)/shard_map/concatenate | solution.py:19
  16.2 0.7 broadcast_in_dim.12.cover_ref
  16.9 7.0 %shard_map.46 = bf16[16,64,128]{2,1,0:T(8,128)(2,1)} custom-call(bf16[24,70,128]{2,1,0:T(8,128)(2,1)} %fusion.5.src_ref, bf16[9,896,128]{2,1,0:T(8,128)(2,1)} %reshape.99.band_ref, bf16[16,64,128]{2,1,0:T(8,128)(2,1)} %bitcast.13, f32[64,128]{1,0:T(8,128)} %broadcast_in_dim.12.cover_ref), custom_call_target="tpu_custom_call" | custom-call | tf_op jit(solution)/shard_map/pallas_call | solution.py:326
  23.9 0.8 %slice_select_fusion = bf16[16,3,128]{2,1,0:T(4,128)(2,1)S(1)} fusion(bf16[16,64,128]{2,1,0:T(8,128)(2,1)} %shard_map.46, pred[]{:T(512)S(6)} %eq.27), kind=kLoop, calls=%fused_computation.19 | loop fusion | flops 6144 | bytes 36865 | tf_op jit(solution)/shard_map/jit(_where)/select_n | solution.py:363
  24.7 1.3 %collective-permute-start.2 = (bf16[16,3,128]{2,1,0:T(4,128)(2,1)S(1)}, bf16[16,3,128]{2,1,0:T(4,128)(2,1)S(1)}, u32[]{:S(2)}, u32[]{:S(2)}) collective-permute-start(bf16[16,3,128]{2,1,0:T(4,128)(2,1)S(1)} %slice_select_fusion), channel_id=1, source_target_pairs={{0,16},{16,0},{32,48},{48,32},{64,80},{80,64},{96,112},{112,96},{1... | collective-permute-start | bytes 36872 | tf_op jit(solution)/shard_map/ppermute | solution.py:37
  26.0 0.7 convolution_convert_fusion
  26.7 2.5 %reshape.101.band_ref = bf16[9,896,128]{2,1,0:T(8,128)(2,1)} reshape(bf16[63,16384]{1,0:T(8,128)(2,1)S(1)} %convolution_convert_fusion) | data formatting | bytes 4128768 | tf_op jit(solution)/shard_map/reshape | solution.py:302
  29.3 0.8 %pad_maximum_fusion.quot_ref = bf16[16,70,128]{2,1,0:T(8,128)(2,1)} fusion(bf16[16,3,128]{2,1,0:T(4,128)(2,1)S(1)} %get-tuple-element.10, bf16[16,64,128]{2,1,0:T(8,128)(2,1)S(1)} %copy-done.1, bf16[16,3,128]{2,1,0:T(4,128)(2,1)S(1)} %get-tuple-element.9), kind=kLoop, calls=%fused_computation.15 | loop fusion | flops 860160 | bytes 573440 | tf_op jit(solution)/shard_map/concatenate | solution.py:367
  30.1 46.0 %shard_map.47 = f32[16,128,128]{2,1,0:T(8,128)} custom-call(bf16[16,70,128]{2,1,0:T(8,128)(2,1)} %pad_maximum_fusion.quot_ref, bf16[9,896,128]{2,1,0:T(8,128)(2,1)} %reshape.101.band_ref, f32[64,128]{1,0:T(8,128)} %broadcast_in_dim.12.cover_ref), custom_call_target="tpu_custom_call" | custom-call | tf_op jit(solution)/shard_map/pallas_call | solution.py:266
  76.1 2.3 %mul.11 = f32[16,128,128]{2,1,0:T(8,128)} multiply(f32[16,128,128]{2,1,0:T(8,128)S(1)} %copy-done, f32[16,128,128]{2,1,0:T(8,128)} %shard_map.47) | non-fusion elementwise | flops 262144 | bytes 3145728 | tf_op jit(solution)/shard_map/mul | solution.py:368
  (16 shorter events, 0.3 us)
Async XLA Ops:
  1.3 12.9 %collective-permute-start = (bf16[4,128,128]{2,1,0:T(8,128)(2,1)S(1)}, bf16[4,128,128]{2,1,0:T(8,128)(2,1)}, u32[]{:S(2)}, u32[]{:S(2)}) collective-permute-start(bf16[4,128,128]{2,1,0:T(8,128)(2,1)S(1)} %get-tuple-element.8), channel_id=1, source_target_pairs={{0,1},{1,2},{2,3},{3,4},{4,5},{5,6},{6,7},{7,8},{8,9},{9,10},{10,1... | collective-permute-start | bytes 393224 | tf_op jit(solution)/shard_map/ppermute | solution.py:21
  4.5 9.8 %collective-permute-start.1 = (bf16[4,128,128]{2,1,0:T(8,128)(2,1)S(1)}, bf16[4,128,128]{2,1,0:T(8,128)(2,1)}, u32[]{:S(2)}, u32[]{:S(2)}) collective-permute-start(bf16[4,128,128]{2,1,0:T(8,128)(2,1)S(1)} %get-tuple-element.7), channel_id=1, source_target_pairs={{1,0},{2,1},{3,2},{4,3},{5,4},{6,5},{7,6},{8,7},{9,8},{10,9},{11,1... | collective-permute-start | bytes 393224 | tf_op jit(solution)/shard_map/ppermute | solution.py:23
  10.5 2.5 %copy-start.2 = (s32[8,1,4]{0,2,1:T(4,128)S(1)}, s32[8,1,4]{0,2,1:T(4,128)}, u32[]{:S(2)}) copy-start(s32[8,1,4]{0,2,1:T(4,128)} %param.7) | copy-start | bytes 388
  24.7 4.6 %collective-permute-start.2 = (bf16[16,3,128]{2,1,0:T(4,128)(2,1)S(1)}, bf16[16,3,128]{2,1,0:T(4,128)(2,1)S(1)}, u32[]{:S(2)}, u32[]{:S(2)}) collective-permute-start(bf16[16,3,128]{2,1,0:T(4,128)(2,1)S(1)} %slice_select_fusion), channel_id=1, source_target_pairs={{0,16},{16,0},{32,48},{48,32},{64,80},{80,64},{96,112},{112,96},{1... | collective-permute-start | bytes 36872 | tf_op jit(solution)/shard_map/ppermute | solution.py:37
  26.7 2.6 %copy-start.1 = (bf16[16,64,128]{2,1,0:T(8,128)(2,1)S(1)}, bf16[16,64,128]{2,1,0:T(8,128)(2,1)}, u32[]{:S(2)}) copy-start(bf16[16,64,128]{2,1,0:T(8,128)(2,1)} %shard_map.46) | copy-start | bytes 786436
  29.3 46.8 %copy-start = (f32[16,128,128]{2,1,0:T(8,128)S(1)}, f32[16,128,128]{2,1,0:T(8,128)}, u32[]{:S(2)}) copy-start(f32[16,128,128]{2,1,0:T(8,128)} %param.4) | copy-start | bytes 3145732

commit v17 on v14

--- a/solution.py
+++ b/solution.py
@@ -345,7 +345,8 @@
     rimmed = with_halo(source, (("blk", 0),), rim_x)
     padded = jnp.pad(rimmed, ((0, 0), (rim_y, rim_y), (0, 0)))
     spread = lax.dynamic_index_in_dim(point_spread, view_id, 0, keepdims=False)
-    kernel = (spread / jnp.sum(spread)).astype(jnp.bfloat16)
+    totals = jnp.sum(point_spread, axis=(1, 2, 3))
+    kernel = (spread / lax.dynamic_index_in_dim(totals, view_id, 0, keepdims=False)).astype(jnp.bfloat16)
     forward = band_table(kernel, depth)
     backward = band_table(kernel[::-1, ::-1, ::-1], depth)
     coverage_row = lax.dynamic_index_in_dim(covered[:, 0, :], view_id, 0, keepdims=False) > 0

time: 76.7 us -> 76.7 us (level)
  other arithmetic: 8.81 us -> 7.41 us
    reduce_sum x1, other arithmetic: 1.63 us -> 0.18 us  [local(): totals = jnp.sum(point_spread, axis=(1, 2, 3))]
  transfers between devices with their start and end apart: 3 -> 3, of which waited for: 0 -> 1; matrix products, arithmetic and copies ran while one was open for 12% -> 11% of each run, Pallas kernels for 0% -> 0%
where the time goes in v17:
time: 76.7 us; the launch traced here: 76 us
  Pallas kernels  52.9 us (69%)
  starting transfers between devices  7.47 us (10%)
  other arithmetic  7.41 us (10%)
  local copies, waits for them, and re-layouts  5.46 us (7%)
  matrix products  2.37 us (3%)
    pallas_call x1, Pallas kernels, product_gather(): pl.pallas_call(functools.partial(product_kernel, n, shares, width), out_s...  45.9 us
    pallas_call x1, Pallas kernels, quotient_of(): pl.pallas_call(functools.partial(conv_kernel, 4), out_shape=jax.ShapeDtyp...  6.99 us
    convert_element_type x2, local copies, waits for them, and re-layouts, band_table(): jnp.einsum('abt,tpz->abpz', kernel, onehot, preferred_element_type=jnp.fl...  3.87 us
    ppermute x1, starting transfers between devices, with_halo(): lax.ppermute(tail, axis, [(i, (i + 1) % count) for i in range(ends)])  3.12 us
    dot_general x2, matrix products, band_table(): jnp.einsum('abt,tpz->abpz', kernel, onehot, preferred_element_type=jnp.fl...  2.37 us
    mul x1, other arithmetic, local(): estimate * product_gather(extended, backward, cover_plane, estimate, shar...  2.31 us
    ppermute x1, starting transfers between devices, swapped(): return lax.ppermute(block, axis, route)  2.19 us
    ppermute x1, starting transfers between devices, with_halo(): lax.ppermute(head, axis, [((i + 1) % count, i) for i in range(ends)])  2.16 us
  transfers between devices with their start and end apart: 3, of which 1 were waited for; matrix products, arithmetic and copies ran while one was open for 11% of the time, Pallas kernels for 0%

profile of v17, /device:TPU:71, one launch (start us, length us, event | category | flops | bytes accessed | tf_op | source)
XLA Modules:
  0.0 76.0 jit_solution(14650292295643632447)
XLA Ops:
  0.0 1.4 %convert_element_type.34 = bf16[16,128,128]{2,1,0:T(8,128)(2,1)S(1)} convert(f32[16,128,128]{2,1,0:T(8,128)} %param.4) | non-fusion elementwise | flops 262144 | bytes 1572864 | tf_op jit(solution)/shard_map/convert_element_type | solution.py:344
  1.4 3.1 %collective-permute-start = (bf16[4,128,128]{2,1,0:T(8,128)(2,1)S(1)}, bf16[4,128,128]{2,1,0:T(8,128)(2,1)S(1)}, u32[]{:S(2)}, u32[]{:S(2)}) collective-permute-start(bf16[4,128,128]{2,1,0:T(8,128)(2,1)S(1)} %get-tuple-element.6), channel_id=1, source_target_pairs={{0,1},{1,2},{2,3},{3,4},{4,5},{5,6},{6,7},{7,8},{8,9},{9,10},{10,1... | collective-permute-start | bytes 393224 | tf_op jit(solution)/shard_map/ppermute | solution.py:21
  4.5 2.2 %collective-permute-start.1 = (bf16[4,128,128]{2,1,0:T(8,128)(2,1)S(1)}, bf16[4,128,128]{2,1,0:T(8,128)(2,1)S(1)}, u32[]{:S(2)}, u32[]{:S(2)}) collective-permute-start(bf16[4,128,128]{2,1,0:T(8,128)(2,1)S(1)} %get-tuple-element.5), channel_id=1, source_target_pairs={{1,0},{2,1},{3,2},{4,3},{5,4},{6,5},{7,6},{8,7},{9,8},{10,9},{11,1... | collective-permute-start | bytes 393224 | tf_op jit(solution)/shard_map/ppermute | solution.py:23
  6.8 0.2 reduce_sum.9
  6.9 0.6 dynamic_slice.20
  7.5 1.5 %fusion.5 = bf16[9,7,128,128]{3,1,2,0:T(8,128)(2,1)S(1)} fusion(f32[1,9,7,25]{3,0,2,1:T(1,128)S(1)} %constant_dynamic-slice_fusion, f32[]{:T(128)} %bitcast), kind=kOutput, calls=%fused_computation.4 | convolution fusion | flops 53873744 | bytes 2070688 | tf_op jit(solution)/shard_map/abt,tpz->abpz/dot_general | solution.py:297
  9.1 1.9 %copy.6 = bf16[9,7,128,128]{3,2,1,0:T(8,128)(2,1)} copy(bf16[9,7,128,128]{3,1,2,0:T(8,128)(2,1)S(1)} %fusion.5) | data formatting | bytes 4128768 | tf_op jit(solution)/shard_map/convert_element_type | solution.py:297
  11.0 0.1 dynamic-slice_compare_fusion
  11.1 0.1 fusion.24
  11.2 0.1 broadcast_in_dim.11
  11.3 0.1 convert_element_type.40
  11.4 0.7 fusion.28
  12.0 0.1 rev.3
  12.1 0.2 collective-permute-done.1
  12.3 1.1 %fusion.18.src_ref = bf16[24,70,128]{2,1,0:T(8,128)(2,1)} fusion(s32[]{:T(128)S(6)} %select_n.48, bf16[4,128,128]{2,1,0:T(8,128)(2,1)S(1)} %collective-permute-done, bf16[16,128,128]{2,1,0:T(8,128)(2,1)S(1)} %convert_element_type.34, bf16[4,128,128]{2,1,0:T(8,128)(2,1)S(1)} %collective-permute-done.1), kind=kLoop, calls=%fused_computation.17 | loop fusion | flops 2795520 | bytes 1217536 | tf_op jit(solution)/shard_map/concatenate | solution.py:19
  13.4 0.7 broadcast_in_dim.12.cover_ref
  14.1 7.0 %shard_map.46 = bf16[16,64,128]{2,1,0:T(8,128)(2,1)} custom-call(bf16[24,70,128]{2,1,0:T(8,128)(2,1)} %fusion.18.src_ref, bf16[9,896,128]{2,1,0:T(8,128)(2,1)} %bitcast.24, bf16[16,64,128]{2,1,0:T(8,128)(2,1)} %bitcast.26, f32[64,128]{1,0:T(8,128)} %broadcast_in_dim.12.cover_ref), custom_call_target="tpu_custom_call" | custom-call | tf_op jit(solution)/shard_map/pallas_call | solution.py:324
  21.1 0.8 %slice_select_fusion = bf16[16,3,128]{2,1,0:T(4,128)(2,1)S(1)} fusion(bf16[16,64,128]{2,1,0:T(8,128)(2,1)} %shard_map.46, pred[]{:T(512)S(6)} %eq.11), kind=kLoop, calls=%fused_computation.25 | loop fusion | flops 6144 | bytes 36865 | tf_op jit(solution)/shard_map/jit(_where)/select_n | solution.py:362
  21.9 2.2 %collective-permute-start.2 = (bf16[16,3,128]{2,1,0:T(4,128)(2,1)S(1)}, bf16[16,3,128]{2,1,0:T(4,128)(2,1)S(1)}, u32[]{:S(2)}, u32[]{:S(2)}) collective-permute-start(bf16[16,3,128]{2,1,0:T(4,128)(2,1)S(1)} %slice_select_fusion), channel_id=1, source_target_pairs={{0,16},{16,0},{32,48},{48,32},{64,80},{80,64},{96,112},{112,96},{1... | collective-permute-start | bytes 36872 | tf_op jit(solution)/shard_map/ppermute | solution.py:37
  24.1 0.9 %fusion.8 = bf16[9,7,128,128]{3,1,2,0:T(8,128)(2,1)S(1)} fusion(bf16[9,7,25]{2,1,0:T(8,128)(2,1)S(1)} %rev.3), kind=kOutput, calls=%fused_computation.5 | convolution fusion | flops 53870592 | bytes 2067534 | tf_op jit(solution)/shard_map/abt,tpz->abpz/dot_general | solution.py:297
  25.0 1.9 %copy.7 = bf16[9,7,128,128]{3,2,1,0:T(8,128)(2,1)} copy(bf16[9,7,128,128]{3,1,2,0:T(8,128)(2,1)S(1)} %fusion.8) | data formatting | bytes 4128768 | tf_op jit(solution)/shard_map/convert_element_type | solution.py:297
  26.9 0.8 %pad_maximum_fusion.quot_ref = bf16[16,70,128]{2,1,0:T(8,128)(2,1)} fusion(bf16[16,3,128]{2,1,0:T(4,128)(2,1)S(1)} %get-tuple-element.8, bf16[16,64,128]{2,1,0:T(8,128)(2,1)S(1)} %copy-done.1, bf16[16,3,128]{2,1,0:T(4,128)(2,1)S(1)} %get-tuple-element.7), kind=kLoop, calls=%fused_computation.20 | loop fusion | flops 860160 | bytes 573440 | tf_op jit(solution)/shard_map/concatenate | solution.py:366
  27.8 45.9 %shard_map.47 = f32[16,128,128]{2,1,0:T(8,128)} custom-call(bf16[16,70,128]{2,1,0:T(8,128)(2,1)} %pad_maximum_fusion.quot_ref, bf16[9,896,128]{2,1,0:T(8,128)(2,1)} %bitcast.25, f32[64,128]{1,0:T(8,128)} %broadcast_in_dim.12.cover_ref), custom_call_target="tpu_custom_call" | custom-call | tf_op jit(solution)/shard_map/pallas_call | solution.py:266
  73.7 2.3 %mul.11 = f32[16,128,128]{2,1,0:T(8,128)} multiply(f32[16,128,128]{2,1,0:T(8,128)S(1)} %copy-done, f32[16,128,128]{2,1,0:T(8,128)} %shard_map.47) | non-fusion elementwise | flops 262144 | bytes 3145728 | tf_op jit(solution)/shard_map/mul | solution.py:367
  (13 shorter events, 0.1 us)
Async XLA Ops:
  0.0 6.7 %copy-start.2 = (f32[8,9,7,25]{3,0,2,1:T(8,128)S(1)}, f32[8,9,7,25]{3,0,2,1:T(8,128)}, u32[]{:S(2)}) copy-start(f32[8,9,7,25]{3,0,2,1:T(8,128)} %param.6) | copy-start | bytes 151204
  1.4 10.7 %collective-permute-start = (bf16[4,128,128]{2,1,0:T(8,128)(2,1)S(1)}, bf16[4,128,128]{2,1,0:T(8,128)(2,1)S(1)}, u32[]{:S(2)}, u32[]{:S(2)}) collective-permute-start(bf16[4,128,128]{2,1,0:T(8,128)(2,1)S(1)} %get-tuple-element.6), channel_id=1, source_target_pairs={{0,1},{1,2},{2,3},{3,4},{4,5},{5,6},{6,7},{7,8},{8,9},{9,10},{10,1... | collective-permute-start | bytes 393224 | tf_op jit(solution)/shard_map/ppermute | solution.py:21
  4.5 7.8 %collective-permute-start.1 = (bf16[4,128,128]{2,1,0:T(8,128)(2,1)S(1)}, bf16[4,128,128]{2,1,0:T(8,128)(2,1)S(1)}, u32[]{:S(2)}, u32[]{:S(2)}) collective-permute-start(bf16[4,128,128]{2,1,0:T(8,128)(2,1)S(1)} %get-tuple-element.5), channel_id=1, source_target_pairs={{1,0},{2,1},{3,2},{4,3},{5,4},{6,5},{7,6},{8,7},{9,8},{10,9},{11,1... | collective-permute-start | bytes 393224 | tf_op jit(solution)/shard_map/ppermute | solution.py:23
  9.0 1.9 %copy-start.3 = (s32[8,1,4]{0,2,1:T(4,128)S(1)}, s32[8,1,4]{0,2,1:T(4,128)}, u32[]{:S(2)}) copy-start(s32[8,1,4]{0,2,1:T(4,128)} %param.7) | copy-start | bytes 388
  21.9 5.0 %collective-permute-start.2 = (bf16[16,3,128]{2,1,0:T(4,128)(2,1)S(1)}, bf16[16,3,128]{2,1,0:T(4,128)(2,1)S(1)}, u32[]{:S(2)}, u32[]{:S(2)}) collective-permute-start(bf16[16,3,128]{2,1,0:T(4,128)(2,1)S(1)} %slice_select_fusion), channel_id=1, source_target_pairs={{0,16},{16,0},{32,48},{48,32},{64,80},{80,64},{96,112},{112,96},{1... | collective-permute-start | bytes 36872 | tf_op jit(solution)/shard_map/ppermute | solution.py:37
  25.0 2.0 %copy-start.1 = (bf16[16,64,128]{2,1,0:T(8,128)(2,1)S(1)}, bf16[16,64,128]{2,1,0:T(8,128)(2,1)}, u32[]{:S(2)}) copy-start(bf16[16,64,128]{2,1,0:T(8,128)(2,1)} %shard_map.46) | copy-start | bytes 786436
  26.9 46.8 %copy-start = (f32[16,128,128]{2,1,0:T(8,128)S(1)}, f32[16,128,128]{2,1,0:T(8,128)}, u32[]{:S(2)}) copy-start(f32[16,128,128]{2,1,0:T(8,128)} %param.4) | copy-start | bytes 3145732

commit v18 on v14

--- a/solution.py
+++ b/solution.py
@@ -46,6 +46,18 @@
     return lax.fori_loop(
         1, lax.axis_size(axis), lambda source, state: combine(state, take(source)), take(0)
     )
+
+
+def cover_mask(cover_ref, shares, share_w, depth):
+    me = lax.axis_index("view")
+    view_id = me // shares
+    part = me % shares
+    blocks = cover_ref.shape[1] // shares
+    block_of = lax.broadcasted_iota(jnp.int32, (share_w, depth), 0) // (share_w // blocks)
+    keep = block_of < 0
+    for j in range(blocks):
+        keep = keep | ((block_of == j) & (cover_ref[view_id, part * blocks + j] > 0))
+    return keep
 
 
 def product_kernel(
@@ -96,7 +108,7 @@
             ]
 
     build_columns(width, rows)
-    keep = cover_ref[...] > 0
+    keep = cover_mask(cover_ref, shares, share_w, depth)
 
     def factor_rows(target):
         acc = None
@@ -259,14 +271,14 @@
     n = lax.axis_size("view")
     groups = n // shares
     slab_x, width_y, depth = estimate.shape
-    share_w = cover_plane.shape[0]
+    share_w = extended.shape[1] - banded.shape[1] // depth + 1
     step = slab_x // groups
     padded_rows = extended.shape[0] + 2 * width
     vmem = pl.BlockSpec(memory_space=pltpu.VMEM)
     return pl.pallas_call(
         functools.partial(product_kernel, n, shares, width),
         out_shape=jax.ShapeDtypeStruct(estimate.shape, jnp.float32),
-        in_specs=[vmem] * 3,
+        in_specs=[vmem, vmem, pl.BlockSpec(memory_space=pltpu.SMEM)],
         out_specs=vmem,
         scratch_shapes=[
             pltpu.VMEM((padded_rows,) + extended.shape[1:], extended.dtype),
@@ -300,13 +312,13 @@
     return banded.reshape(taps_x, taps_y * depth, depth)
 
 
-def conv_kernel(tile_x, src_ref, band_ref, image_ref, cover_ref, out_ref, cols_ref):
+def conv_kernel(tile_x, shares, src_ref, band_ref, image_ref, cover_ref, out_ref, cols_ref):
     rows_x, rows_y, depth = out_ref.shape
     taps_x = src_ref.shape[0] - rows_x + 1
     taps_y = src_ref.shape[1] - rows_y + 1
     for step_y in range(taps_y):
         cols_ref[:, :, step_y * depth : (step_y + 1) * depth] = src_ref[:, step_y : step_y + rows_y, :]
-    keep = cover_ref[...] > 0
+    keep = cover_mask(cover_ref, shares, rows_y, depth)
     for start in range(0, rows_x, tile_x):
         acc = None
         for shift_x in range(taps_x):
@@ -318,13 +330,13 @@
         out_ref[start : start + tile_x] = jnp.where(keep[None], ratio, 0.0).astype(out_ref.dtype)
 
 
-def quotient_of(padded_part, banded, image, cover_plane):
+def quotient_of(padded_part, banded, image, cover_plane, shares):
     rows_x, rows_y, depth = image.shape
     vmem = pl.BlockSpec(memory_space=pltpu.VMEM)
     return pl.pallas_call(
-        functools.partial(conv_kernel, 4),
+        functools.partial(conv_kernel, 4, shares),
         out_shape=jax.ShapeDtypeStruct((rows_x, rows_y, depth), jnp.bfloat16),
-        in_specs=[vmem] * 4,
+        in_specs=[vmem, vmem, vmem, pl.BlockSpec(memory_space=pltpu.SMEM)],
         out_specs=vmem,
         scratch_shapes=[pltpu.VMEM((padded_part.shape[0], rows_y, banded.shape[1]), jnp.bfloat16)],
     )(padded_part, banded, image, cover_plane)
@@ -355,8 +367,8 @@
     region = lax.dynamic_slice(
         padded, (0, y_start, 0), (slab_x + 2 * rim_x, share_w + 2 * rim_y, depth)
     )
-    cover_plane = jnp.broadcast_to(cell_cover[0].astype(jnp.float32), (share_w, depth))
-    quotient = quotient_of(region, forward, image, cover_plane)
+    cover_plane = covered[:, 0, :]
+    quotient = quotient_of(region, forward, image, cover_plane, shares)
     rim_zeros = jnp.zeros((slab_x, rim_y, depth), jnp.bfloat16)
     edge_rows = jnp.where(part == 0, quotient[:, share_w - rim_y :, :], quotient[:, :rim_y, :])
     partner = swapped(edge_rows, "view", 0)

time: 76.7 us -> 76.6 us (level)
  no operation moved by 1% of the time
where the time goes in v18:
time: 76.6 us; the launch traced here: 75.7 us
  Pallas kernels  53.3 us (70%)
  other arithmetic  8.62 us (11%)
  starting transfers between devices  6.6 us (9%)
  local copies, waits for them, and re-layouts  4.63 us (6%)
  matrix products  2.37 us (3%)
    pallas_call x1, Pallas kernels, product_gather(): pl.pallas_call(functools.partial(product_kernel, n, shares, width), out_s...  46.3 us
    pallas_call x1, Pallas kernels, quotient_of(): pl.pallas_call(functools.partial(conv_kernel, 4, shares), out_shape=jax.S...  6.98 us
    convert_element_type x2, local copies, waits for them, and re-layouts, band_table(): jnp.einsum('abt,tpz->abpz', kernel, onehot, preferred_element_type=jnp.fl...  3.84 us
    ppermute x1, starting transfers between devices, with_halo(): lax.ppermute(tail, axis, [(i, (i + 1) % count) for i in range(ends)])  3.12 us
    dot_general x2, matrix products, band_table(): jnp.einsum('abt,tpz->abpz', kernel, onehot, preferred_element_type=jnp.fl...  2.37 us
    mul x1, other arithmetic, local(): estimate * product_gather(extended, backward, cover_plane, estimate, shar...  2.31 us
    ppermute x1, starting transfers between devices, with_halo(): lax.ppermute(head, axis, [((i + 1) % count, i) for i in range(ends)])  2.16 us
    reduce_sum x1, other arithmetic, local(): kernel = (spread / jnp.sum(spread)).astype(jnp.bfloat16)  1.63 us
  transfers between devices with their start and end apart: 3, of which 0 were waited for; matrix products, arithmetic and copies ran while one was open for 12% of the time, Pallas kernels for 0%

profile of v18, /device:TPU:71, one launch (start us, length us, event | category | flops | bytes accessed | tf_op | source)
XLA Modules:
  0.0 75.7 jit_solution(17741811208800199311)
XLA Ops:
  0.0 1.3 %convert_element_type.19 = bf16[16,128,128]{2,1,0:T(8,128)(2,1)S(1)} convert(f32[16,128,128]{2,1,0:T(8,128)} %param.4) | non-fusion elementwise | flops 262144 | bytes 1572864 | tf_op jit(solution)/shard_map/convert_element_type | solution.py:356
  1.3 3.1 %collective-permute-start = (bf16[4,128,128]{2,1,0:T(8,128)(2,1)S(1)}, bf16[4,128,128]{2,1,0:T(8,128)(2,1)S(1)}, u32[]{:S(2)}, u32[]{:S(2)}) collective-permute-start(bf16[4,128,128]{2,1,0:T(8,128)(2,1)S(1)} %get-tuple-element.8), channel_id=1, source_target_pairs={{0,1},{1,2},{2,3},{3,4},{4,5},{5,6},{6,7},{7,8},{8,9},{9,10},{10,1... | collective-permute-start | bytes 393224 | tf_op jit(solution)/shard_map/ppermute | solution.py:21
  4.5 2.2 %collective-permute-start.1 = (bf16[4,128,128]{2,1,0:T(8,128)(2,1)S(1)}, bf16[4,128,128]{2,1,0:T(8,128)(2,1)S(1)}, u32[]{:S(2)}, u32[]{:S(2)}) collective-permute-start(bf16[4,128,128]{2,1,0:T(8,128)(2,1)S(1)} %get-tuple-element.7), channel_id=1, source_target_pairs={{1,0},{2,1},{3,2},{4,3},{5,4},{6,5},{7,6},{8,7},{9,8},{10,9},{11,1... | collective-permute-start | bytes 393224 | tf_op jit(solution)/shard_map/ppermute | solution.py:23
  6.7 1.6 %fusion.28 = (f32[]{:T(128)}, f32[1,9,7,25]{3,0,2,1:T(1,128)S(1)}) fusion(f32[8,9,7,25]{3,0,2,1:T(8,128)} %param.6, s32[]{:T(128)S(6)} %select_n.43), kind=kLoop, calls=%fused_computation.32 | loop fusion | flops 1574 | bytes 12608 | tf_op jit(solution)/shard_map/reduce_sum | solution.py:360
  8.3 1.5 %fusion.5 = bf16[9,7,128,128]{3,1,2,0:T(8,128)(2,1)S(1)} fusion(f32[1,9,7,25]{3,0,2,1:T(1,128)S(1)} %get-tuple-element.6, f32[]{:T(128)} %get-tuple-element.5), kind=kOutput, calls=%fused_computation.4 | convolution fusion | flops 53873744 | bytes 2070688 | tf_op jit(solution)/shard_map/abt,tpz->abpz/dot_general | solution.py:309
  9.8 0.0 copy-start.2
  9.8 1.9 %copy.6 = bf16[9,7,128,128]{3,2,1,0:T(8,128)(2,1)} copy(bf16[9,7,128,128]{3,1,2,0:T(8,128)(2,1)S(1)} %fusion.5) | data formatting | bytes 4128768 | tf_op jit(solution)/shard_map/convert_element_type | solution.py:309
  11.7 0.0 copy-done.2
  11.7 0.7 copy.7.cover_ref
  12.4 0.7 fusion.27
  13.1 0.1 rev.3
  13.2 0.0 collective-permute-done
  13.2 0.0 collective-permute-done.1
  13.2 1.1 %fusion.18.src_ref = bf16[24,70,128]{2,1,0:T(8,128)(2,1)} fusion(s32[]{:T(128)S(6)} %select_n.41, bf16[4,128,128]{2,1,0:T(8,128)(2,1)S(1)} %collective-permute-done, bf16[16,128,128]{2,1,0:T(8,128)(2,1)S(1)} %convert_element_type.19, bf16[4,128,128]{2,1,0:T(8,128)(2,1)S(1)} %collective-permute-done.1), kind=kLoop, calls=%fused_computation.17 | loop fusion | flops 2795520 | bytes 1217536 | tf_op jit(solution)/shard_map/concatenate | solution.py:19
  14.3 7.0 %shard_map.46 = bf16[16,64,128]{2,1,0:T(8,128)(2,1)} custom-call(bf16[24,70,128]{2,1,0:T(8,128)(2,1)} %fusion.18.src_ref, bf16[9,896,128]{2,1,0:T(8,128)(2,1)} %bitcast.24, bf16[16,64,128]{2,1,0:T(8,128)(2,1)} %bitcast.26, s32[8,4]{1,0:T(8,128)} %copy.7.cover_ref), custom_call_target="tpu_custom_call" | custom-call | tf_op jit(solution)/shard_map/pallas_call | solution.py:336
  21.3 0.8 %slice_select_fusion = bf16[16,3,128]{2,1,0:T(4,128)(2,1)S(1)} fusion(bf16[16,64,128]{2,1,0:T(8,128)(2,1)} %shard_map.46, pred[]{:T(512)S(6)} %eq.11), kind=kLoop, calls=%fused_computation.25 | loop fusion | flops 6144 | bytes 36865 | tf_op jit(solution)/shard_map/jit(_where)/select_n | solution.py:373
  22.1 1.3 %collective-permute-start.2 = (bf16[16,3,128]{2,1,0:T(4,128)(2,1)S(1)}, bf16[16,3,128]{2,1,0:T(4,128)(2,1)S(1)}, u32[]{:S(2)}, u32[]{:S(2)}) collective-permute-start(bf16[16,3,128]{2,1,0:T(4,128)(2,1)S(1)} %slice_select_fusion), channel_id=1, source_target_pairs={{0,16},{16,0},{32,48},{48,32},{64,80},{80,64},{96,112},{112,96},{1... | collective-permute-start | bytes 36872 | tf_op jit(solution)/shard_map/ppermute | solution.py:37
  23.4 0.9 %fusion.8 = bf16[9,7,128,128]{3,1,2,0:T(8,128)(2,1)S(1)} fusion(bf16[9,7,25]{2,1,0:T(8,128)(2,1)S(1)} %rev.3), kind=kOutput, calls=%fused_computation.5 | convolution fusion | flops 53870592 | bytes 2067534 | tf_op jit(solution)/shard_map/abt,tpz->abpz/dot_general | solution.py:309
  24.3 1.9 %copy.8 = bf16[9,7,128,128]{3,2,1,0:T(8,128)(2,1)} copy(bf16[9,7,128,128]{3,1,2,0:T(8,128)(2,1)S(1)} %fusion.8) | data formatting | bytes 4128768 | tf_op jit(solution)/shard_map/convert_element_type | solution.py:309
  26.2 0.0 collective-permute-done.2
  26.2 0.0 copy-done.1
  26.2 0.8 %pad_maximum_fusion.quot_ref = bf16[16,70,128]{2,1,0:T(8,128)(2,1)} fusion(bf16[16,3,128]{2,1,0:T(4,128)(2,1)S(1)} %get-tuple-element.10, bf16[16,64,128]{2,1,0:T(8,128)(2,1)S(1)} %copy-done.1, bf16[16,3,128]{2,1,0:T(4,128)(2,1)S(1)} %get-tuple-element.9), kind=kLoop, calls=%fused_computation.20 | loop fusion | flops 860160 | bytes 573440 | tf_op jit(solution)/shard_map/concatenate | solution.py:377
  27.0 46.3 %shard_map.47 = f32[16,128,128]{2,1,0:T(8,128)} custom-call(bf16[16,70,128]{2,1,0:T(8,128)(2,1)} %pad_maximum_fusion.quot_ref, bf16[9,896,128]{2,1,0:T(8,128)(2,1)} %bitcast.25, s32[8,4]{1,0:T(8,128)} %copy.7.cover_ref), custom_call_target="tpu_custom_call" | custom-call | tf_op jit(solution)/shard_map/pallas_call | solution.py:278
  73.4 2.3 %mul.7 = f32[16,128,128]{2,1,0:T(8,128)} multiply(f32[16,128,128]{2,1,0:T(8,128)S(1)} %copy-done, f32[16,128,128]{2,1,0:T(8,128)} %shard_map.47) | non-fusion elementwise | flops 262144 | bytes 3145728 | tf_op jit(solution)/shard_map/mul | solution.py:378
  (5 shorter events, 0.0 us)
Async XLA Ops:
  1.3 11.8 %collective-permute-start = (bf16[4,128,128]{2,1,0:T(8,128)(2,1)S(1)}, bf16[4,128,128]{2,1,0:T(8,128)(2,1)S(1)}, u32[]{:S(2)}, u32[]{:S(2)}) collective-permute-start(bf16[4,128,128]{2,1,0:T(8,128)(2,1)S(1)} %get-tuple-element.8), channel_id=1, source_target_pairs={{0,1},{1,2},{2,3},{3,4},{4,5},{5,6},{6,7},{7,8},{8,9},{9,10},{10,1... | collective-permute-start | bytes 393224 | tf_op jit(solution)/shard_map/ppermute | solution.py:21
  4.5 8.7 %collective-permute-start.1 = (bf16[4,128,128]{2,1,0:T(8,128)(2,1)S(1)}, bf16[4,128,128]{2,1,0:T(8,128)(2,1)S(1)}, u32[]{:S(2)}, u32[]{:S(2)}) collective-permute-start(bf16[4,128,128]{2,1,0:T(8,128)(2,1)S(1)} %get-tuple-element.7), channel_id=1, source_target_pairs={{1,0},{2,1},{3,2},{4,3},{5,4},{6,5},{7,6},{8,7},{9,8},{10,9},{11,1... | collective-permute-start | bytes 393224 | tf_op jit(solution)/shard_map/ppermute | solution.py:23
  9.8 1.9 %copy-start.2 = (s32[8,1,4]{0,2,1:T(4,128)S(1)}, s32[8,1,4]{0,2,1:T(4,128)}, u32[]{:S(2)}) copy-start(s32[8,1,4]{0,2,1:T(4,128)} %param.7) | copy-start | bytes 388
  22.1 4.1 %collective-permute-start.2 = (bf16[16,3,128]{2,1,0:T(4,128)(2,1)S(1)}, bf16[16,3,128]{2,1,0:T(4,128)(2,1)S(1)}, u32[]{:S(2)}, u32[]{:S(2)}) collective-permute-start(bf16[16,3,128]{2,1,0:T(4,128)(2,1)S(1)} %slice_select_fusion), channel_id=1, source_target_pairs={{0,16},{16,0},{32,48},{48,32},{64,80},{80,64},{96,112},{112,96},{1... | collective-permute-start | bytes 36872 | tf_op jit(solution)/shard_map/ppermute | solution.py:37
  24.3 2.0 %copy-start.1 = (bf16[16,64,128]{2,1,0:T(8,128)(2,1)S(1)}, bf16[16,64,128]{2,1,0:T(8,128)(2,1)}, u32[]{:S(2)}) copy-start(bf16[16,64,128]{2,1,0:T(8,128)(2,1)} %shard_map.46) | copy-start | bytes 786436
  26.2 47.2 %copy-start = (f32[16,128,128]{2,1,0:T(8,128)S(1)}, f32[16,128,128]{2,1,0:T(8,128)}, u32[]{:S(2)}) copy-start(f32[16,128,128]{2,1,0:T(8,128)} %param.4) | copy-start | bytes 3145732

commit v19 on v18

--- a/solution.py
+++ b/solution.py
@@ -99,7 +99,6 @@
     def _():
         pl.semaphore_signal(barrier, inc=1, device_id={"blk": down}, device_id_type=mesh_kind)
 
-    ext_ref[pl.ds(width, rows)] = quot_ref[...]
 
     def build_columns(first, count):
         for step_y in range(taps_y):
@@ -107,7 +106,10 @@
                 pl.ds(first, count), step_y : step_y + share_w, :
             ]
 
-    build_columns(width, rows)
+    for step_y in range(taps_y):
+        cols_ref[pl.ds(width, rows), :, step_y * depth : (step_y + 1) * depth] = quot_ref[
+            :, step_y : step_y + share_w, :
+        ]
     keep = cover_mask(cover_ref, shares, share_w, depth)
 
     def factor_rows(target):

time: 76.6 us -> 76.6 us (level)
  no operation moved by 1% of the time
where the time goes in v19:
time: 76.6 us; the launch traced here: 75.7 us
  Pallas kernels  53.3 us (70%)
  other arithmetic  8.62 us (11%)
  starting transfers between devices  6.6 us (9%)
  local copies, waits for them, and re-layouts  4.63 us (6%)
  matrix products  2.37 us (3%)
    pallas_call x1, Pallas kernels, product_gather(): pl.pallas_call(functools.partial(product_kernel, n, shares, width), out_s...  46.3 us
    pallas_call x1, Pallas kernels, quotient_of(): pl.pallas_call(functools.partial(conv_kernel, 4, shares), out_shape=jax.S...  6.98 us
    convert_element_type x2, local copies, waits for them, and re-layouts, band_table(): jnp.einsum('abt,tpz->abpz', kernel, onehot, preferred_element_type=jnp.fl...  3.84 us
    ppermute x1, starting transfers between devices, with_halo(): lax.ppermute(tail, axis, [(i, (i + 1) % count) for i in range(ends)])  3.12 us
    dot_general x2, matrix products, band_table(): jnp.einsum('abt,tpz->abpz', kernel, onehot, preferred_element_type=jnp.fl...  2.37 us
    mul x1, other arithmetic, local(): estimate * product_gather(extended, backward, cover_plane, estimate, shar...  2.31 us
    ppermute x1, starting transfers between devices, with_halo(): lax.ppermute(head, axis, [((i + 1) % count, i) for i in range(ends)])  2.16 us
    reduce_sum x1, other arithmetic, local(): kernel = (spread / jnp.sum(spread)).astype(jnp.bfloat16)  1.63 us
  transfers between devices with their start and end apart: 3, of which 0 were waited for; matrix products, arithmetic and copies ran while one was open for 12% of the time, Pallas kernels for 0%

profile of v19, /device:TPU:71, one launch (start us, length us, event | category | flops | bytes accessed | tf_op | source)
XLA Modules:
  0.0 75.7 jit_solution(16210689894071112678)
XLA Ops:
  0.0 1.3 %convert_element_type.19 = bf16[16,128,128]{2,1,0:T(8,128)(2,1)S(1)} convert(f32[16,128,128]{2,1,0:T(8,128)} %param.4) | non-fusion elementwise | flops 262144 | bytes 1572864 | tf_op jit(solution)/shard_map/convert_element_type | solution.py:358
  1.3 3.1 %collective-permute-start = (bf16[4,128,128]{2,1,0:T(8,128)(2,1)S(1)}, bf16[4,128,128]{2,1,0:T(8,128)(2,1)S(1)}, u32[]{:S(2)}, u32[]{:S(2)}) collective-permute-start(bf16[4,128,128]{2,1,0:T(8,128)(2,1)S(1)} %get-tuple-element.8), channel_id=1, source_target_pairs={{0,1},{1,2},{2,3},{3,4},{4,5},{5,6},{6,7},{7,8},{8,9},{9,10},{10,1... | collective-permute-start | bytes 393224 | tf_op jit(solution)/shard_map/ppermute | solution.py:21
  4.5 2.2 %collective-permute-start.1 = (bf16[4,128,128]{2,1,0:T(8,128)(2,1)S(1)}, bf16[4,128,128]{2,1,0:T(8,128)(2,1)S(1)}, u32[]{:S(2)}, u32[]{:S(2)}) collective-permute-start(bf16[4,128,128]{2,1,0:T(8,128)(2,1)S(1)} %get-tuple-element.7), channel_id=1, source_target_pairs={{1,0},{2,1},{3,2},{4,3},{5,4},{6,5},{7,6},{8,7},{9,8},{10,9},{11,1... | collective-permute-start | bytes 393224 | tf_op jit(solution)/shard_map/ppermute | solution.py:23
  6.7 1.6 %fusion.28 = (f32[]{:T(128)}, f32[1,9,7,25]{3,0,2,1:T(1,128)S(1)}) fusion(f32[8,9,7,25]{3,0,2,1:T(8,128)} %param.6, s32[]{:T(128)S(6)} %select_n.43), kind=kLoop, calls=%fused_computation.32 | loop fusion | flops 1574 | bytes 12608 | tf_op jit(solution)/shard_map/reduce_sum | solution.py:362
  8.3 1.5 %fusion.5 = bf16[9,7,128,128]{3,1,2,0:T(8,128)(2,1)S(1)} fusion(f32[1,9,7,25]{3,0,2,1:T(1,128)S(1)} %get-tuple-element.6, f32[]{:T(128)} %get-tuple-element.5), kind=kOutput, calls=%fused_computation.4 | convolution fusion | flops 53873744 | bytes 2070688 | tf_op jit(solution)/shard_map/abt,tpz->abpz/dot_general | solution.py:311
  9.8 0.0 copy-start.2
  9.8 1.9 %copy.6 = bf16[9,7,128,128]{3,2,1,0:T(8,128)(2,1)} copy(bf16[9,7,128,128]{3,1,2,0:T(8,128)(2,1)S(1)} %fusion.5) | data formatting | bytes 4128768 | tf_op jit(solution)/shard_map/convert_element_type | solution.py:311
  11.7 0.0 copy-done.2
  11.7 0.7 copy.7.cover_ref
  12.4 0.7 fusion.27
  13.1 0.1 rev.3
  13.2 0.0 collective-permute-done
  13.2 0.0 collective-permute-done.1
  13.2 1.1 %fusion.18.src_ref = bf16[24,70,128]{2,1,0:T(8,128)(2,1)} fusion(s32[]{:T(128)S(6)} %select_n.41, bf16[4,128,128]{2,1,0:T(8,128)(2,1)S(1)} %collective-permute-done, bf16[16,128,128]{2,1,0:T(8,128)(2,1)S(1)} %convert_element_type.19, bf16[4,128,128]{2,1,0:T(8,128)(2,1)S(1)} %collective-permute-done.1), kind=kLoop, calls=%fused_computation.17 | loop fusion | flops 2795520 | bytes 1217536 | tf_op jit(solution)/shard_map/concatenate | solution.py:19
  14.3 7.0 %shard_map.46 = bf16[16,64,128]{2,1,0:T(8,128)(2,1)} custom-call(bf16[24,70,128]{2,1,0:T(8,128)(2,1)} %fusion.18.src_ref, bf16[9,896,128]{2,1,0:T(8,128)(2,1)} %bitcast.24, bf16[16,64,128]{2,1,0:T(8,128)(2,1)} %bitcast.26, s32[8,4]{1,0:T(8,128)} %copy.7.cover_ref), custom_call_target="tpu_custom_call" | custom-call | tf_op jit(solution)/shard_map/pallas_call | solution.py:338
  21.3 0.8 %slice_select_fusion = bf16[16,3,128]{2,1,0:T(4,128)(2,1)S(1)} fusion(bf16[16,64,128]{2,1,0:T(8,128)(2,1)} %shard_map.46, pred[]{:T(512)S(6)} %eq.11), kind=kLoop, calls=%fused_computation.25 | loop fusion | flops 6144 | bytes 36865 | tf_op jit(solution)/shard_map/jit(_where)/select_n | solution.py:375
  22.1 1.3 %collective-permute-start.2 = (bf16[16,3,128]{2,1,0:T(4,128)(2,1)S(1)}, bf16[16,3,128]{2,1,0:T(4,128)(2,1)S(1)}, u32[]{:S(2)}, u32[]{:S(2)}) collective-permute-start(bf16[16,3,128]{2,1,0:T(4,128)(2,1)S(1)} %slice_select_fusion), channel_id=1, source_target_pairs={{0,16},{16,0},{32,48},{48,32},{64,80},{80,64},{96,112},{112,96},{1... | collective-permute-start | bytes 36872 | tf_op jit(solution)/shard_map/ppermute | solution.py:37
  23.4 0.9 %fusion.8 = bf16[9,7,128,128]{3,1,2,0:T(8,128)(2,1)S(1)} fusion(bf16[9,7,25]{2,1,0:T(8,128)(2,1)S(1)} %rev.3), kind=kOutput, calls=%fused_computation.5 | convolution fusion | flops 53870592 | bytes 2067534 | tf_op jit(solution)/shard_map/abt,tpz->abpz/dot_general | solution.py:311
  24.3 1.9 %copy.8 = bf16[9,7,128,128]{3,2,1,0:T(8,128)(2,1)} copy(bf16[9,7,128,128]{3,1,2,0:T(8,128)(2,1)S(1)} %fusion.8) | data formatting | bytes 4128768 | tf_op jit(solution)/shard_map/convert_element_type | solution.py:311
  26.2 0.0 collective-permute-done.2
  26.2 0.0 copy-done.1
  26.2 0.8 %pad_maximum_fusion.quot_ref = bf16[16,70,128]{2,1,0:T(8,128)(2,1)} fusion(bf16[16,3,128]{2,1,0:T(4,128)(2,1)S(1)} %get-tuple-element.10, bf16[16,64,128]{2,1,0:T(8,128)(2,1)S(1)} %copy-done.1, bf16[16,3,128]{2,1,0:T(4,128)(2,1)S(1)} %get-tuple-element.9), kind=kLoop, calls=%fused_computation.20 | loop fusion | flops 860160 | bytes 573440 | tf_op jit(solution)/shard_map/concatenate | solution.py:379
  27.0 46.3 %shard_map.47 = f32[16,128,128]{2,1,0:T(8,128)} custom-call(bf16[16,70,128]{2,1,0:T(8,128)(2,1)} %pad_maximum_fusion.quot_ref, bf16[9,896,128]{2,1,0:T(8,128)(2,1)} %bitcast.25, s32[8,4]{1,0:T(8,128)} %copy.7.cover_ref), custom_call_target="tpu_custom_call" | custom-call | tf_op jit(solution)/shard_map/pallas_call | solution.py:280
  73.4 2.3 %mul.7 = f32[16,128,128]{2,1,0:T(8,128)} multiply(f32[16,128,128]{2,1,0:T(8,128)S(1)} %copy-done, f32[16,128,128]{2,1,0:T(8,128)} %shard_map.47) | non-fusion elementwise | flops 262144 | bytes 3145728 | tf_op jit(solution)/shard_map/mul | solution.py:380
  (5 shorter events, 0.0 us)
Async XLA Ops:
  1.3 11.8 %collective-permute-start = (bf16[4,128,128]{2,1,0:T(8,128)(2,1)S(1)}, bf16[4,128,128]{2,1,0:T(8,128)(2,1)S(1)}, u32[]{:S(2)}, u32[]{:S(2)}) collective-permute-start(bf16[4,128,128]{2,1,0:T(8,128)(2,1)S(1)} %get-tuple-element.8), channel_id=1, source_target_pairs={{0,1},{1,2},{2,3},{3,4},{4,5},{5,6},{6,7},{7,8},{8,9},{9,10},{10,1... | collective-permute-start | bytes 393224 | tf_op jit(solution)/shard_map/ppermute | solution.py:21
  4.5 8.7 %collective-permute-start.1 = (bf16[4,128,128]{2,1,0:T(8,128)(2,1)S(1)}, bf16[4,128,128]{2,1,0:T(8,128)(2,1)S(1)}, u32[]{:S(2)}, u32[]{:S(2)}) collective-permute-start(bf16[4,128,128]{2,1,0:T(8,128)(2,1)S(1)} %get-tuple-element.7), channel_id=1, source_target_pairs={{1,0},{2,1},{3,2},{4,3},{5,4},{6,5},{7,6},{8,7},{9,8},{10,9},{11,1... | collective-permute-start | bytes 393224 | tf_op jit(solution)/shard_map/ppermute | solution.py:23
  9.8 1.9 %copy-start.2 = (s32[8,1,4]{0,2,1:T(4,128)S(1)}, s32[8,1,4]{0,2,1:T(4,128)}, u32[]{:S(2)}) copy-start(s32[8,1,4]{0,2,1:T(4,128)} %param.7) | copy-start | bytes 388
  22.1 4.1 %collective-permute-start.2 = (bf16[16,3,128]{2,1,0:T(4,128)(2,1)S(1)}, bf16[16,3,128]{2,1,0:T(4,128)(2,1)S(1)}, u32[]{:S(2)}, u32[]{:S(2)}) collective-permute-start(bf16[16,3,128]{2,1,0:T(4,128)(2,1)S(1)} %slice_select_fusion), channel_id=1, source_target_pairs={{0,16},{16,0},{32,48},{48,32},{64,80},{80,64},{96,112},{112,96},{1... | collective-permute-start | bytes 36872 | tf_op jit(solution)/shard_map/ppermute | solution.py:37
  24.3 2.0 %copy-start.1 = (bf16[16,64,128]{2,1,0:T(8,128)(2,1)S(1)}, bf16[16,64,128]{2,1,0:T(8,128)(2,1)}, u32[]{:S(2)}) copy-start(bf16[16,64,128]{2,1,0:T(8,128)(2,1)} %shard_map.46) | copy-start | bytes 786436
  26.2 47.2 %copy-start = (f32[16,128,128]{2,1,0:T(8,128)S(1)}, f32[16,128,128]{2,1,0:T(8,128)}, u32[]{:S(2)}) copy-start(f32[16,128,128]{2,1,0:T(8,128)} %param.4) | copy-start | bytes 3145732
